TPU v7x, 32 devices: a whole 2x2x4 slice. The times are simulated.
32 devices in a mesh: blk: 8 (over z, y), grp: 4 (over x, core).
Axes of the slice: x: 2, y: 2, z: 4, core: 2. Of those that a mesh axis runs over, the one named last changes fastest.
Arguments:
- spectra: bfloat16 [4, 2048, 2, 16, 256], P('grp', 'blk'), may hold values from -6 to 6
- detector_valid: int32 [4, 2048], P('grp', 'blk'), may hold values 0 or 1
Outputs:
- coherence: float32 [2, 4, 2048, 8192], P(None, None, 'blk', 'grp')
All inputs are finite; a program needn't handle non-finite values. No bound on the sum of `detector_valid` on one device may be relied on, other than what follows from the above.
Results may differ from a plain program's by a relative error of at most 0.0003.
Values may be sent and summed in bfloat16 or wider, within the bound.
No kernel may reach another device: no remote copies, remote signals or barrier semaphores. Data moves between devices by JAX's collectives and lax.ppermute only.
A program may use at most 128 MiB of HBM per device.

v0:
```python
import math

import jax
import jax.numpy as jnp
from jax import lax
from jax.sharding import PartitionSpec as P


def from_behind(block, axis, distance):
    devices = range(lax.axis_size(axis))
    route = [((i - distance) % len(devices), i) for i in devices]
    return lax.ppermute(block, axis, route)


def factors(flattened, flag_vals):
    widened = flattened.astype(jnp.float32)
    power_mean = jnp.mean(widened * widened, axis=1) + 1e-06
    return flag_vals.astype(jnp.float32) * lax.rsqrt(power_mean)


def shards(spectra, detector_valid):
    shard_rows = spectra.shape[1]
    half_width = spectra.shape[3] * spectra.shape[4]
    full_width = 2 * half_width
    cycle_size = lax.axis_size("blk")
    group_size = lax.axis_size("grp")
    position = lax.axis_index("blk")
    scale_coef = 0.5 / math.sqrt(half_width)
    row_spec, row_flags = (
        lax.all_gather(spectra, "grp", axis=0, tiled=True),
        lax.all_gather(detector_valid, "grp", axis=0, tiled=True),
    )
    row_count = group_size * shard_rows
    rows_flat = row_spec.reshape(row_count, full_width)
    row_factor = factors(rows_flat, row_flags.reshape(row_count)) * scale_coef

    def cross_tile(col_spec, col_flags):
        flattened = col_spec.reshape(shard_rows, full_width)
        col_factor = factors(flattened, col_flags.reshape(shard_rows))
        rotated = jnp.concatenate([-flattened[:, half_width:], flattened[:, :half_width]], axis=1)
        stacked = jnp.concatenate([flattened, rotated], axis=0)
        product = lax.dot_general(
            rows_flat, stacked, (((1,), (1,)), ((), ())), preferred_element_type=jnp.float32
        )
        product = product * row_factor[:, None] * jnp.concatenate([col_factor, col_factor])[None, :]
        return product.reshape(row_count, 2, shard_rows).transpose(1, 0, 2)

    def put_block(output_tile, block_vals, slot_index):
        start = slot_index * shard_rows
        return lax.dynamic_update_slice(
            output_tile, block_vals, (jnp.int32(0), jnp.int32(0), start)
        )

    output_tile = jnp.zeros((2, row_count, cycle_size * shard_rows), jnp.float32)
    output_tile = put_block(output_tile, cross_tile(spectra, detector_valid), position)
    sign_pair = jnp.array([1.0, -1.0], jnp.float32).reshape(2, 1, 1, 1)
    col_state = (spectra, detector_valid)
    for offset in range(1, cycle_size // 2 + 1):
        col_state = from_behind((col_state[0], col_state[1]), "blk", 1)
        block_vals = cross_tile(col_state[0], col_state[1])
        output_tile = put_block(output_tile, block_vals, (position - offset) % cycle_size)
        if offset < cycle_size // 2:
            flipped = (
                block_vals.reshape(2, group_size, shard_rows, shard_rows).transpose(0, 1, 3, 2)
                * sign_pair
            )
            swapped = lax.all_to_all(flipped, "grp", split_axis=1, concat_axis=1, tiled=True)
            returned = from_behind(swapped, "blk", -offset)
            output_tile = put_block(
                output_tile,
                returned.reshape(2, row_count, shard_rows),
                (position + offset) % cycle_size,
            )
    return output_tile.reshape(2, group_size, shard_rows, cycle_size * shard_rows)


def solution(mesh):
    return jax.shard_map(
        shards,
        mesh=mesh,
        in_specs=(P("grp", "blk", None, None, None), P("grp", "blk")),
        out_specs=P(None, None, "blk", "grp"),
        check_vma=False,
    )
```

profile of v0, /device:TPU:31, one launch (start us, length us, event | category | flops | bytes accessed | tf_op | source)
XLA Modules:
  0.0 727.0 jit_solution(74707175019630629)
XLA Ops:
  7.3 91.8 %collective-permute-done = bf16[1,256,2,16,256]{4,3,2,1,0:T(8,128)(2,1)S(1)} collective-permute-done((bf16[1,256,2,16,256]{4,3,2,1,0:T(8,128)(2,1)}, bf16[1,256,2,16,256]{4,3,2,1,0:T(8,128)(2,1)S(1)}, u32[]{:S(2)}, u32[]{:S(2)}) %collective-permute-start) | collective-permute-done | bytes 4194336 | tf_op jit(solution)/shard_map/ppermute | solution.py:12
  103.8 88.5 %collective-permute-done.3 = bf16[1,256,2,16,256]{4,3,2,1,0:T(8,128)(2,1)} collective-permute-done((bf16[1,256,2,16,256]{4,3,2,1,0:T(8,128)(2,1)S(1)}, bf16[1,256,2,16,256]{4,3,2,1,0:T(8,128)(2,1)}, u32[]{:S(2)}, u32[]{:S(2)}) %collective-permute-start.3) | collective-permute-done | bytes 4194336 | tf_op jit(solution)/shard_map/ppermute | solution.py:12
  192.3 5.0 collective-permute-start.6
  197.4 88.0 %collective-permute-done.1 = s32[1,256]{1,0:T(1,128)S(1)} collective-permute-done((s32[1,256]{1,0:T(1,128)S(1)}, s32[1,256]{1,0:T(1,128)S(1)}, u32[]{:S(2)}, u32[]{:S(2)}) %collective-permute-start.1) | collective-permute-done | bytes 1056 | tf_op jit(solution)/shard_map/ppermute | solution.py:12
  285.3 4.9 collective-permute-start.4
  291.0 4.4 collective-permute-start.7
  295.4 9.4 %all-gather = s32[4,1,256]{2,1,0:T(1,128)S(1)} all-gather(s32[1,1,256]{2,1,0:T(1,128)S(1)} %bitcast.81), channel_id=1, replica_groups=mesh['blk'=8,'grp'=4] {'grp'}, dimensions={0}, use_global_device_ids=true | all-gather | bytes 5120 | tf_op jit(solution)/shard_map/all_gather | solution.py:31
  304.8 7.4 %reshape.98 = bf16[256,8192]{1,0:T(8,128)(2,1)} reshape(bf16[1,256,2,16,256]{4,3,2,1,0:T(8,128)(2,1)} %copy-done.5) | data formatting | bytes 8388608 | tf_op jit(solution)/shard_map/reshape | solution.py:38
  312.2 3.9 multiply_reduce_fusion.4
  318.4 7.4 %reshape.102 = bf16[256,8192]{1,0:T(8,128)(2,1)} reshape(bf16[1,256,2,16,256]{4,3,2,1,0:T(8,128)(2,1)} %collective-permute-done.3) | data formatting | bytes 8388608 | tf_op jit(solution)/shard_map/reshape | solution.py:38
  325.9 3.9 multiply_reduce_fusion.3
  332.0 7.4 %reshape.106 = bf16[256,8192]{1,0:T(8,128)(2,1)} reshape(bf16[1,256,2,16,256]{4,3,2,1,0:T(8,128)(2,1)} %collective-permute-done.6) | data formatting | bytes 8388608 | tf_op jit(solution)/shard_map/reshape | solution.py:38
  339.9 4.0 multiply_reduce_fusion.2
  346.1 9.8 %multiply_reduce_fusion = f32[4,256]{1,0:T(4,128)S(1)} fusion(bf16[4,256,2,16,256]{4,3,2,1,0:T(8,128)(2,1)} %all-gather.3.cloned.1.call-done), kind=kLoop, calls=%fused_computation | loop fusion | flops 25164800 | bytes 16781312 | tf_op jit(solution)/shard_map/reduce_sum | solution.py:17
  356.0 25.5 %reshape.96 = bf16[1024,8192]{1,0:T(8,128)(2,1)} reshape(bf16[4,256,2,16,256]{4,3,2,1,0:T(8,128)(2,1)} %all-gather.3.cloned.1.call-done) | data formatting | bytes 33554432 | tf_op jit(solution)/shard_map/reshape | solution.py:34
  381.5 14.6 %multiply_multiply_fusion.3 = f32[512,1024]{1,0:T(8,128)S(1)} fusion(bf16[1024,8192]{1,0:T(8,128)(2,1)} %reshape.96, bf16[256,4096]{1,0:T(8,128)(2,1)} %get-tuple-element.12, bf16[256,4096]{1,0:T(8,128)(2,1)} %get-tuple-element.11, bf16[256,8192]{1,0:T(8,128)(2,1)} %reshape.98, f32[512]{0:T(512)S(1)} %pad_maximum_fusion.1, f32[1024]{0:T(1024)S(1)} %bitcast.87), kind=kOutput, calls=%fused_computation.50 | convolution fusion | flops 8616148992 | bytes 27269120 | tf_op jit(solution)/shard_map/dot_general | solution.py:42
  397.9 14.6 %multiply_multiply_fusion.2 = f32[512,1024]{1,0:T(8,128)S(1)} fusion(bf16[1024,8192]{1,0:T(8,128)(2,1)} %reshape.96, bf16[256,4096]{1,0:T(8,128)(2,1)} %get-tuple-element.10, bf16[256,4096]{1,0:T(8,128)(2,1)} %get-tuple-element.9, bf16[256,8192]{1,0:T(8,128)(2,1)} %reshape.102, f32[512]{0:T(512)S(1)} %pad_maximum_fusion.2, f32[1024]{0:T(1024)S(1)} %bitcast.88), kind=kOutput, calls=%fused_computation.48 | convolution fusion | flops 8616148992 | bytes 27269120 | tf_op jit(solution)/shard_map/dot_general | solution.py:42
  414.4 16.1 %multiply_multiply_fusion.1 = f32[512,1024]{1,0:T(8,128)} fusion(bf16[1024,8192]{1,0:T(8,128)(2,1)} %reshape.96, bf16[256,4096]{1,0:T(8,128)(2,1)} %get-tuple-element.8, bf16[256,4096]{1,0:T(8,128)(2,1)} %get-tuple-element.7, bf16[256,8192]{1,0:T(8,128)(2,1)} %reshape.106, f32[512]{0:T(512)S(1)} %pad_maximum_fusion.3, f32[1024]{0:T(1024)S(1)} %bitcast.89), kind=kOutput, calls=%fused_computation.46 | convolution fusion | flops 8616148992 | bytes 27269120 | tf_op jit(solution)/shard_map/dot_general | solution.py:42
  432.4 5.2 multiply_bitcast_fusion
  440.5 6.0 all-to-all-start.1
  450.4 7.5 %reshape.95 = bf16[256,8192]{1,0:T(8,128)(2,1)} reshape(bf16[1,256,2,16,256]{4,3,2,1,0:T(8,128)(2,1)} %param.3) | data formatting | bytes 8388608 | tf_op jit(solution)/shard_map/reshape | solution.py:38
  457.8 4.5 slice_negate_fusion.4
  470.5 6.3 all-to-all-start
  480.5 7.4 %reshape.110 = bf16[256,8192]{1,0:T(8,128)(2,1)} reshape(bf16[1,256,2,16,256]{4,3,2,1,0:T(8,128)(2,1)} %collective-permute-done.9) | data formatting | bytes 8388608 | tf_op jit(solution)/shard_map/reshape | solution.py:38
  487.9 4.5 slice_negate_fusion
  495.3 5.4 all-to-all-done
  500.6 6.5 all-to-all-start.2
  507.2 15.9 %multiply_multiply_fusion.4 = f32[512,1024]{1,0:T(8,128)} fusion(bf16[1024,8192]{1,0:T(8,128)(2,1)} %reshape.96, bf16[256,4096]{1,0:T(8,128)(2,1)} %get-tuple-element.14, bf16[256,4096]{1,0:T(8,128)(2,1)} %get-tuple-element.13, bf16[256,8192]{1,0:T(8,128)(2,1)} %reshape.95, f32[512]{0:T(512)S(1)} %pad_maximum_fusion, f32[1024]{0:T(1024)S(1)} %bitcast.90), kind=kOutput, calls=%fused_computation.51 | convolution fusion | flops 8616148992 | bytes 27269120 | tf_op jit(solution)/shard_map/dot_general | solution.py:42
  534.2 15.9 %multiply_multiply_fusion = f32[512,1024]{1,0:T(8,128)} fusion(bf16[1024,8192]{1,0:T(8,128)(2,1)} %reshape.96, bf16[256,4096]{1,0:T(8,128)(2,1)} %get-tuple-element.6, bf16[256,4096]{1,0:T(8,128)(2,1)} %get-tuple-element.5, bf16[256,8192]{1,0:T(8,128)(2,1)} %reshape.110, f32[512]{0:T(512)S(1)} %pad_maximum_fusion.4, f32[1024]{0:T(1024)S(1)} %bitcast.91), kind=kOutput, calls=%fused_computation.44 | convolution fusion | flops 8616148992 | bytes 27269120 | tf_op jit(solution)/shard_map/dot_general | solution.py:42
  559.9 16.1 %collective-permute-done.2 = f32[2,4,256,256]{3,2,1,0:T(8,128)} collective-permute-done((f32[2,4,256,256]{3,2,1,0:T(8,128)}, f32[2,4,256,256]{3,2,1,0:T(8,128)}, u32[]{:S(2)}, u32[]{:S(2)}) %collective-permute-start.2) | collective-permute-done | bytes 2097184 | tf_op jit(solution)/shard_map/ppermute | solution.py:12
  580.6 130.9 %collective-permute-done.8 = f32[2,4,256,256]{3,2,1,0:T(8,128)} collective-permute-done((f32[2,4,256,256]{3,2,1,0:T(8,128)}, f32[2,4,256,256]{3,2,1,0:T(8,128)}, u32[]{:S(2)}, u32[]{:S(2)}) %collective-permute-start.8) | collective-permute-done | bytes 2097184 | tf_op jit(solution)/shard_map/ppermute | solution.py:12
  713.8 6.2 copy-done.2
  (83 shorter events, 68.3 us)
Async XLA Ops:
  6.5 190.8 %copy-start.9 = (s32[1,256]{1,0:T(1,128)S(1)}, s32[1,256]{1,0:T(1,128)}, u32[]{:S(2)}) copy-start(s32[1,256]{1,0:T(1,128)} %param.4) | copy-start | bytes 3076
  6.5 339.5 %all-gather.3.cloned.1.call-start = ((), (), s32[]{:S(2)}) async-start(), calls=%async_computation.3 | async-start | bytes 20971520 | tf_op jit(solution)/shard_map/all_gather | solution.py:30
  7.3 91.8 %collective-permute-start = (bf16[1,256,2,16,256]{4,3,2,1,0:T(8,128)(2,1)}, bf16[1,256,2,16,256]{4,3,2,1,0:T(8,128)(2,1)S(1)}, u32[]{:S(2)}, u32[]{:S(2)}) collective-permute-start(bf16[1,256,2,16,256]{4,3,2,1,0:T(8,128)(2,1)} %param.3), channel_id=1, source_target_pairs={{28,0},{0,4},{4,8},{8,12},{12,16},{16,20},{20,24},{24,28},{29,1},{... | collective-permute-start | bytes 12582920 | tf_op jit(solution)/shard_map/ppermute | solution.py:12
  99.1 2.0 copy-start.5
  101.1 91.2 %collective-permute-start.3 = (bf16[1,256,2,16,256]{4,3,2,1,0:T(8,128)(2,1)S(1)}, bf16[1,256,2,16,256]{4,3,2,1,0:T(8,128)(2,1)}, u32[]{:S(2)}, u32[]{:S(2)}) collective-permute-start(bf16[1,256,2,16,256]{4,3,2,1,0:T(8,128)(2,1)S(1)} %collective-permute-done), channel_id=1, source_target_pairs={{28,0},{0,4},{4,8},{8,12},{12,16},{16,20},{20,24},{24,28},{29,1},{... | collective-permute-start | bytes 12582920 | tf_op jit(solution)/shard_map/ppermute | solution.py:12
  192.3 139.7 %collective-permute-start.6 = (bf16[1,256,2,16,256]{4,3,2,1,0:T(8,128)(2,1)}, bf16[1,256,2,16,256]{4,3,2,1,0:T(8,128)(2,1)}, u32[]{:S(2)}, u32[]{:S(2)}) collective-permute-start(bf16[1,256,2,16,256]{4,3,2,1,0:T(8,128)(2,1)} %collective-permute-done.3), channel_id=1, source_target_pairs={{28,0},{0,4},{4,8},{8,12},{12,16},{16,20},{20,24},{24,28},{29,1},{... | collective-permute-start | bytes 12582920 | tf_op jit(solution)/shard_map/ppermute | solution.py:12
  197.3 88.0 %collective-permute-start.1 = (s32[1,256]{1,0:T(1,128)S(1)}, s32[1,256]{1,0:T(1,128)S(1)}, u32[]{:S(2)}, u32[]{:S(2)}) collective-permute-start(s32[1,256]{1,0:T(1,128)S(1)} %copy-done.9), channel_id=1, source_target_pairs={{28,0},{0,4},{4,8},{8,12},{12,16},{16,20},{20,24},{24,28},{29,1},{... | collective-permute-start | bytes 3080 | tf_op jit(solution)/shard_map/ppermute | solution.py:12
  285.3 5.6 collective-permute-start.4
  291.0 13.8 %collective-permute-start.7 = (s32[1,256]{1,0:T(1,128)S(1)}, s32[1,256]{1,0:T(1,128)S(1)}, u32[]{:S(2)}, u32[]{:S(2)}) collective-permute-start(s32[1,256]{1,0:T(1,128)S(1)} %collective-permute-done.4), channel_id=1, source_target_pairs={{28,0},{0,4},{4,8},{8,12},{12,16},{16,20},{20,24},{24,28},{29,1},{... | collective-permute-start | bytes 3080 | tf_op jit(solution)/shard_map/ppermute | solution.py:12
  312.2 3.9 copy-start.3
  325.8 3.9 copy-start.4
  339.4 4.4 copy-start.6
  339.4 137.3 %collective-permute-start.9 = (bf16[1,256,2,16,256]{4,3,2,1,0:T(8,128)(2,1)}, bf16[1,256,2,16,256]{4,3,2,1,0:T(8,128)(2,1)}, u32[]{:S(2)}, u32[]{:S(2)}) collective-permute-start(bf16[1,256,2,16,256]{4,3,2,1,0:T(8,128)(2,1)} %collective-permute-done.6), channel_id=1, source_target_pairs={{28,0},{0,4},{4,8},{8,12},{12,16},{16,20},{20,24},{24,28},{29,1},{... | collective-permute-start | bytes 12582920 | tf_op jit(solution)/shard_map/ppermute | solution.py:12
  430.4 1.9 copy-start.10
  440.5 30.0 %all-to-all-start.1 = ((f32[2,4,256,256]{3,2,0,1:T(8,128)}), f32[2,4,256,256]{3,2,0,1:T(8,128)}, u32[]{:S(2)}, u32[]{:S(2)}) async-start(f32[2,4,256,256]{3,2,0,1:T(8,128)} %copy.22), calls=%async_computation.1 | async-start | bytes 4194304 | tf_op jit(solution)/shard_map/all_to_all | solution.py:67
  462.4 2.8 collective-permute-start.10
  470.5 30.2 %all-to-all-start = ((f32[2,4,256,256]{3,2,0,1:T(8,128)}), f32[2,4,256,256]{3,2,0,1:T(8,128)}, u32[]{:S(2)}, u32[]{:S(2)}) async-start(f32[2,4,256,256]{3,2,0,1:T(8,128)} %copy.19), calls=%async_computation | async-start | bytes 4194304 | tf_op jit(solution)/shard_map/all_to_all | solution.py:67
  500.6 30.4 %all-to-all-start.2 = ((f32[2,4,256,256]{3,2,0,1:T(8,128)}), f32[2,4,256,256]{3,2,0,1:T(8,128)}, u32[]{:S(2)}, u32[]{:S(2)}) async-start(f32[2,4,256,256]{3,2,0,1:T(8,128)} %copy.25), calls=%async_computation.2 | async-start | bytes 4194304 | tf_op jit(solution)/shard_map/all_to_all | solution.py:67
  526.2 49.9 %collective-permute-start.2 = (f32[2,4,256,256]{3,2,1,0:T(8,128)}, f32[2,4,256,256]{3,2,1,0:T(8,128)}, u32[]{:S(2)}, u32[]{:S(2)}) collective-permute-start(f32[2,4,256,256]{3,2,1,0:T(8,128)} %copy.20), channel_id=1, source_target_pairs={{4,0},{8,4},{12,8},{16,12},{20,16},{24,20},{28,24},{0,28},{5,1},{9... | collective-permute-start | bytes 6291464 | tf_op jit(solution)/shard_map/ppermute | solution.py:12
  529.8 48.6 %collective-permute-start.5 = (f32[2,4,256,256]{3,2,1,0:T(8,128)}, f32[2,4,256,256]{3,2,1,0:T(8,128)}, u32[]{:S(2)}, u32[]{:S(2)}) collective-permute-start(f32[2,4,256,256]{3,2,1,0:T(8,128)} %copy.23), channel_id=1, source_target_pairs={{8,0},{12,4},{16,8},{20,12},{24,16},{28,20},{0,24},{4,28},{9,1},{1... | collective-permute-start | bytes 6291464 | tf_op jit(solution)/shard_map/ppermute | solution.py:12
  534.2 177.4 %collective-permute-start.8 = (f32[2,4,256,256]{3,2,1,0:T(8,128)}, f32[2,4,256,256]{3,2,1,0:T(8,128)}, u32[]{:S(2)}, u32[]{:S(2)}) collective-permute-start(f32[2,4,256,256]{3,2,1,0:T(8,128)} %copy.26), channel_id=1, source_target_pairs={{12,0},{16,4},{20,8},{24,12},{28,16},{0,20},{4,24},{8,28},{13,1},{... | collective-permute-start | bytes 6291464 | tf_op jit(solution)/shard_map/ppermute | solution.py:12
  555.8 2.1 copy-start.8
  558.0 1.6 copy-start.1
  559.6 18.4 %copy-start = (f32[1024,2,256]{2,0,1:T(8,128)S(1)}, f32[1024,2,256]{2,0,1:T(8,128)}, u32[]{:S(2)}) copy-start(f32[1024,2,256]{2,0,1:T(8,128)} %copy.21) | copy-start | bytes 6291460
  580.3 133.1 %copy-start.7 = (f32[2,1024,256]{2,1,0:T(8,128)S(1)}, f32[2,1024,256]{2,1,0:T(8,128)}, u32[]{:S(2)}) copy-start(f32[2,1024,256]{2,1,0:T(8,128)} %copy.27) | copy-start | bytes 6291460
  713.8 6.2 copy-start.2
Sparse Core Ops, SparseCore 0:
  8.9 106.2 all-gather.2
where the time goes:
time: 733 us; the launch traced here: 727 us
  waiting for transfers between devices  429 us (59%)
  local copies, waits for them, and re-layouts  111 us (15%)
  matrix products  77 us (11%)
  other arithmetic  50.1 us (7%)
  starting transfers between devices  37 us (5%)
  between operations  14 us (2%)
  blocking collectives  9.42 us (1%)
    ppermute x11, waiting for transfers between devices, from_behind(): return lax.ppermute(block, axis, route)  419 us
    dot_general x5, matrix products, cross_tile(): lax.dot_general(rows_flat, stacked, (((1,), (1,)), ((), ())), preferred_e...  77 us
    reshape x5, local copies, waits for them, and re-layouts, cross_tile(): flattened = col_spec.reshape(shard_rows, full_width)  37.1 us
    reduce_sum x6, other arithmetic, factors(): power_mean = jnp.mean(widened * widened, axis=1) + 1e-06  29 us
    reshape x1, local copies, waits for them, and re-layouts, shards(): rows_flat = row_spec.reshape(row_count, full_width)  25.5 us
    all_to_all x3, starting transfers between devices, shards(): lax.all_to_all(flipped, 'grp', split_axis=1, concat_axis=1, tiled=True)  18.8 us
    ppermute x11, starting transfers between devices, from_behind(): return lax.ppermute(block, axis, route)  18.1 us
    neg x5, other arithmetic, cross_tile(): -flattened[:, half_width:]  15.8 us
  transfers between devices with their start and end apart: 15, of which 11 were waited for; matrix products, arithmetic and copies ran while one was open for 31% of the time, Pallas kernels for 0%

commit v1 on v0

v1 whole, which is shorter than its diff:
```python
import functools
import math

import jax
import jax.numpy as jnp
from jax import lax
from jax.experimental import pallas as pl
from jax.experimental.pallas import tpu as pltpu
from jax.sharding import PartitionSpec as P

NT = (((1,), (1,)), ((), ()))


def tile_of(size, most):
    tile = 1
    while tile * 2 <= most and size % (tile * 2) == 0:
        tile *= 2
    return tile


def factors(flattened, flag_vals):
    widened = flattened.astype(jnp.float32)
    power_mean = jnp.mean(widened * widened, axis=1) + 1e-06
    return flag_vals.astype(jnp.float32) * lax.rsqrt(power_mean)


def tile_body(pieces, steps, slot_ref, real_ref, imag_ref, *refs):
    col_real, col_imag = refs[:pieces], refs[pieces : 2 * pieces]
    row_factor, col_factor = refs[2 * pieces : 2 * pieces + 2]
    out_ref, total = refs[-2:]
    step = pl.program_id(1)
    rows_real, rows_imag = real_ref[...], imag_ref[...]
    cols_real = jnp.concatenate([ref[...] for ref in col_real], axis=0)
    cols_imag = jnp.concatenate([ref[...] for ref in col_imag], axis=0)

    def dot(left, right):
        return lax.dot_general(left, right, NT, preferred_element_type=jnp.float32)

    real = dot(rows_real, cols_real) + dot(rows_imag, cols_imag)
    imag = dot(rows_imag, cols_real) - dot(rows_real, cols_imag)

    @pl.when(step == 0)
    def _():
        total[0] = real
        total[1] = imag

    @pl.when(step > 0)
    def _():
        total[0] += real
        total[1] += imag

    @pl.when(step == steps - 1)
    def _():
        scaling = row_factor[...] * col_factor[...]
        out_ref[0] = total[0] * scaling
        out_ref[1] = total[1] * scaling


def put_tile(output_tile, rows, pieces, slot, row_factor, col_factor):
    row_count, full_width = rows.shape
    half_width = full_width // 2
    shard_rows = sum(piece.shape[0] for piece in pieces)
    depth = tile_of(half_width, 1024)
    high = tile_of(row_count, 1024)
    steps = half_width // depth
    count = len(pieces)
    specs = [
        pl.BlockSpec((high, depth), lambda i, k, s: (i, k)),
        pl.BlockSpec((high, depth), lambda i, k, s: (i, k + steps)),
    ]
    specs += [pl.BlockSpec((p.shape[0], depth), lambda i, k, s: (0, k)) for p in pieces]
    specs += [pl.BlockSpec((p.shape[0], depth), lambda i, k, s: (0, k + steps)) for p in pieces]
    specs += [
        pl.BlockSpec((high, 1), lambda i, k, s: (i, 0)),
        pl.BlockSpec((1, shard_rows), lambda i, k, s: (0, s[0])),
    ]
    operands = [slot.reshape(1), rows, rows, *pieces, *pieces, row_factor, col_factor]
    aliases = {}
    if output_tile is not None:
        specs.append(pl.BlockSpec(memory_space=pl.ANY))
        aliases = {len(operands): 0}
        operands.append(output_tile)
    return pl.pallas_call(
        functools.partial(tile_body, count, steps),
        grid_spec=pltpu.PrefetchScalarGridSpec(
            num_scalar_prefetch=1,
            grid=(row_count // high, steps),
            in_specs=specs,
            out_specs=pl.BlockSpec((2, high, shard_rows), lambda i, k, s: (0, i, s[0])),
            scratch_shapes=[pltpu.VMEM((2, high, shard_rows), jnp.float32)],
        ),
        out_shape=jax.ShapeDtypeStruct((2, row_count, col_factor.shape[1]), jnp.float32),
        input_output_aliases=aliases,
        cost_estimate=pl.CostEstimate(
            flops=4 * row_count * shard_rows * full_width,
            bytes_accessed=2 * full_width * (row_count + shard_rows) + 8 * row_count * shard_rows,
            transcendentals=0,
        ),
        compiler_params=pltpu.CompilerParams(dimension_semantics=("arbitrary", "arbitrary")),
    )(*operands)


def cycle_of(count):
    return list(range(0, count, 2)) + list(range(count - 1, 0, -2))


def gathered(flattened, own_factor, scale_coef):
    half_width = flattened.shape[1] // 2
    rows = lax.all_gather(flattened, "grp", axis=0, tiled=True)
    cols = lax.all_gather(flattened, "blk", axis=0, tiled=True)
    row_factor = lax.all_gather(own_factor, "grp", axis=0, tiled=True) * scale_coef
    col_factor = lax.all_gather(own_factor, "blk", axis=0, tiled=True)
    rotated = jnp.concatenate([-cols[:, half_width:], cols[:, :half_width]], axis=1)
    scaling = row_factor[:, None] * col_factor[None, :]
    parts = [
        lax.dot_general(rows, right, NT, preferred_element_type=jnp.float32) * scaling
        for right in (cols, rotated)
    ]
    return jnp.stack(parts)


def shards(spectra, detector_valid):
    shard_rows = spectra.shape[1]
    half_width = spectra.shape[3] * spectra.shape[4]
    cycle_size = lax.axis_size("blk")
    group_size = lax.axis_size("grp")
    scale_coef = 0.5 / math.sqrt(half_width)
    flattened = spectra.reshape(shard_rows, 2 * half_width)
    own_factor = factors(flattened, detector_valid.reshape(shard_rows))
    shape = (2, group_size, shard_rows, cycle_size * shard_rows)
    if shard_rows % 128 or half_width % 128 or cycle_size % 2 or cycle_size < 4:
        return gathered(flattened, own_factor, scale_coef).reshape(shape)

    ring = cycle_of(cycle_size)
    onward = [(ring[i], ring[(i + 1) % cycle_size]) for i in range(cycle_size)]
    backward = [(there, here) for here, there in onward]
    place = jnp.array([ring.index(i) for i in range(cycle_size)], jnp.int32)[lax.axis_index("blk")]
    at = jnp.array(ring + ring, jnp.int32)

    rows = lax.all_gather(flattened, "grp", axis=0, tiled=True)
    row_factor = lax.all_gather(own_factor, "grp", axis=0, tiled=True) * scale_coef
    col_factor = lax.all_gather(own_factor, "blk", axis=0, tiled=True)

    def put(output_tile, pieces, offset):
        slot = at[place + offset % cycle_size]
        return put_tile(output_tile, rows, pieces, slot, row_factor[:, None], col_factor[None, :])

    half = shard_rows // 2
    last = cycle_size // 2
    low, high = flattened, flattened
    waiting = [((flattened,), 0)]
    output_tile = None
    for offset in range(1, last + 1):
        if offset == last:
            low, high = low[:half], high[half:]
        low = lax.ppermute(low, "blk", onward)
        high = lax.ppermute(high, "blk", backward)
        if offset > 1:
            for pieces, behind in waiting:
                output_tile = put(output_tile, pieces, behind)
            waiting = []
        if offset == last:
            output_tile = put(output_tile, (low, high), last)
        else:
            waiting += [((low,), -offset), ((high,), offset)]
            if offset > 1:
                low, high, output_tile = lax.optimization_barrier((low, high, output_tile))
    return output_tile.reshape(shape)


def solution(mesh):
    return jax.shard_map(
        shards,
        mesh=mesh,
        in_specs=(P("grp", "blk", None, None, None), P("grp", "blk")),
        out_specs=P(None, None, "blk", "grp"),
        check_vma=False,
    )
```

time: 733 us -> 423 us (0.58)
  the two profiles are of different devices: /device:TPU:31 before, /device:TPU:0 now
where the time goes in v1:
time: 423 us; the launch traced here: 422 us
  waiting for transfers between devices  155 us (37%)
  Pallas kernels  126 us (30%)
  blocking collectives  87.3 us (21%)
  between operations  24.5 us (6%)
  local copies, waits for them, and re-layouts  15.9 us (4%)
  starting transfers between devices  9.24 us (2%)
    ppermute x4, waiting for transfers between devices, shards(): low = lax.ppermute(low, 'blk', onward)  152 us
    pallas_call x8, Pallas kernels, put_tile(): pl.pallas_call(functools.partial(tile_body, count, steps), grid_spec=pltp...  126 us
    all_gather x1, blocking collectives, shards(): col_factor = lax.all_gather(own_factor, 'blk', axis=0, tiled=True)  82.2 us
  transfers between devices with their start and end apart: 9, of which 5 were waited for; matrix products, arithmetic and copies ran while one was open for 2% of the time, Pallas kernels for 26%

profile of v1, /device:TPU:0, one launch (start us, length us, event | category | flops | bytes accessed | tf_op | source)
XLA Modules:
  0.0 422.4 jit_solution(5214229572499905257)
XLA Ops:
  6.5 7.4 %reshape.8.refs_0_.refs_1_ = bf16[256,8192]{1,0:T(8,128)(2,1)} reshape(bf16[1,256,2,16,256]{4,3,2,1,0:T(8,128)(2,1)} %param.4) | data formatting | bytes 8388608 | tf_op jit(solution)/shard_map/reshape | solution.py:128
  13.9 0.0 all-gather.4.cloned.1.call-update
  14.0 3.1 collective-permute-start
  17.1 0.0 collective-permute-start.2
  17.1 90.8 %collective-permute-done.refs_0_.refs_1_ = bf16[256,8192]{1,0:T(8,128)(2,1)} collective-permute-done((bf16[256,8192]{1,0:T(8,128)(2,1)}, bf16[256,8192]{1,0:T(8,128)(2,1)}, u32[]{:S(2)}, u32[]{:S(2)}) %collective-permute-start) | collective-permute-done | bytes 4194336 | tf_op jit(solution)/shard_map/ppermute | solution.py:156
  107.9 1.8 collective-permute-start.1
  109.7 0.0 collective-permute-done.2.refs_0_.refs_1_
  109.7 0.2 collective-permute-start.3
  109.9 0.6 dynamic_slice.27
  120.9 3.9 multiply_reduce_fusion
  124.8 5.1 %all-gather = f32[4,1,256]{2,1,0:T(1,128)S(1)} all-gather(f32[1,1,256]{2,1,0:T(1,128)S(1)} %bitcast.17), channel_id=1, replica_groups=mesh['blk'=8,'grp'=4] {'grp'}, dimensions={0}, use_global_device_ids=true | all-gather | bytes 5120 | tf_op jit(solution)/shard_map/all_gather | solution.py:141
  129.9 1.0 copy.22.refs_2_.refs_4_
  131.6 0.7 fusion
  132.3 82.2 %all-gather.1 = f32[8,1,256]{2,1,0:T(1,128)} all-gather(f32[1,1,256]{2,1,0:T(1,128)S(1)} %bitcast.18), channel_id=1, replica_groups=mesh['blk'=8,'grp'=4] {'blk'}, dimensions={0}, use_global_device_ids=true | all-gather | bytes 9216 | tf_op jit(solution)/shard_map/all_gather | solution.py:142
  214.5 15.8 %shard_map.46.refs_4_ = f32[2,1024,2048]{2,1,0:T(8,128)} custom-call(s32[1]{0:T(128)} %get-tuple-element.20.slot_ref, bf16[1024,8192]{1,0:T(8,128)(2,1)} %all-gather.4.cloned.1.call-done.real_ref.imag_ref, bf16[1024,8192]{1,0:T(8,128)(2,1)} %all-gather.4.cloned.1.call-done.real_ref.imag_ref, bf16[256,8192]{1,0:T(8,128)(2,1)} %reshape.8.refs_0_.refs_1_, ...), custom_call_target="tpu_custom_call" | custom-call | flops 8589934592 | bytes 23068672 | tf_op jit(solution)/shard_map/pallas_call | solution.py:83
  230.3 15.7 %shard_map.47.refs_4_ = f32[2,1024,2048]{2,1,0:T(8,128)} custom-call(s32[1]{0:T(128)} %get-tuple-element.21.slot_ref, bf16[1024,8192]{1,0:T(8,128)(2,1)} %all-gather.4.cloned.1.call-done.real_ref.imag_ref, bf16[1024,8192]{1,0:T(8,128)(2,1)} %all-gather.4.cloned.1.call-done.real_ref.imag_ref, ...), custom_call_target="tpu_custom_call", output_to_operand_aliasing={{}: (7, {})} | custom-call | flops 8589934592 | bytes 23068672 | tf_op jit(solution)/shard_map/pallas_call | solution.py:83
  246.0 15.8 %shard_map.48.refs_4_ = f32[2,1024,2048]{2,1,0:T(8,128)} custom-call(s32[1]{0:T(128)} %get-tuple-element.22.slot_ref, bf16[1024,8192]{1,0:T(8,128)(2,1)} %all-gather.4.cloned.1.call-done.real_ref.imag_ref, bf16[1024,8192]{1,0:T(8,128)(2,1)} %all-gather.4.cloned.1.call-done.real_ref.imag_ref, ...), custom_call_target="tpu_custom_call", output_to_operand_aliasing={{}: (7, {})} | custom-call | flops 8589934592 | bytes 23068672 | tf_op jit(solution)/shard_map/pallas_call | solution.py:83
  261.8 0.1 collective-permute-start.4
  261.9 2.0 collective-permute-start.5
  263.9 15.8 %shard_map.49.refs_4_ = f32[2,1024,2048]{2,1,0:T(8,128)} custom-call(s32[1]{0:T(128)} %get-tuple-element.18.slot_ref, bf16[1024,8192]{1,0:T(8,128)(2,1)} %all-gather.4.cloned.1.call-done.real_ref.imag_ref, bf16[1024,8192]{1,0:T(8,128)(2,1)} %all-gather.4.cloned.1.call-done.real_ref.imag_ref, ...), custom_call_target="tpu_custom_call", output_to_operand_aliasing={{}: (7, {})} | custom-call | flops 8589934592 | bytes 23068672 | tf_op jit(solution)/shard_map/pallas_call | solution.py:83
  279.7 15.7 %shard_map.50.refs_4_ = f32[2,1024,2048]{2,1,0:T(8,128)} custom-call(s32[1]{0:T(128)} %get-tuple-element.19.slot_ref, bf16[1024,8192]{1,0:T(8,128)(2,1)} %all-gather.4.cloned.1.call-done.real_ref.imag_ref, bf16[1024,8192]{1,0:T(8,128)(2,1)} %all-gather.4.cloned.1.call-done.real_ref.imag_ref, ...), custom_call_target="tpu_custom_call", output_to_operand_aliasing={{}: (7, {})} | custom-call | flops 8589934592 | bytes 23068672 | tf_op jit(solution)/shard_map/pallas_call | solution.py:83
  295.4 55.0 %collective-permute-done.4.refs_0_.refs_1_ = bf16[256,8192]{1,0:T(8,128)(2,1)} collective-permute-done((bf16[256,8192]{1,0:T(8,128)(2,1)}, bf16[256,8192]{1,0:T(8,128)(2,1)}, u32[]{:S(2)}, u32[]{:S(2)}) %collective-permute-start.4) | collective-permute-done | bytes 4194336 | tf_op jit(solution)/shard_map/ppermute | solution.py:156
  350.5 0.2 collective-permute-done.5.refs_0_.refs_1_
  350.7 3.1 slice.6
  353.8 0.0 collective-permute-start.6
  353.9 3.1 slice.7
  356.9 2.0 collective-permute-start.7
  358.9 15.9 %shard_map.51.refs_4_ = f32[2,1024,2048]{2,1,0:T(8,128)} custom-call(s32[1]{0:T(128)} %get-tuple-element.17.slot_ref, bf16[1024,8192]{1,0:T(8,128)(2,1)} %all-gather.4.cloned.1.call-done.real_ref.imag_ref, bf16[1024,8192]{1,0:T(8,128)(2,1)} %all-gather.4.cloned.1.call-done.real_ref.imag_ref, ...), custom_call_target="tpu_custom_call", output_to_operand_aliasing={{}: (7, {})} | custom-call | flops 8589934592 | bytes 23068672 | tf_op jit(solution)/shard_map/pallas_call | solution.py:83
  374.8 15.8 %shard_map.52.refs_6_ = f32[2,1024,2048]{2,1,0:T(8,128)} custom-call(s32[1]{0:T(128)} %get-tuple-element.24.slot_ref, bf16[1024,8192]{1,0:T(8,128)(2,1)} %all-gather.4.cloned.1.call-done.real_ref.imag_ref, bf16[1024,8192]{1,0:T(8,128)(2,1)} %all-gather.4.cloned.1.call-done.real_ref.imag_ref, ...), custom_call_target="tpu_custom_call", output_to_operand_aliasing={{}: (7, {})} | custom-call | flops 8589934592 | bytes 23068672 | tf_op jit(solution)/shard_map/pallas_call | solution.py:83
  390.6 5.9 %collective-permute-done.6.refs_0_.refs_2_ = bf16[128,8192]{1,0:T(8,128)(2,1)S(1)} collective-permute-done((bf16[128,8192]{1,0:T(8,128)(2,1)}, bf16[128,8192]{1,0:T(8,128)(2,1)S(1)}, u32[]{:S(2)}, u32[]{:S(2)}) %collective-permute-start.6) | collective-permute-done | bytes 2097184 | tf_op jit(solution)/shard_map/ppermute | solution.py:156
  396.5 3.2 collective-permute-done.7.refs_1_.refs_3_
  399.7 15.8 %shard_map.53 = f32[2,1024,2048]{2,1,0:T(8,128)} custom-call(s32[1]{0:T(128)} %get-tuple-element.23.slot_ref, bf16[1024,8192]{1,0:T(8,128)(2,1)} %all-gather.4.cloned.1.call-done.real_ref.imag_ref, bf16[1024,8192]{1,0:T(8,128)(2,1)} %all-gather.4.cloned.1.call-done.real_ref.imag_ref, bf16[128,8192]{1,0:T(8,128)(2,1)} %copy-done, ...), custom_call_target="tpu_custom_call", output_to_operand_aliasing={{}: (9, {})} | custom-call | flops 8589934592 | bytes 23068672 | tf_op jit(solution)/shard_map/pallas_call | solution.py:83
  (15 shorter events, 0.0 us)
Async XLA Ops:
  6.5 208.0 %all-gather.4.cloned.1.call-start = ((), (), s32[]{:S(2)}) async-start(), calls=%async_computation | async-start | bytes 20971520 | tf_op jit(solution)/shard_map/all_gather | solution.py:140
  13.9 96.0 %copy-start.3 = (s32[8]{0:T(128)S(1)}, s32[8]{0:T(128)}, u32[]{:S(2)}) copy-start(s32[8]{0:T(128)} %constant.53.clone) | copy-start | bytes 100
  13.9 106.9 %copy-start.2 = (s32[1,256]{1,0:T(1,128)S(1)}, s32[1,256]{1,0:T(1,128)}, u32[]{:S(2)}) copy-start(s32[1,256]{1,0:T(1,128)} %param.5) | copy-start | bytes 3076
  13.9 117.6 %copy-start.1 = (s32[16]{0:T(128)S(1)}, s32[16]{0:T(128)}, u32[]{:S(2)}) copy-start(s32[16]{0:T(128)} %constant.54.clone) | copy-start | bytes 196
  14.0 93.9 %collective-permute-start = (bf16[256,8192]{1,0:T(8,128)(2,1)}, bf16[256,8192]{1,0:T(8,128)(2,1)}, u32[]{:S(2)}, u32[]{:S(2)}) collective-permute-start(bf16[256,8192]{1,0:T(8,128)(2,1)} %reshape.8.refs_0_.refs_1_), channel_id=1, source_target_pairs={{0,8},{8,16},{16,24},{24,28},{28,20},{20,12},{12,4},{4,0},{1,9},{9... | collective-permute-start | bytes 12582920 | tf_op jit(solution)/shard_map/ppermute | solution.py:156
  17.1 92.6 %collective-permute-start.2 = (bf16[256,8192]{1,0:T(8,128)(2,1)}, bf16[256,8192]{1,0:T(8,128)(2,1)}, u32[]{:S(2)}, u32[]{:S(2)}) collective-permute-start(bf16[256,8192]{1,0:T(8,128)(2,1)} %reshape.8.refs_0_.refs_1_), channel_id=1, source_target_pairs={{8,0},{16,8},{24,16},{28,24},{20,28},{12,20},{4,12},{0,4},{9,1},{1... | collective-permute-start | bytes 12582920 | tf_op jit(solution)/shard_map/ppermute | solution.py:157
  107.9 153.9 %collective-permute-start.1 = (bf16[256,8192]{1,0:T(8,128)(2,1)}, bf16[256,8192]{1,0:T(8,128)(2,1)}, u32[]{:S(2)}, u32[]{:S(2)}) collective-permute-start(bf16[256,8192]{1,0:T(8,128)(2,1)} %collective-permute-done.refs_0_.refs_1_), channel_id=1, source_target_pairs={{0,8},{8,16},{16,24},{24,28},{28,20},{20,12},{12,4},{4,0},{1,9},{9... | collective-permute-start | bytes 12582920 | tf_op jit(solution)/shard_map/ppermute | solution.py:156
  109.7 152.1 %collective-permute-start.3 = (bf16[256,8192]{1,0:T(8,128)(2,1)}, bf16[256,8192]{1,0:T(8,128)(2,1)}, u32[]{:S(2)}, u32[]{:S(2)}) collective-permute-start(bf16[256,8192]{1,0:T(8,128)(2,1)} %collective-permute-done.2.refs_0_.refs_1_), channel_id=1, source_target_pairs={{8,0},{16,8},{24,16},{28,24},{20,28},{12,20},{4,12},{0,4},{9,1},{1... | collective-permute-start | bytes 12582920 | tf_op jit(solution)/shard_map/ppermute | solution.py:157
  261.8 88.6 %collective-permute-start.4 = (bf16[256,8192]{1,0:T(8,128)(2,1)}, bf16[256,8192]{1,0:T(8,128)(2,1)}, u32[]{:S(2)}, u32[]{:S(2)}) collective-permute-start(bf16[256,8192]{1,0:T(8,128)(2,1)} %collective-permute-done.1.refs_0_.refs_1_), channel_id=1, source_target_pairs={{0,8},{8,16},{16,24},{24,28},{28,20},{20,12},{12,4},{4,0},{1,9},{9... | collective-permute-start | bytes 12582920 | tf_op jit(solution)/shard_map/ppermute | solution.py:156
  261.9 88.8 %collective-permute-start.5 = (bf16[256,8192]{1,0:T(8,128)(2,1)}, bf16[256,8192]{1,0:T(8,128)(2,1)}, u32[]{:S(2)}, u32[]{:S(2)}) collective-permute-start(bf16[256,8192]{1,0:T(8,128)(2,1)} %collective-permute-done.3.refs_0_.refs_1_), channel_id=1, source_target_pairs={{8,0},{16,8},{24,16},{28,24},{20,28},{12,20},{4,12},{0,4},{9,1},{1... | collective-permute-start | bytes 12582920 | tf_op jit(solution)/shard_map/ppermute | solution.py:157
  353.8 42.7 %collective-permute-start.6 = (bf16[128,8192]{1,0:T(8,128)(2,1)}, bf16[128,8192]{1,0:T(8,128)(2,1)S(1)}, u32[]{:S(2)}, u32[]{:S(2)}) collective-permute-start(bf16[128,8192]{1,0:T(8,128)(2,1)} %slice.6), channel_id=1, source_target_pairs={{0,8},{8,16},{16,24},{24,28},{28,20},{20,12},{12,4},{4,0},{1,9},{9... | collective-permute-start | bytes 6291464 | tf_op jit(solution)/shard_map/ppermute | solution.py:156
  356.9 42.8 %collective-permute-start.7 = (bf16[128,8192]{1,0:T(8,128)(2,1)}, bf16[128,8192]{1,0:T(8,128)(2,1)}, u32[]{:S(2)}, u32[]{:S(2)}) collective-permute-start(bf16[128,8192]{1,0:T(8,128)(2,1)} %slice.7), channel_id=1, source_target_pairs={{8,0},{16,8},{24,16},{28,24},{20,28},{12,20},{4,12},{0,4},{9,1},{1... | collective-permute-start | bytes 6291464 | tf_op jit(solution)/shard_map/ppermute | solution.py:157
  396.5 3.2 copy-start
Sparse Core Ops, SparseCore 0:
  14.1 108.6 all-gather.3

commit v2 on v0

v2 whole, which is shorter than its diff:
```python
import functools
import math

import jax
import jax.numpy as jnp
from jax import lax
from jax.experimental import pallas as pl
from jax.experimental.pallas import tpu as pltpu
from jax.sharding import PartitionSpec as P


NT = (((1,), (1,)), ((), ()))
LANES = 128
FLOOR = 1e-30


def tile_of(size, most):
    tile = 1
    while tile * 2 <= most and size % (tile * 2) == 0:
        tile *= 2
    return tile


def exchange(value, axis, pairs):
    return lax.ppermute(value, axis, pairs)


def tied(*values):
    return lax.optimization_barrier(values)


def split_in_three(value):
    parts = []
    for _ in range(2):
        part = value.astype(jnp.bfloat16).astype(jnp.float32)
        parts.append(part)
        value = value - part
    return parts + [value]


def laid_out_body(spectra_ref, flags_ref, out_ref):
    high, parts, bins, taps = spectra_ref.shape
    half_width = bins * taps
    power = jnp.zeros((high, 1), jnp.float32)
    for part in range(parts):
        flat = spectra_ref[:, part].reshape(high, half_width)
        out_ref[:, part * half_width : (part + 1) * half_width] = flat
        widened = flat.astype(jnp.float32)
        power = power + jnp.sum(widened * widened, axis=1, keepdims=True)
    power_mean = power / (parts * half_width)
    factor = flags_ref[...].astype(jnp.float32) * lax.rsqrt(power_mean + 1e-06)
    norm = lax.rsqrt(jnp.maximum(power_mean, FLOOR))
    lane = lax.broadcasted_iota(jnp.int32, (high, LANES), 1)
    marks = jnp.zeros((high, LANES), jnp.float32)
    for index, value in enumerate(split_in_three(factor) + split_in_three(norm)):
        marks = jnp.where(lane == index, value, marks)
    out_ref[:, parts * half_width :] = marks.astype(jnp.bfloat16)


def laid_out(spectra, flags):
    rows, parts, bins, taps = spectra.shape
    width = parts * bins * taps + LANES
    high = tile_of(rows, 64)
    return pl.pallas_call(
        laid_out_body,
        grid=(rows // high,),
        in_specs=[
            pl.BlockSpec((high, parts, bins, taps), lambda i: (i, 0, 0, 0)),
            pl.BlockSpec((high, 1), lambda i: (i, 0)),
        ],
        out_specs=pl.BlockSpec((high, width), lambda i: (i, 0)),
        out_shape=jax.ShapeDtypeStruct((rows, width), spectra.dtype),
    )(spectra, flags.reshape(rows, 1))


def products_body(sizes, scale_coef, raw, plan_ref, *refs):
    row_total, shapes, kept, units, steps = sizes
    refs = list(refs)

    def take(count):
        taken = refs[:count]
        del refs[:count]
        return taken

    rows_real, rows_imag, row_marks = take(row_total), take(row_total), take(row_total)
    columns = [(take(len(s)), take(len(s)), take(len(s))) for s in shapes]
    placed = [take(2) for _ in range(kept)]
    total, right = refs[-2:]
    outs = refs[-4:-2] if raw else refs[-3:-2]
    out_ref = outs[0]
    unit, step = pl.program_id(0), pl.program_id(1)
    chosen = plan_ref[unit]
    depth = rows_real[0].shape[1]
    shard_rows = right.shape[0] // 2

    def marks_of(values, first):
        return (values[first + 2] + values[first + 1]) + values[first]

    def column_marks(marks):
        flipped = jnp.concatenate([m[...] for m in marks], axis=0).astype(jnp.float32).T
        rows = [flipped[i : i + 1] for i in range(6)]
        return marks_of(rows, 0), marks_of(rows, 3)

    def marks_of_rows(ref):
        values = ref[...].astype(jnp.float32)
        values = [values[:, i : i + 1] for i in range(6)]
        return marks_of(values, 0), marks_of(values, 3)

    for index, (reals, imags, _) in enumerate(columns):

        @pl.when(chosen == index)
        def _():
            at = 0
            for real_ref, imag_ref in zip(reals, imags):
                end = at + real_ref.shape[0]
                right[at:end, :depth] = real_ref[...]
                right[at:end, depth:] = imag_ref[...]
                right[shard_rows + at : shard_rows + end, :depth] = -imag_ref[...]
                right[shard_rows + at : shard_rows + end, depth:] = real_ref[...]
                at = end

    @pl.when(jnp.logical_and(chosen >= 0, chosen < len(columns)))
    def _():
        left = jnp.concatenate(
            [
                jnp.concatenate([ref[...] for ref in rows_real], axis=0),
                jnp.concatenate([ref[...] for ref in rows_imag], axis=0),
            ],
            axis=1,
        )
        product = lax.dot_general(left, right[...], NT, preferred_element_type=jnp.float32)

        @pl.when(step == 0)
        def _():
            total[...] = product

        @pl.when(step > 0)
        def _():
            total[...] += product

    for index, (_, _, marks) in enumerate(columns):

        @pl.when(jnp.logical_and(chosen == index, step == steps - 1))
        def _():
            col_factor, col_norm = column_marks(marks)
            if raw:
                outs[1][...] = jnp.broadcast_to(col_factor / col_norm, outs[1].shape)
            for row in range(row_total):
                row_factor, row_norm = marks_of_rows(row_marks[row])
                scaling = row_norm * col_norm if raw else (row_factor * scale_coef) * col_factor
                group = plan_ref[2 * units + row]
                held = slice(row * shard_rows, (row + 1) * shard_rows)
                out_ref[0, group] = total[held, :shard_rows] * scaling
                out_ref[1, group] = total[held, shard_rows:] * scaling

    for index, (block_ref, ratio_ref) in enumerate(placed):

        @pl.when(jnp.logical_and(chosen == len(columns) + index, step == steps - 1))
        def _():
            ratio = ratio_ref[0:1]
            for row in range(row_total):
                row_factor, row_norm = marks_of_rows(row_marks[row])
                scaling = (row_factor / row_norm * scale_coef) * ratio
                group = plan_ref[2 * units + row]
                out_ref[0, group] = block_ref[0, group] * scaling
                out_ref[1, group] = block_ref[1, group] * scaling


def products(out, rows, columns, placed, choice, slots, groups, blocks, scale_coef, raw=False):
    shard_rows, width = rows[0].shape
    half_width = (width - LANES) // 2
    depth = tile_of(half_width, 1024)
    steps = half_width // depth
    units = len(choice)
    count = len(rows)
    last = (width - LANES) // LANES

    def fixed(row_height, first):
        return pl.BlockSpec((row_height, depth), lambda i, k, s: (0, k + first))

    def picked(row_height, index, first):
        return pl.BlockSpec(
            (row_height, depth), lambda i, k, s: (0, jnp.where(s[i] == index, k, 0) + first)
        )

    def marks(row_height):
        return pl.BlockSpec((row_height, LANES), lambda i, k, s: (0, last))

    specs = [fixed(shard_rows, 0)] * count + [fixed(shard_rows, steps)] * count
    specs += [marks(shard_rows)] * count
    operands = list(rows) * 3
    for index, pieces in enumerate(columns):
        specs += [picked(p.shape[0], index, 0) for p in pieces]
        specs += [picked(p.shape[0], index, steps) for p in pieces]
        specs += [marks(p.shape[0]) for p in pieces]
        operands += list(pieces) * 3
    block = (2, count, shard_rows, shard_rows)
    for pair in placed:
        specs.append(pl.BlockSpec(block, lambda i, k, s: (0, 0, 0, 0)))
        specs.append(pl.BlockSpec(pair[1].shape, lambda i, k, s: (0, 0)))
        operands += list(pair)
    plan = jnp.stack(list(choice) + list(slots) + list(groups)).astype(jnp.int32)
    aliases = {}
    if out is not None:
        specs.append(pl.BlockSpec(memory_space=pl.ANY))
        aliases = {1 + len(operands): 0}
        operands.append(out)
    whole = (2, count, shard_rows, shard_rows * (1 if raw else blocks))
    out_shape = [jax.ShapeDtypeStruct(whole, jnp.float32)]
    out_specs = [pl.BlockSpec(block, lambda i, k, s: (0, 0, 0, s[units + i]))]
    if raw:
        out_shape.append(jax.ShapeDtypeStruct((8, shard_rows), jnp.float32))
        out_specs.append(pl.BlockSpec((8, shard_rows), lambda i, k, s: (0, 0)))
    sizes = (count, [[p.shape[0] for p in c] for c in columns], len(placed), units, steps)
    given = pl.pallas_call(
        functools.partial(products_body, sizes, scale_coef, raw),
        grid_spec=pltpu.PrefetchScalarGridSpec(
            num_scalar_prefetch=1,
            grid=(units, steps),
            in_specs=specs,
            out_specs=out_specs,
            scratch_shapes=[
                pltpu.VMEM((count * shard_rows, 2 * shard_rows), jnp.float32),
                pltpu.VMEM((2 * shard_rows, 2 * depth), rows[0].dtype),
            ],
        ),
        out_shape=out_shape,
        input_output_aliases=aliases,
        cost_estimate=pl.CostEstimate(
            flops=8 * units * count * shard_rows * shard_rows * half_width,
            bytes_accessed=4 * units * half_width * (count + 1) * shard_rows,
            transcendentals=0,
        ),
        compiler_params=pltpu.CompilerParams(
            dimension_semantics=("arbitrary", "arbitrary"), vmem_limit_bytes=60 * 2**20
        ),
    )(plan, *operands)
    return given if raw else given[0]


def gathered(spectra, detector_valid, scale_coef):
    shard_rows = spectra.shape[1]
    half_width = spectra.shape[3] * spectra.shape[4]
    flattened = spectra.reshape(shard_rows, 2 * half_width)
    widened = flattened.astype(jnp.float32)
    power_mean = jnp.mean(widened * widened, axis=1) + 1e-06
    own_factor = detector_valid.reshape(shard_rows).astype(jnp.float32) * lax.rsqrt(power_mean)
    rows = lax.all_gather(flattened, "grp", axis=0, tiled=True)
    cols = lax.all_gather(flattened, "blk", axis=0, tiled=True)
    row_factor = lax.all_gather(own_factor, "grp", axis=0, tiled=True) * scale_coef
    col_factor = lax.all_gather(own_factor, "blk", axis=0, tiled=True)
    rotated = jnp.concatenate([-cols[:, half_width:], cols[:, :half_width]], axis=1)
    scaling = row_factor[:, None] * col_factor[None, :]
    parts = [
        lax.dot_general(rows, right, NT, preferred_element_type=jnp.float32) * scaling
        for right in (cols, rotated)
    ]
    return jnp.stack(parts)


def shards(spectra, detector_valid):
    shard_rows = spectra.shape[1]
    half_width = spectra.shape[3] * spectra.shape[4]
    blocks = lax.axis_size("blk")
    group_size = lax.axis_size("grp")
    scale_coef = 0.5 / math.sqrt(half_width)
    shape = (2, group_size, shard_rows, blocks * shard_rows)
    fits = shard_rows % 256 == 0 and half_width % 256 == 0 and group_size & (group_size - 1) == 0
    if blocks != 8 or not fits:
        return gathered(spectra, detector_valid, scale_coef).reshape(shape)

    devices = range(blocks)
    inner = [b for b in devices if 0 < b // 2 < blocks // 2 - 1]
    ends = [b for b in devices if b not in inner]
    me = lax.axis_index("blk")
    mine = lax.axis_index("grp")
    is_end = jnp.logical_or(me // 2 == 0, me // 2 == blocks // 2 - 1)

    def swap(value, among, by):
        return exchange(value, "blk", [(b, b ^ by) for b in among])

    def spread(value, by):
        return exchange(value, "grp", [(g, g ^ by) for g in range(group_size)])

    groups = [mine]
    by = group_size // 2
    while by:
        groups += [g ^ by for g in groups]
        by //= 2

    def over_groups(value):
        arrays, by = [value], group_size // 2
        while by:
            arrays += [spread(array, by) for array in arrays]
            by //= 2
        return arrays

    def either(inner_value, end_value):
        return jnp.where(is_end, end_value, inner_value)

    def put(out, rows, columns, placed, units):
        choice = [either(m, e) for m, e, _, _ in units]
        slots = [either(me ^ m, me ^ e) for _, _, m, e in units]
        return products(
            out, rows, columns, placed, choice, slots, groups, blocks, scale_coef
        )

    own = laid_out(spectra[0], detector_valid[0])
    near = swap(own, devices, 2)
    beside = swap(own, devices, 1)
    across = swap(own, inner, 6)
    rows = over_groups(own)

    across_beside = swap(across, inner, 1)
    near_beside = swap(near, ends, 1)
    end_beside = swap(beside, ends, 2)
    far_inner = swap(across, inner, 2)
    far_end = swap(near, inner, 6)
    client = over_groups(near)
    out = put(
        None,
        rows,
        [(own,), (near,), (beside,), (across,)],
        [],
        [(0, 0, 0, 0), (1, 1, 2, 2), (2, 2, 1, 1), (3, -1, 6, 5)],
    )

    far_end, end_beside, out = tied(far_end, end_beside, out)
    half = shard_rows // 2
    low = swap(far_end[:half], inner, 1)
    high = swap(end_beside[half:], inner, 6)

    def serve(columns):
        choice = [either(0, -1)]
        return products(
            None, client, [columns], [], choice, [me * 0], groups, blocks, scale_coef, raw=True
        )

    def deliver(block, ratio):
        return swap(block.astype(jnp.float16), inner, 2), swap(ratio, inner, 2)

    block_a, ratio_a = serve((across_beside,))
    sent_a = deliver(block_a, ratio_a)
    far_end, ratio_a = tied(far_end, ratio_a)
    block_b, ratio_b = serve((far_end,))
    sent_b = deliver(block_b, ratio_b)
    out, ratio_b = tied(out, ratio_b)
    out = put(out, rows, [(across_beside,), (near_beside,)], [], [(0, 1, 7, 3)])
    low, high, out = tied(low, high, out)
    block_c, ratio_c = serve((low, high))
    sent_c = deliver(block_c, ratio_c)
    out, ratio_c = tied(out, ratio_c)
    out = put(
        out,
        rows,
        [(end_beside,), (far_inner,), (far_end,)],
        [],
        [(0, 1, 3, 4), (2, -1, 4, 6)],
    )
    placed = [(block.astype(jnp.float32), ratio) for block, ratio in (sent_a, sent_b, sent_c)]
    out = put(
        out,
        rows,
        [(low, high)],
        placed,
        [(-1, 1, 5, 5), (-1, 2, 5, 6), (-1, 3, 5, 7), (0, -1, 5, 7)],
    )
    return out.reshape(shape)


def solution(mesh):
    return jax.shard_map(
        shards,
        mesh=mesh,
        in_specs=(P("grp", "blk", None, None, None), P("grp", "blk")),
        out_specs=P(None, None, "blk", "grp"),
        check_vma=False,
    )
```

time: 733 us -> 446 us (0.61)
  waiting for transfers between devices: 429 us -> 225 us
  Pallas kernels: 0 us -> 150 us
  local copies, waits for them, and re-layouts: 111 us -> 14.2 us
  matrix products: 77 us -> 0 us
  other arithmetic: 50.1 us -> 13.1 us
  between operations: 14 us -> 0.36 us
  blocking collectives: 9.42 us -> 0 us
    ppermute x11 -> x22, waiting for transfers between devices: 419 us -> 225 us  [exchange(): return lax.ppermute(value, axis, pairs)]
    pallas_call x0 -> x8, Pallas kernels: none -> 150 us  [the longest x7 144 us: products(): pl.pallas_call(functools.partial(products_body, sizes, scale_coef, raw),...]
    dot_general x5 -> x0, matrix products: 77 us -> none  [cross_tile(): lax.dot_general(rows_flat, stacked, (((1,), (1,)), ((), ())), preferred_e...]
    reshape x9 -> x0, local copies, waits for them, and re-layouts: 68.3 us -> none  [the longest x5 37.1 us: cross_tile(): flattened = col_spec.reshape(shard_rows, full_width)]
    reduce_sum x6 -> x0, other arithmetic: 29 us -> none  [factors(): power_mean = jnp.mean(widened * widened, axis=1) + 1e-06]
    all_to_all x3 -> x0, starting transfers between devices: 18.8 us -> none  [shards(): lax.all_to_all(flipped, 'grp', split_axis=1, concat_axis=1, tiled=True)]
    ppermute x11 -> x22, starting transfers between devices: 18.1 us -> 35.7 us  [exchange(): return lax.ppermute(value, axis, pairs)]
    neg x5 -> x0, other arithmetic: 15.8 us -> none  [cross_tile(): -flattened[:, half_width:]]
  transfers between devices with their start and end apart: 15 -> 22, of which waited for: 11 -> 7; matrix products, arithmetic and copies ran while one was open for 31% -> 5% of each run, Pallas kernels for 0% -> 26%
where the time goes in v2:
time: 446 us; the launch traced here: 439 us
  waiting for transfers between devices  225 us (50%)
  Pallas kernels  150 us (34%)
  starting transfers between devices  35.7 us (8%)
  local copies, waits for them, and re-layouts  14.2 us (3%)
  other arithmetic  13.1 us (3%)
    ppermute x22, waiting for transfers between devices, exchange(): return lax.ppermute(value, axis, pairs)  225 us
    pallas_call x7, Pallas kernels, products(): pl.pallas_call(functools.partial(products_body, sizes, scale_coef, raw),...  144 us
    ppermute x22, starting transfers between devices, exchange(): return lax.ppermute(value, axis, pairs)  35.7 us
  transfers between devices with their start and end apart: 22, of which 7 were waited for; matrix products, arithmetic and copies ran while one was open for 5% of the time, Pallas kernels for 26%

profile of v2, /device:TPU:31, one launch (start us, length us, event | category | flops | bytes accessed | tf_op | source)
XLA Modules:
  0.0 438.7 jit_solution(13698454327986437480)
XLA Ops:
  1.5 5.8 %shard_map.28.refs_0_.refs_4_.refs_8_.refs_12_.refs_13_.refs_14_ = bf16[256,8320]{1,0:T(8,128)(2,1)} custom-call(bf16[256,2,16,256]{3,2,1,0:T(8,128)(2,1)} %bitcast.23, s32[256,1]{1,0:T(8,128)} %copy.6.flags_ref), custom_call_target="tpu_custom_call" | custom-call | tf_op jit(solution)/shard_map/pallas_call | solution.py:64
  7.7 2.6 collective-permute-start.7
  12.1 88.4 %collective-permute-done.5.refs_18_.refs_19_.refs_20_ = bf16[256,8320]{1,0:T(8,128)(2,1)S(1)} collective-permute-done((bf16[256,8320]{1,0:T(8,128)(2,1)}, bf16[256,8320]{1,0:T(8,128)(2,1)S(1)}, u32[]{:S(2)}, u32[]{:S(2)}) %collective-permute-start.5) | collective-permute-done | bytes 4259872 | tf_op jit(solution)/shard_map/ppermute | solution.py:25
  100.4 2.1 copy-done.1
  102.5 4.1 collective-permute-start.6
  106.9 2.7 collective-permute-start.4
  109.7 2.0 collective-permute-start.2
  111.6 2.6 collective-permute-start.10
  114.3 80.2 %collective-permute-done.6.refs_12_.refs_13_.refs_14_ = bf16[256,8320]{1,0:T(8,128)(2,1)} collective-permute-done((bf16[256,8320]{1,0:T(8,128)(2,1)S(1)}, bf16[256,8320]{1,0:T(8,128)(2,1)}, u32[]{:S(2)}, u32[]{:S(2)}) %collective-permute-start.6) | collective-permute-done | bytes 4259872 | tf_op jit(solution)/shard_map/ppermute | solution.py:25
  194.5 2.3 collective-permute-start.13
  196.8 2.0 collective-permute-done.12.refs_1_.refs_5_.refs_9_
  198.8 2.6 collective-permute-start.14
  205.9 2.1 collective-permute-start.11
  208.1 49.6 %shard_map.29.refs_18_ = f32[2,4,256,2048]{3,2,1,0:T(8,128)} custom-call(s32[12]{0:T(128)} %stack.129.plan_ref, bf16[256,8320]{1,0:T(8,128)(2,1)} %shard_map.28.refs_0_.refs_4_.refs_8_.refs_12_.refs_13_.refs_14_, bf16[256,8320]{1,0:T(8,128)(2,1)} %collective-permute-done.refs_1_.refs_5_.refs_9_, ...), custom_call_target="tpu_custom_call" | custom-call | flops 34359738368 | bytes 83886080 | tf_op jit(solution)/shard_map/pallas_call | solution.py:215
  257.7 3.1 slice.6
  260.7 3.1 slice.7
  264.6 2.0 collective-permute-start.8
  266.6 8.5 %shard_map.30 = (f32[2,4,256,256]{3,2,1,0:T(8,128)}, f32[8,256]{1,0:T(8,128)}) custom-call(s32[6]{0:T(128)} %stack.133.plan_ref, bf16[256,8320]{1,0:T(8,128)(2,1)} %collective-permute-done.3.refs_15_.refs_16_.refs_17_.refs_0_.refs_4_.refs_8_, bf16[256,8320]{1,0:T(8,128)(2,1)} %collective-permute-done.12.refs_1_.refs_5_.refs_9_, ...), custom_call_target="tpu_custom_call" | custom-call | flops 8589934592 | bytes 20971520 | tf_op jit(solution)/shard_map/pallas_call | solution.py:215
  276.6 2.7 convert_element_type.18
  279.4 8.5 %shard_map.31 = (f32[2,4,256,256]{3,2,1,0:T(8,128)}, f32[8,256]{1,0:T(8,128)}) custom-call(s32[6]{0:T(128)} %stack.133.plan_ref, bf16[256,8320]{1,0:T(8,128)(2,1)} %collective-permute-done.3.refs_15_.refs_16_.refs_17_.refs_0_.refs_4_.refs_8_, bf16[256,8320]{1,0:T(8,128)(2,1)} %collective-permute-done.12.refs_1_.refs_5_.refs_9_, ...), custom_call_target="tpu_custom_call" | custom-call | flops 8589934592 | bytes 20971520 | tf_op jit(solution)/shard_map/pallas_call | solution.py:215
  287.9 13.8 %collective-permute-done.11.refs_15_.refs_16_.refs_17_ = bf16[256,8320]{1,0:T(8,128)(2,1)} collective-permute-done((bf16[256,8320]{1,0:T(8,128)(2,1)}, bf16[256,8320]{1,0:T(8,128)(2,1)}, u32[]{:S(2)}, u32[]{:S(2)}) %collective-permute-start.11) | collective-permute-done | bytes 4259872 | tf_op jit(solution)/shard_map/ppermute | solution.py:25
  303.0 16.9 %shard_map.32.refs_21_ = f32[2,4,256,2048]{3,2,1,0:T(8,128)} custom-call(s32[6]{0:T(128)} %stack.132.plan_ref, bf16[256,8320]{1,0:T(8,128)(2,1)} %shard_map.28.refs_0_.refs_4_.refs_8_.refs_12_.refs_13_.refs_14_, bf16[256,8320]{1,0:T(8,128)(2,1)} %collective-permute-done.refs_1_.refs_5_.refs_9_, ...), custom_call_target="tpu_custom_call", output_to_operand_aliasing={{}: (19, {})} | custom-call | flops 8589934592 | bytes 20971520 | tf_op jit(solution)/shard_map/pallas_call | solution.py:215
  319.8 2.7 convert_element_type.20
  324.0 8.5 %shard_map.33 = (f32[2,4,256,256]{3,2,1,0:T(8,128)}, f32[8,256]{1,0:T(8,128)}) custom-call(s32[6]{0:T(128)} %stack.133.plan_ref, bf16[256,8320]{1,0:T(8,128)(2,1)} %collective-permute-done.3.refs_15_.refs_16_.refs_17_.refs_0_.refs_4_.refs_8_, bf16[256,8320]{1,0:T(8,128)(2,1)} %collective-permute-done.12.refs_1_.refs_5_.refs_9_, ...), custom_call_target="tpu_custom_call" | custom-call | flops 8589934592 | bytes 20971520 | tf_op jit(solution)/shard_map/pallas_call | solution.py:215
  332.5 1.8 convert_element_type.22
  336.8 4.2 collective-permute-done.15
  342.6 23.2 %shard_map.34.refs_24_ = f32[2,4,256,2048]{3,2,1,0:T(8,128)} custom-call(s32[8]{0:T(128)} %stack.137.plan_ref, bf16[256,8320]{1,0:T(8,128)(2,1)} %shard_map.28.refs_0_.refs_4_.refs_8_.refs_12_.refs_13_.refs_14_, bf16[256,8320]{1,0:T(8,128)(2,1)} %collective-permute-done.refs_1_.refs_5_.refs_9_, ...), custom_call_target="tpu_custom_call", output_to_operand_aliasing={{}: (22, {})} | custom-call | flops 17179869184 | bytes 41943040 | tf_op jit(solution)/shard_map/pallas_call | solution.py:215
  365.8 1.5 convert_element_type.19.refs_18_
  367.4 15.7 %collective-permute-done.17 = f16[2,4,256,256]{3,2,1,0:T(8,128)(2,1)S(1)} collective-permute-done((f16[2,4,256,256]{3,2,1,0:T(8,128)(2,1)}, f16[2,4,256,256]{3,2,1,0:T(8,128)(2,1)S(1)}, u32[]{:S(2)}, u32[]{:S(2)}) %collective-permute-start.17) | collective-permute-done | bytes 1048608 | tf_op jit(solution)/shard_map/ppermute | solution.py:25
  384.6 21.1 %collective-permute-done.19 = f16[2,4,256,256]{3,2,1,0:T(8,128)(2,1)} collective-permute-done((f16[2,4,256,256]{3,2,1,0:T(8,128)(2,1)S(1)}, f16[2,4,256,256]{3,2,1,0:T(8,128)(2,1)}, u32[]{:S(2)}, u32[]{:S(2)}) %collective-permute-start.19) | collective-permute-done | bytes 1048608 | tf_op jit(solution)/shard_map/ppermute | solution.py:25
  405.6 2.8 convert_element_type.23.refs_22_
  409.6 28.9 %shard_map.35 = f32[2,4,256,2048]{3,2,1,0:T(8,128)} custom-call(s32[12]{0:T(128)} %stack.123.plan_ref, bf16[256,8320]{1,0:T(8,128)(2,1)} %shard_map.28.refs_0_.refs_4_.refs_8_.refs_12_.refs_13_.refs_14_, bf16[256,8320]{1,0:T(8,128)(2,1)} %collective-permute-done.refs_1_.refs_5_.refs_9_, ...), custom_call_target="tpu_custom_call", output_to_operand_aliasing={{}: (25, {})} | custom-call | flops 34359738368 | bytes 83886080 | tf_op jit(solution)/shard_map/pallas_call | solution.py:215
  (46 shorter events, 20.1 us)
Async XLA Ops:
  7.3 93.2 %collective-permute-start.5 = (bf16[256,8320]{1,0:T(8,128)(2,1)}, bf16[256,8320]{1,0:T(8,128)(2,1)S(1)}, u32[]{:S(2)}, u32[]{:S(2)}) collective-permute-start(bf16[256,8320]{1,0:T(8,128)(2,1)} %shard_map.28.refs_0_.refs_4_.refs_8_.refs_12_.refs_13_.refs_14_), channel_id=1, source_target_pairs={{0,4},{4,0},{8,12},{12,8},{16,20},{20,16},{24,28},{28,24},{1,5},{5... | collective-permute-start | bytes 12779528 | tf_op jit(solution)/shard_map/ppermute | solution.py:25
  7.5 99.2 %collective-permute-start.3 = (bf16[256,8320]{1,0:T(8,128)(2,1)}, bf16[256,8320]{1,0:T(8,128)(2,1)}, u32[]{:S(2)}, u32[]{:S(2)}) collective-permute-start(bf16[256,8320]{1,0:T(8,128)(2,1)} %shard_map.28.refs_0_.refs_4_.refs_8_.refs_12_.refs_13_.refs_14_), channel_id=1, source_target_pairs={{0,8},{4,12},{8,0},{12,4},{16,24},{20,28},{24,16},{28,20},{1,9},{5... | collective-permute-start | bytes 12779528 | tf_op jit(solution)/shard_map/ppermute | solution.py:25
  7.7 99.2 %collective-permute-start.7 = (bf16[256,8320]{1,0:T(8,128)(2,1)}, bf16[256,8320]{1,0:T(8,128)(2,1)}, u32[]{:S(2)}, u32[]{:S(2)}) collective-permute-start(bf16[256,8320]{1,0:T(8,128)(2,1)} %shard_map.28.refs_0_.refs_4_.refs_8_.refs_12_.refs_13_.refs_14_), channel_id=1, source_target_pairs={{8,16},{12,20},{16,8},{20,12},{9,17},{13,21},{17,9},{21,13},{10,18... | collective-permute-start | bytes 12779528 | tf_op jit(solution)/shard_map/ppermute | solution.py:25
  10.3 99.4 %collective-permute-start = (bf16[256,8320]{1,0:T(8,128)(2,1)}, bf16[256,8320]{1,0:T(8,128)(2,1)}, u32[]{:S(2)}, u32[]{:S(2)}) collective-permute-start(bf16[256,8320]{1,0:T(8,128)(2,1)} %shard_map.28.refs_0_.refs_4_.refs_8_.refs_12_.refs_13_.refs_14_), channel_id=1, source_target_pairs={{0,2},{1,3},{2,0},{3,1},{4,6},{5,7},{6,4},{7,5},{8,10},{9,11},{10,... | collective-permute-start | bytes 12779528 | tf_op jit(solution)/shard_map/ppermute | solution.py:25
  10.6 101.1 %collective-permute-start.1 = (bf16[256,8320]{1,0:T(8,128)(2,1)}, bf16[256,8320]{1,0:T(8,128)(2,1)}, u32[]{:S(2)}, u32[]{:S(2)}) collective-permute-start(bf16[256,8320]{1,0:T(8,128)(2,1)} %shard_map.28.refs_0_.refs_4_.refs_8_.refs_12_.refs_13_.refs_14_), channel_id=1, source_target_pairs={{0,1},{1,0},{2,3},{3,2},{4,5},{5,4},{6,7},{7,6},{8,9},{9,8},{10,11... | collective-permute-start | bytes 12779528 | tf_op jit(solution)/shard_map/ppermute | solution.py:25
  100.4 2.1 copy-start.1
  102.5 92.0 %collective-permute-start.6 = (bf16[256,8320]{1,0:T(8,128)(2,1)S(1)}, bf16[256,8320]{1,0:T(8,128)(2,1)}, u32[]{:S(2)}, u32[]{:S(2)}) collective-permute-start(bf16[256,8320]{1,0:T(8,128)(2,1)S(1)} %collective-permute-done.5.refs_18_.refs_19_.refs_20_), channel_id=1, source_target_pairs={{0,8},{4,12},{24,16},{28,20},{1,9},{5,13},{25,17},{29,21},{2,10},{... | collective-permute-start | bytes 12779528 | tf_op jit(solution)/shard_map/ppermute | solution.py:25
  106.7 92.1 %collective-permute-start.12 = (bf16[256,8320]{1,0:T(8,128)(2,1)}, bf16[256,8320]{1,0:T(8,128)(2,1)}, u32[]{:S(2)}, u32[]{:S(2)}) collective-permute-start(bf16[256,8320]{1,0:T(8,128)(2,1)} %collective-permute-done.3.refs_15_.refs_16_.refs_17_.refs_0_.refs_4_.refs_8_), channel_id=1, source_target_pairs={{0,2},{1,3},{2,0},{3,1},{4,6},{5,7},{6,4},{7,5},{8,10},{9,11},{10,... | collective-permute-start | bytes 12779528 | tf_op jit(solution)/shard_map/ppermute | solution.py:25
  106.9 97.7 %collective-permute-start.4 = (bf16[256,8320]{1,0:T(8,128)(2,1)}, bf16[256,8320]{1,0:T(8,128)(2,1)}, u32[]{:S(2)}, u32[]{:S(2)}) collective-permute-start(bf16[256,8320]{1,0:T(8,128)(2,1)} %collective-permute-done.3.refs_15_.refs_16_.refs_17_.refs_0_.refs_4_.refs_8_), channel_id=1, source_target_pairs={{8,16},{12,20},{16,8},{20,12},{9,17},{13,21},{17,9},{21,13},{10,18... | collective-permute-start | bytes 12779528 | tf_op jit(solution)/shard_map/ppermute | solution.py:25
  109.7 96.3 %collective-permute-start.2 = (bf16[256,8320]{1,0:T(8,128)(2,1)}, bf16[256,8320]{1,0:T(8,128)(2,1)}, u32[]{:S(2)}, u32[]{:S(2)}) collective-permute-start(bf16[256,8320]{1,0:T(8,128)(2,1)} %collective-permute-done.refs_1_.refs_5_.refs_9_), channel_id=1, source_target_pairs={{0,1},{1,0},{2,3},{3,2},{4,5},{5,4},{6,7},{7,6},{8,9},{9,8},{10,11... | collective-permute-start | bytes 12779528 | tf_op jit(solution)/shard_map/ppermute | solution.py:25
  111.6 152.2 %collective-permute-start.10 = (bf16[256,8320]{1,0:T(8,128)(2,1)}, bf16[256,8320]{1,0:T(8,128)(2,1)}, u32[]{:S(2)}, u32[]{:S(2)}) collective-permute-start(bf16[256,8320]{1,0:T(8,128)(2,1)} %collective-permute-done.7.refs_21_.refs_22_.refs_23_), channel_id=1, source_target_pairs={{8,12},{12,8},{16,20},{20,16},{9,13},{13,9},{17,21},{21,17},{10,14... | collective-permute-start | bytes 12779528 | tf_op jit(solution)/shard_map/ppermute | solution.py:25
  194.5 70.1 %collective-permute-start.13 = (bf16[256,8320]{1,0:T(8,128)(2,1)}, bf16[256,8320]{1,0:T(8,128)(2,1)}, u32[]{:S(2)}, u32[]{:S(2)}) collective-permute-start(bf16[256,8320]{1,0:T(8,128)(2,1)} %collective-permute-done.3.refs_15_.refs_16_.refs_17_.refs_0_.refs_4_.refs_8_), channel_id=1, source_target_pairs={{0,1},{1,0},{2,3},{3,2},{4,5},{5,4},{6,7},{7,6},{8,9},{9,8},{10,11... | collective-permute-start | bytes 12779528 | tf_op jit(solution)/shard_map/ppermute | solution.py:25
  198.8 67.8 %collective-permute-start.14 = (bf16[256,8320]{1,0:T(8,128)(2,1)}, bf16[256,8320]{1,0:T(8,128)(2,1)}, u32[]{:S(2)}, u32[]{:S(2)}) collective-permute-start(bf16[256,8320]{1,0:T(8,128)(2,1)} %collective-permute-done.12.refs_1_.refs_5_.refs_9_), channel_id=1, source_target_pairs={{0,1},{1,0},{2,3},{3,2},{4,5},{5,4},{6,7},{7,6},{8,9},{9,8},{10,11... | collective-permute-start | bytes 12779528 | tf_op jit(solution)/shard_map/ppermute | solution.py:25
  204.6 130.9 %collective-permute-start.21 = (bf16[256,8320]{1,0:T(8,128)(2,1)}, bf16[256,8320]{1,0:T(8,128)(2,1)}, u32[]{:S(2)}, u32[]{:S(2)}) collective-permute-start(bf16[256,8320]{1,0:T(8,128)(2,1)} %collective-permute-done.7.refs_21_.refs_22_.refs_23_), channel_id=1, source_target_pairs={{8,0},{12,4},{16,24},{20,28},{9,1},{13,5},{17,25},{21,29},{10,2},{... | collective-permute-start | bytes 12779528 | tf_op jit(solution)/shard_map/ppermute | solution.py:25
  205.9 95.7 %collective-permute-start.11 = (bf16[256,8320]{1,0:T(8,128)(2,1)}, bf16[256,8320]{1,0:T(8,128)(2,1)}, u32[]{:S(2)}, u32[]{:S(2)}) collective-permute-start(bf16[256,8320]{1,0:T(8,128)(2,1)} %collective-permute-done.3.refs_15_.refs_16_.refs_17_.refs_0_.refs_4_.refs_8_), channel_id=1, source_target_pairs={{0,4},{4,0},{24,28},{28,24},{1,5},{5,1},{25,29},{29,25},{2,6},{6,2... | collective-permute-start | bytes 12779528 | tf_op jit(solution)/shard_map/ppermute | solution.py:25
  263.8 58.7 %collective-permute-start.9 = (bf16[128,8320]{1,0:T(8,128)(2,1)}, bf16[128,8320]{1,0:T(8,128)(2,1)S(1)}, u32[]{:S(2)}, u32[]{:S(2)}) collective-permute-start(bf16[128,8320]{1,0:T(8,128)(2,1)} %slice.7), channel_id=1, source_target_pairs={{8,16},{12,20},{16,8},{20,12},{9,17},{13,21},{17,9},{21,13},{10,18... | collective-permute-start | bytes 6389768 | tf_op jit(solution)/shard_map/ppermute | solution.py:25
  264.6 59.3 %collective-permute-start.8 = (bf16[128,8320]{1,0:T(8,128)(2,1)}, bf16[128,8320]{1,0:T(8,128)(2,1)}, u32[]{:S(2)}, u32[]{:S(2)}) collective-permute-start(bf16[128,8320]{1,0:T(8,128)(2,1)} %slice.6), channel_id=1, source_target_pairs={{8,12},{12,8},{16,20},{20,16},{9,13},{13,9},{17,21},{21,17},{10,14... | collective-permute-start | bytes 6389768 | tf_op jit(solution)/shard_map/ppermute | solution.py:25
  275.1 133.2 %collective-permute-start.16 = (f32[8,256]{1,0:T(8,128)}, f32[8,256]{1,0:T(8,128)S(1)}, u32[]{:S(2)}, u32[]{:S(2)}) collective-permute-start(f32[8,256]{1,0:T(8,128)} %get-tuple-element.23), channel_id=1, source_target_pairs={{8,0},{12,4},{16,24},{20,28},{9,1},{13,5},{17,25},{21,29},{10,2},{... | collective-permute-start | bytes 24584 | tf_op jit(solution)/shard_map/ppermute | solution.py:25
  287.9 34.7 %copy-start.3 = (f32[8,256]{1,0:T(8,128)S(1)}, f32[8,256]{1,0:T(8,128)}, u32[]{:S(2)}) copy-start(f32[8,256]{1,0:T(8,128)} %get-tuple-element.25) | copy-start | bytes 24580
  301.7 39.4 %collective-permute-start.15 = (f16[2,4,256,256]{3,2,1,0:T(8,128)(2,1)}, f16[2,4,256,256]{3,2,1,0:T(8,128)(2,1)S(1)}, u32[]{:S(2)}, u32[]{:S(2)}) collective-permute-start(f16[2,4,256,256]{3,2,1,0:T(8,128)(2,1)} %convert_element_type.18), channel_id=1, source_target_pairs={{8,0},{12,4},{16,24},{20,28},{9,1},{13,5},{17,25},{21,29},{10,2},{... | collective-permute-start | bytes 3145736 | tf_op jit(solution)/shard_map/ppermute | solution.py:25
  322.6 1.4 copy-start
  322.6 85.8 %collective-permute-start.18 = (f32[8,256]{1,0:T(8,128)S(1)}, f32[8,256]{1,0:T(8,128)S(1)}, u32[]{:S(2)}, u32[]{:S(2)}) collective-permute-start(f32[8,256]{1,0:T(8,128)S(1)} %copy-done.3), channel_id=1, source_target_pairs={{8,0},{12,4},{16,24},{20,28},{9,1},{13,5},{17,25},{21,29},{10,2},{... | collective-permute-start | bytes 24584 | tf_op jit(solution)/shard_map/ppermute | solution.py:25
  334.2 74.2 %collective-permute-start.20 = (f32[8,256]{1,0:T(8,128)}, f32[8,256]{1,0:T(8,128)S(1)}, u32[]{:S(2)}, u32[]{:S(2)}) collective-permute-start(f32[8,256]{1,0:T(8,128)} %get-tuple-element.32), channel_id=1, source_target_pairs={{8,0},{12,4},{16,24},{20,28},{9,1},{13,5},{17,25},{21,29},{10,2},{... | collective-permute-start | bytes 24584 | tf_op jit(solution)/shard_map/ppermute | solution.py:25
  335.5 47.5 %collective-permute-start.17 = (f16[2,4,256,256]{3,2,1,0:T(8,128)(2,1)}, f16[2,4,256,256]{3,2,1,0:T(8,128)(2,1)S(1)}, u32[]{:S(2)}, u32[]{:S(2)}) collective-permute-start(f16[2,4,256,256]{3,2,1,0:T(8,128)(2,1)} %convert_element_type.20), channel_id=1, source_target_pairs={{8,0},{12,4},{16,24},{20,28},{9,1},{13,5},{17,25},{21,29},{10,2},{... | collective-permute-start | bytes 3145736 | tf_op jit(solution)/shard_map/ppermute | solution.py:25
  341.1 64.5 %collective-permute-start.19 = (f16[2,4,256,256]{3,2,1,0:T(8,128)(2,1)S(1)}, f16[2,4,256,256]{3,2,1,0:T(8,128)(2,1)}, u32[]{:S(2)}, u32[]{:S(2)}) collective-permute-start(f16[2,4,256,256]{3,2,1,0:T(8,128)(2,1)S(1)} %convert_element_type.22), channel_id=1, source_target_pairs={{8,0},{12,4},{16,24},{20,28},{9,1},{13,5},{17,25},{21,29},{10,2},{... | collective-permute-start | bytes 3145736 | tf_op jit(solution)/shard_map/ppermute | solution.py:25
  408.4 0.6 copy-start.2
  408.4 0.6 copy-start.4
  409.0 0.6 copy-start.5

commit v3 on v0

v3 whole, which is shorter than its diff:
```python
import functools
import math

import jax
import jax.numpy as jnp
from jax import lax
from jax.experimental import pallas as pl
from jax.experimental.pallas import tpu as pltpu
from jax.sharding import PartitionSpec as P


NT = (((1,), (1,)), ((), ()))
LANES = 128
FLOOR = 1e-30


def tile_of(size, most):
    tile = 1
    while tile * 2 <= most and size % (tile * 2) == 0:
        tile *= 2
    return tile


def tied(*values):
    return lax.optimization_barrier(values)


def split_in_three(value):
    parts = []
    for _ in range(2):
        part = value.astype(jnp.bfloat16).astype(jnp.float32)
        parts.append(part)
        value = value - part
    return parts + [value]


def laid_out_body(pieces, spectra_ref, flags_ref, *out_refs):
    high, parts, bins, taps = spectra_ref.shape
    per_piece = pl.num_programs(0) // pieces
    half_width = bins * taps

    def fill(out_ref):
        power = jnp.zeros((high, 1), jnp.float32)
        for part in range(parts):
            flat = spectra_ref[:, part].reshape(high, half_width)
            out_ref[:, part * half_width : (part + 1) * half_width] = flat
            widened = flat.astype(jnp.float32)
            power = power + jnp.sum(widened * widened, axis=1, keepdims=True)
        power_mean = power / (parts * half_width)
        factor = flags_ref[...].astype(jnp.float32) * lax.rsqrt(power_mean + 1e-06)
        norm = lax.rsqrt(jnp.maximum(power_mean, FLOOR))
        lane = lax.broadcasted_iota(jnp.int32, (high, LANES), 1)
        marks = jnp.zeros((high, LANES), jnp.float32)
        for index, value in enumerate(split_in_three(factor) + split_in_three(norm)):
            marks = jnp.where(lane == index, value, marks)
        out_ref[:, parts * half_width :] = marks.astype(jnp.bfloat16)

    for piece, out_ref in enumerate(out_refs):
        pl.when(pl.program_id(0) // per_piece == piece)(functools.partial(fill, out_ref))


def laid_out(spectra, flags, pieces):
    rows, parts, bins, taps = spectra.shape
    width = parts * bins * taps + LANES
    high = tile_of(rows // pieces, 64)
    per_piece = rows // pieces // high

    def place(piece):
        first = piece * per_piece
        return lambda i: (jnp.clip(i - first, 0, per_piece - 1), 0)

    return pl.pallas_call(
        functools.partial(laid_out_body, pieces),
        grid=(rows // high,),
        in_specs=[
            pl.BlockSpec((high, parts, bins, taps), lambda i: (i, 0, 0, 0)),
            pl.BlockSpec((high, 1), lambda i: (i, 0)),
        ],
        out_specs=[pl.BlockSpec((high, width), place(piece)) for piece in range(pieces)],
        out_shape=[jax.ShapeDtypeStruct((rows // pieces, width), spectra.dtype)] * pieces,
    )(spectra, flags.reshape(rows, 1))


def products_body(sizes, scale_coef, raw, plan_ref, *refs):
    row_total, at_once, shapes, units = sizes
    refs = list(refs)
    rows = refs[:row_total]
    columns, at = [], row_total
    for shape in shapes:
        columns.append(refs[at : at + len(shape)])
        at += len(shape)
    held, right, col_marks, row_sems, col_sems = refs[-5:]
    outs = refs[-7:-5] if raw else refs[-6:-5]
    out_ref = outs[0]
    unit, part = pl.program_id(0), pl.program_id(1)
    parts = row_total // at_once
    now = unit * parts + part
    shard_rows = held.shape[1] // at_once
    cols = right.shape[1] // 2
    half_width = right.shape[2] // 2

    def row_copy(index, row, slot):
        where = held.at[slot, pl.ds(row * shard_rows, shard_rows)]
        return pltpu.make_async_copy(rows[index], where, row_sems.at[slot, row])

    def start_rows(which, slot):
        for index in range(parts):

            @pl.when(which == index)
            def _():
                for row in range(at_once):
                    row_copy(index * at_once + row, row, slot).start()

    def col_copies(index, slot):
        copies, top = [], 0
        for number, piece in enumerate(columns[index]):
            high = piece.shape[0]
            real, imag = piece.at[:, pl.ds(0, half_width)], piece.at[:, pl.ds(half_width, half_width)]
            marks = piece.at[:, pl.ds(2 * half_width, LANES)]
            places = [
                (real, right.at[slot, pl.ds(top, high), pl.ds(0, half_width)]),
                (imag, right.at[slot, pl.ds(top, high), pl.ds(half_width, half_width)]),
                (real, right.at[slot, pl.ds(cols + top, high), pl.ds(half_width, half_width)]),
                (marks, col_marks.at[slot, pl.ds(top, high)]),
            ]
            for kind, (source, target) in enumerate(places):
                copies.append(
                    pltpu.make_async_copy(source, target, col_sems.at[slot, 4 * number + kind])
                )
            top += high
        return copies

    def for_cols(which, slot, wait):
        for index in range(len(columns)):

            @pl.when(plan_ref[which] == index)
            def _():
                for copy in col_copies(index, slot):
                    copy.wait() if wait else copy.start()

    slot, col_slot = lax.rem(now, 2), lax.rem(unit, 2)

    @pl.when(now == 0)
    def _():
        start_rows(0, 0)
        for_cols(0, 0, False)

    @pl.when(now + 1 < units * parts)
    def _():
        start_rows(lax.rem(part + 1, parts), lax.rem(now + 1, 2))

    @pl.when(jnp.logical_and(part == 0, unit + 1 < units))
    def _():
        for_cols(unit + 1, lax.rem(unit + 1, 2), False)

    @pl.when(part == 0)
    def _():
        for_cols(unit, col_slot, True)
        right[col_slot, cols:, :half_width] = -right[col_slot, :cols, half_width:]

    for row in range(at_once):
        row_copy(row, row, slot).wait()

    left = held[slot, :, : 2 * half_width]
    product = lax.dot_general(left, right[col_slot], NT, preferred_element_type=jnp.float32)

    def sums(values, axis):
        def one(first):
            take = [lax.slice_in_dim(values, i, i + 1, axis=axis) for i in range(first, first + 3)]
            return (take[2] + take[1]) + take[0]

        return one(0), one(3)

    col_factor, col_norm = sums(col_marks[col_slot].astype(jnp.float32).T, 0)
    for row in range(at_once):
        top = row * shard_rows
        marks = held[slot, pl.ds(top, shard_rows), pl.ds(2 * half_width, LANES)]
        row_factor, row_norm = sums(marks.astype(jnp.float32), 1)
        place = plan_ref[2 * units + parts + part * at_once + row]
        scaling = (row_factor * scale_coef) * col_factor
        if raw:
            bound = jnp.max(row_factor / row_norm, axis=0, keepdims=True)
            bound = bound * jnp.max(col_factor / col_norm, axis=1, keepdims=True)
            unit_size = jnp.maximum(bound * (2 * half_width * scale_coef), FLOOR) / 32768
            outs[1][place] = jnp.broadcast_to(unit_size, outs[1].shape[1:])
            scaling = scaling * (1 / unit_size)
        out_ref[0, place] = product[top : top + shard_rows, :cols] * scaling
        out_ref[1, place] = product[top : top + shard_rows, cols:] * scaling


def products(out, rows, columns, choice, slots, mine, blocks, scale_coef, raw=False):
    shard_rows, width = rows[0].shape
    half_width = (width - LANES) // 2
    units, count = len(choice), len(rows)
    at_once = 2 if units > 1 and count > 1 else 1
    parts = count // at_once
    cols = sum(piece.shape[0] for piece in columns[0])
    whole = pl.BlockSpec(memory_space=pl.ANY)
    operands = list(rows) + [piece for pieces in columns for piece in pieces]
    aliases = {}
    if out is not None:
        aliases = {1 + len(operands): 0}
        operands.append(out)
    groups = [mine ^ j for j in range(count)]
    plan = jnp.stack(
        list(choice)
        + list(slots)
        + [group // at_once for group in groups[::at_once]]
        + [group % at_once for group in groups]
    ).astype(jnp.int32)
    shape = (2, count, shard_rows, cols if raw else shard_rows * blocks)
    out_shape = [jax.ShapeDtypeStruct(shape, jnp.float32)]
    out_specs = [
        pl.BlockSpec(
            (2, at_once, shard_rows, cols),
            lambda i, j, s: (0, s[2 * units + j], 0, s[units + i]),
        )
    ]
    if raw:
        out_shape.append(jax.ShapeDtypeStruct((count, 8, LANES), jnp.float32))
        out_specs.append(
            pl.BlockSpec((at_once, 8, LANES), lambda i, j, s: (s[2 * units + j], 0, 0))
        )
    shapes = [[piece.shape[0] for piece in pieces] for pieces in columns]
    most = max(len(pieces) for pieces in columns)
    given = pl.pallas_call(
        functools.partial(products_body, (count, at_once, shapes, units), scale_coef, raw),
        grid_spec=pltpu.PrefetchScalarGridSpec(
            num_scalar_prefetch=1,
            grid=(units, parts),
            in_specs=[whole] * len(operands),
            out_specs=out_specs,
            scratch_shapes=[
                pltpu.VMEM((2, at_once * shard_rows, width), rows[0].dtype),
                pltpu.VMEM((2, 2 * cols, 2 * half_width), rows[0].dtype),
                pltpu.VMEM((2, cols, LANES), rows[0].dtype),
                pltpu.SemaphoreType.DMA((2, at_once)),
                pltpu.SemaphoreType.DMA((2, 4 * most)),
            ],
        ),
        out_shape=out_shape,
        input_output_aliases=aliases,
        cost_estimate=pl.CostEstimate(
            flops=8 * units * count * shard_rows * cols * half_width,
            bytes_accessed=4 * units * half_width * (count * shard_rows + cols),
            transcendentals=0,
        ),
        compiler_params=pltpu.CompilerParams(
            dimension_semantics=("arbitrary", "arbitrary"), vmem_limit_bytes=60 * 2**20
        ),
    )(plan, *operands)
    return given if raw else given[0]


def gathered(spectra, detector_valid, scale_coef):
    shard_rows = spectra.shape[1]
    half_width = spectra.shape[3] * spectra.shape[4]
    flattened = spectra.reshape(shard_rows, 2 * half_width)
    widened = flattened.astype(jnp.float32)
    power_mean = jnp.mean(widened * widened, axis=1) + 1e-06
    own_factor = detector_valid.reshape(shard_rows).astype(jnp.float32) * lax.rsqrt(power_mean)
    rows = lax.all_gather(flattened, "grp", axis=0, tiled=True)
    cols = lax.all_gather(flattened, "blk", axis=0, tiled=True)
    row_factor = lax.all_gather(own_factor, "grp", axis=0, tiled=True) * scale_coef
    col_factor = lax.all_gather(own_factor, "blk", axis=0, tiled=True)
    rotated = jnp.concatenate([-cols[:, half_width:], cols[:, :half_width]], axis=1)
    scaling = row_factor[:, None] * col_factor[None, :]
    parts = [
        lax.dot_general(rows, right, NT, preferred_element_type=jnp.float32) * scaling
        for right in (cols, rotated)
    ]
    return jnp.stack(parts)


def shards(spectra, detector_valid):
    shard_rows = spectra.shape[1]
    half_width = spectra.shape[3] * spectra.shape[4]
    blocks = lax.axis_size("blk")
    group_size = lax.axis_size("grp")
    scale_coef = 0.5 / math.sqrt(half_width)
    shape = (2, group_size, shard_rows, blocks * shard_rows)
    fits = shard_rows % 256 == 0 and half_width % 256 == 0 and group_size & (group_size - 1) == 0
    if blocks != 8 or not fits:
        return gathered(spectra, detector_valid, scale_coef).reshape(shape)

    devices = range(blocks)
    inner = [b for b in devices if 0 < b // 2 < blocks // 2 - 1]
    ends = [b for b in devices if b not in inner]
    me = lax.axis_index("blk")
    mine = lax.axis_index("grp")
    is_end = jnp.logical_or(me // 2 == 0, me // 2 == blocks // 2 - 1)

    def moved(value, axis, route):
        if isinstance(value, tuple):
            return tuple(moved(piece, axis, route) for piece in value)
        return lax.ppermute(value, axis, route)

    def swap(value, among, by):
        return moved(value, "blk", [(b, b ^ by) for b in among])

    def spread(value, by):
        return moved(value, "grp", [(g, g ^ by) for g in range(group_size)])

    def over_groups(value):
        arrays, by = {0: value}, group_size // 2
        while by:
            arrays.update({key ^ by: spread(array, by) for key, array in arrays.items()})
            by //= 2
        return [arrays[key] for key in range(group_size)]

    def either(inner_value, end_value):
        return jnp.where(is_end, end_value, inner_value)

    def put(out, columns, units):
        choice = [either(m, e) for m, e, _, _ in units]
        slots = [either(me ^ m, me ^ e) for _, _, m, e in units]
        return products(out, rows, columns, choice, slots, mine, blocks, scale_coef)

    (own,) = laid_out(spectra[0], detector_valid[0], 1)
    near = swap(own, devices, 2)
    beside = swap(own, devices, 1)
    across = swap(own, inner, 6)
    rows = over_groups(own)

    across_beside = swap(across, inner, 1)
    near_beside = swap(near, ends, 1)
    end_beside = swap(beside, ends, 2)
    far_inner = swap(across, inner, 2)
    far_end = swap(near, inner, 6)
    client = {0: near}
    if group_size > 1:
        client[group_size // 2] = spread(near, group_size // 2)

    out = put(
        None,
        [(own,), (near,), (beside,), (across,)],
        [(0, 0, 0, 0), (1, 1, 2, 2), (2, 2, 1, 1), (3, 0, 6, 5)],
    )
    half = shard_rows // 2
    far_end, end_beside, far_inner, client[group_size // 2], out = tied(
        far_end, end_beside, far_inner, client[group_size // 2], out
    )
    low = swap(far_end[:half], inner, 1)
    high = swap(end_beside[half:], inner, 6)
    far_inner_beside = swap(far_inner, ends, 1)
    by = group_size // 4
    while by:
        client.update({key ^ by: spread(array, by) for key, array in client.items()})
        by //= 2
    client = [client[key] for key in range(group_size)]
    out = put(
        out,
        [(across_beside,), (near_beside,), (end_beside,), (far_inner,)],
        [(0, 1, 7, 3), (2, 3, 3, 4)],
    )

    def serve(columns):
        return products(
            None, client, [columns], [me * 0], [me * 0], mine, blocks, scale_coef, raw=True
        )

    def deliver(block, unit_size):
        return swap(block.astype(jnp.float16), inner, 2), swap(unit_size, inner, 2)

    def place(out, sent, end_slot):
        block, unit_size = sent
        block = block.astype(jnp.float32) * unit_size[None, :, :1, :1]
        start = either(me ^ 5, me ^ end_slot) * shard_rows
        zero = jnp.zeros_like(start)
        return lax.dynamic_update_slice(out, block, (zero, zero, zero, start))

    far_end, out = tied(far_end, out)
    first = serve((far_end,))
    sent_a = deliver(*first)
    low, high, _ = tied(low, high, first[1])
    second = serve((low, high))
    sent_b = deliver(*second)
    out, _ = tied(out, second[1])
    out = put(out, [(far_end,)], [(0, 0, 4, 6)])
    out = place(out, sent_a, 6)
    out = place(out, sent_b, 7)
    out = put(out, [(low, high), (far_inner_beside,)], [(0, 1, 5, 5)])
    return out.reshape(shape)


def solution(mesh):
    return jax.shard_map(
        shards,
        mesh=mesh,
        in_specs=(P("grp", "blk", None, None, None), P("grp", "blk")),
        out_specs=P(None, None, "blk", "grp"),
        check_vma=False,
    )
```

time: 733 us -> 412 us (0.56)
  waiting for transfers between devices: 429 us -> 203 us
  Pallas kernels: 0 us -> 146 us
  local copies, waits for them, and re-layouts: 111 us -> 11.2 us
  matrix products: 77 us -> 0 us
  other arithmetic: 50.1 us -> 8.73 us
  between operations: 14 us -> 0.36 us
  blocking collectives: 9.42 us -> 0 us
    ppermute x11 -> x21, waiting for transfers between devices: 419 us -> 203 us  [moved(): return lax.ppermute(value, axis, route)]
    pallas_call x0 -> x7, Pallas kernels: none -> 146 us  [the longest x6 140 us: products(): pl.pallas_call(functools.partial(products_body, (count, at_once, shapes,...]
    dot_general x5 -> x0, matrix products: 77 us -> none  [cross_tile(): lax.dot_general(rows_flat, stacked, (((1,), (1,)), ((), ())), preferred_e...]
    reshape x9 -> x0, local copies, waits for them, and re-layouts: 68.3 us -> none  [the longest x5 37.1 us: cross_tile(): flattened = col_spec.reshape(shard_rows, full_width)]
    reduce_sum x6 -> x0, other arithmetic: 29 us -> none  [factors(): power_mean = jnp.mean(widened * widened, axis=1) + 1e-06]
    ppermute x11 -> x21, starting transfers between devices: 18.1 us -> 37.2 us  [moved(): return lax.ppermute(value, axis, route)]
    all_to_all x3 -> x0, starting transfers between devices: 18.8 us -> none  [shards(): lax.all_to_all(flipped, 'grp', split_axis=1, concat_axis=1, tiled=True)]
    neg x5 -> x0, other arithmetic: 15.8 us -> none  [cross_tile(): -flattened[:, half_width:]]
  transfers between devices with their start and end apart: 15 -> 21, of which waited for: 11 -> 6; matrix products, arithmetic and copies ran while one was open for 31% -> 5% of each run, Pallas kernels for 0% -> 30%
where the time goes in v3:
time: 412 us; the launch traced here: 407 us
  waiting for transfers between devices  203 us (49%)
  Pallas kernels  146 us (35%)
  starting transfers between devices  37.2 us (9%)
  local copies, waits for them, and re-layouts  11.2 us (3%)
  other arithmetic  8.73 us (2%)
    ppermute x21, waiting for transfers between devices, moved(): return lax.ppermute(value, axis, route)  203 us
    pallas_call x6, Pallas kernels, products(): pl.pallas_call(functools.partial(products_body, (count, at_once, shapes,...  140 us
    ppermute x21, starting transfers between devices, moved(): return lax.ppermute(value, axis, route)  37.2 us
  transfers between devices with their start and end apart: 21, of which 6 were waited for; matrix products, arithmetic and copies ran while one was open for 5% of the time, Pallas kernels for 30%

profile of v3, /device:TPU:31, one launch (start us, length us, event | category | flops | bytes accessed | tf_op | source)
XLA Modules:
  0.0 406.7 jit_solution(15547758490378761283)
XLA Ops:
  0.0 1.5 copy.6.flags_ref
  1.5 5.8 %shard_map.28.refs_0_.refs_4_ = bf16[256,8320]{1,0:T(8,128)(2,1)} custom-call(bf16[256,2,16,256]{3,2,1,0:T(8,128)(2,1)} %bitcast.23, s32[256,1]{1,0:T(8,128)} %copy.6.flags_ref), custom_call_target="tpu_custom_call" | custom-call | tf_op jit(solution)/shard_map/pallas_call | solution.py:72
  8.9 2.8 collective-permute-start.7
  12.0 88.5 %collective-permute-done.1.refs_2_ = bf16[256,8320]{1,0:T(8,128)(2,1)} collective-permute-done((bf16[256,8320]{1,0:T(8,128)(2,1)}, bf16[256,8320]{1,0:T(8,128)(2,1)}, u32[]{:S(2)}, u32[]{:S(2)}) %collective-permute-start.1) | collective-permute-done | bytes 4259872 | tf_op jit(solution)/shard_map/ppermute | solution.py:296
  100.5 1.5 collective-permute-start.2
  102.0 2.7 collective-permute-start.4
  106.3 8.0 %collective-permute-start.6 = (bf16[256,8320]{1,0:T(8,128)(2,1)}, bf16[256,8320]{1,0:T(8,128)(2,1)}, u32[]{:S(2)}, u32[]{:S(2)}) collective-permute-start(bf16[256,8320]{1,0:T(8,128)(2,1)} %collective-permute-done.5.refs_6_), channel_id=1, source_target_pairs={{0,8},{4,12},{24,16},{28,20},{1,9},{5,13},{25,17},{29,21},{2,10},{... | collective-permute-start | bytes 12779528 | tf_op jit(solution)/shard_map/ppermute | solution.py:296
  114.9 2.1 collective-permute-start.15
  117.1 2.7 collective-permute-start.14
  119.8 48.0 %shard_map.29.refs_8_ = f32[2,4,256,2048]{3,2,1,0:T(8,128)} custom-call(s32[14]{0:T(128)} %stack.136.plan_ref, bf16[256,8320]{1,0:T(8,128)(2,1)} %shard_map.28.refs_0_.refs_4_, bf16[256,8320]{1,0:T(8,128)(2,1)} %collective-permute-done.refs_1_, bf16[256,8320]{1,0:T(8,128)(2,1)} %collective-permute-done.1.refs_2_, ...), custom_call_target="tpu_custom_call" | custom-call | flops 34359738368 | bytes 83886080 | tf_op jit(solution)/shard_map/pallas_call | solution.py:226
  167.9 30.4 %collective-permute-done.9.refs_2_ = bf16[256,8320]{1,0:T(8,128)(2,1)} collective-permute-done((bf16[256,8320]{1,0:T(8,128)(2,1)}, bf16[256,8320]{1,0:T(8,128)(2,1)}, u32[]{:S(2)}, u32[]{:S(2)}) %collective-permute-start.9) | collective-permute-done | bytes 4259872 | tf_op jit(solution)/shard_map/ppermute | solution.py:296
  199.4 2.7 collective-permute-done.6.refs_6_
  202.1 2.6 collective-permute-start.13
  207.3 3.0 slice.12
  211.1 3.1 slice.13
  214.3 2.0 collective-permute-start.11
  216.3 2.1 collective-permute-start.16
  218.4 25.7 %shard_map.30.refs_5_ = f32[2,4,256,2048]{3,2,1,0:T(8,128)} custom-call(s32[10]{0:T(128)} %stack.141.plan_ref, bf16[256,8320]{1,0:T(8,128)(2,1)} %shard_map.28.refs_0_.refs_4_, bf16[256,8320]{1,0:T(8,128)(2,1)} %collective-permute-done.refs_1_, bf16[256,8320]{1,0:T(8,128)(2,1)} %collective-permute-done.1.refs_2_, ...), custom_call_target="tpu_custom_call", output_to_operand_aliasing={{}: (9, {})} | custom-call | flops 17179869184 | bytes 41943040 | tf_op jit(solution)/shard_map/pallas_call | solution.py:226
  244.1 16.5 %shard_map.31 = (f32[2,4,256,256]{3,2,1,0:T(8,128)}, f32[4,8,128]{2,1,0:T(8,128)}) custom-call(s32[10]{0:T(128)} %stack.137.plan_ref, bf16[256,8320]{1,0:T(8,128)(2,1)} %collective-permute-done.3.refs_5_.refs_0_, bf16[256,8320]{1,0:T(8,128)(2,1)} %collective-permute-done.12.refs_1_, bf16[256,8320]{1,0:T(8,128)(2,1)} %collective-permute-done.9.refs_2_, ...), custom_call_target="tpu_custom_call" | custom-call | flops 8589934592 | bytes 20971520 | tf_op jit(solution)/shard_map/pallas_call | solution.py:226
  260.6 1.5 collective-permute-start.18
  262.1 2.5 convert_element_type.12
  264.7 1.3 collective-permute-start.17
  266.0 16.8 %shard_map.32 = (f32[2,4,256,256]{3,2,1,0:T(8,128)}, f32[4,8,128]{2,1,0:T(8,128)}) custom-call(s32[10]{0:T(128)} %stack.137.plan_ref, bf16[256,8320]{1,0:T(8,128)(2,1)} %collective-permute-done.3.refs_5_.refs_0_, bf16[256,8320]{1,0:T(8,128)(2,1)} %collective-permute-done.12.refs_1_, bf16[256,8320]{1,0:T(8,128)(2,1)} %collective-permute-done.9.refs_2_, ...), custom_call_target="tpu_custom_call" | custom-call | flops 8589934592 | bytes 20971520 | tf_op jit(solution)/shard_map/pallas_call | solution.py:226
  282.8 1.3 collective-permute-start.20
  284.1 1.8 convert_element_type.14
  287.1 16.4 %shard_map.33 = f32[2,4,256,2048]{3,2,1,0:T(8,128)} custom-call(s32[10]{0:T(128)} %stack.143.plan_ref, bf16[256,8320]{1,0:T(8,128)(2,1)} %shard_map.28.refs_0_.refs_4_, bf16[256,8320]{1,0:T(8,128)(2,1)} %collective-permute-done.refs_1_, bf16[256,8320]{1,0:T(8,128)(2,1)} %collective-permute-done.1.refs_2_, ...), custom_call_target="tpu_custom_call", output_to_operand_aliasing={{}: (6, {})} | custom-call | flops 8589934592 | bytes 20971520 | tf_op jit(solution)/shard_map/pallas_call | solution.py:226
  303.5 38.3 %collective-permute-done.18 = f32[4,8,128]{2,1,0:T(8,128)S(1)} collective-permute-done((f32[4,8,128]{2,1,0:T(8,128)}, f32[4,8,128]{2,1,0:T(8,128)S(1)}, u32[]{:S(2)}, u32[]{:S(2)}) %collective-permute-start.18) | collective-permute-done | bytes 16416 | tf_op jit(solution)/shard_map/ppermute | solution.py:296
  341.9 23.6 %collective-permute-done.20 = f32[4,8,128]{2,1,0:T(8,128)S(1)} collective-permute-done((f32[4,8,128]{2,1,0:T(8,128)}, f32[4,8,128]{2,1,0:T(8,128)S(1)}, u32[]{:S(2)}, u32[]{:S(2)}) %collective-permute-start.20) | collective-permute-done | bytes 16416 | tf_op jit(solution)/shard_map/ppermute | solution.py:296
  365.6 2.8 multiply_dynamic-update-slice_fusion.1
  368.4 19.7 %collective-permute-done.19 = f16[2,4,256,256]{3,2,1,0:T(8,128)(2,1)S(1)} collective-permute-done((f16[2,4,256,256]{3,2,1,0:T(8,128)(2,1)S(1)}, f16[2,4,256,256]{3,2,1,0:T(8,128)(2,1)S(1)}, u32[]{:S(2)}, u32[]{:S(2)}) %collective-permute-start.19) | collective-permute-done | bytes 1048608 | tf_op jit(solution)/shard_map/ppermute | solution.py:296
  388.1 1.6 multiply_dynamic-update-slice_fusion.refs_7_
  389.7 16.9 %shard_map.34 = f32[2,4,256,2048]{3,2,1,0:T(8,128)} custom-call(s32[10]{0:T(128)} %stack.58.plan_ref, bf16[256,8320]{1,0:T(8,128)(2,1)} %shard_map.28.refs_0_.refs_4_, bf16[256,8320]{1,0:T(8,128)(2,1)} %collective-permute-done.refs_1_, bf16[256,8320]{1,0:T(8,128)(2,1)} %collective-permute-done.1.refs_2_, ...), custom_call_target="tpu_custom_call", output_to_operand_aliasing={{}: (8, {})} | custom-call | flops 8589934592 | bytes 20971520 | tf_op jit(solution)/shard_map/pallas_call | solution.py:226
  (34 shorter events, 10.1 us)
Async XLA Ops:
  7.3 93.2 %collective-permute-start.1 = (bf16[256,8320]{1,0:T(8,128)(2,1)}, bf16[256,8320]{1,0:T(8,128)(2,1)}, u32[]{:S(2)}, u32[]{:S(2)}) collective-permute-start(bf16[256,8320]{1,0:T(8,128)(2,1)} %shard_map.28.refs_0_.refs_4_), channel_id=1, source_target_pairs={{0,2},{1,3},{2,0},{3,1},{4,6},{5,7},{6,4},{7,5},{8,10},{9,11},{10,... | collective-permute-start | bytes 12779528 | tf_op jit(solution)/shard_map/ppermute | solution.py:296
  7.5 94.5 %collective-permute-start.3 = (bf16[256,8320]{1,0:T(8,128)(2,1)}, bf16[256,8320]{1,0:T(8,128)(2,1)}, u32[]{:S(2)}, u32[]{:S(2)}) collective-permute-start(bf16[256,8320]{1,0:T(8,128)(2,1)} %shard_map.28.refs_0_.refs_4_), channel_id=1, source_target_pairs={{0,8},{4,12},{8,0},{12,4},{16,24},{20,28},{24,16},{28,20},{1,9},{5... | collective-permute-start | bytes 12779528 | tf_op jit(solution)/shard_map/ppermute | solution.py:296
  7.7 97.0 %collective-permute-start = (bf16[256,8320]{1,0:T(8,128)(2,1)}, bf16[256,8320]{1,0:T(8,128)(2,1)}, u32[]{:S(2)}, u32[]{:S(2)}) collective-permute-start(bf16[256,8320]{1,0:T(8,128)(2,1)} %shard_map.28.refs_0_.refs_4_), channel_id=1, source_target_pairs={{0,1},{1,0},{2,3},{3,2},{4,5},{5,4},{6,7},{7,6},{8,9},{9,8},{10,11... | collective-permute-start | bytes 12779528 | tf_op jit(solution)/shard_map/ppermute | solution.py:296
  8.9 96.0 %collective-permute-start.7 = (bf16[256,8320]{1,0:T(8,128)(2,1)}, bf16[256,8320]{1,0:T(8,128)(2,1)}, u32[]{:S(2)}, u32[]{:S(2)}) collective-permute-start(bf16[256,8320]{1,0:T(8,128)(2,1)} %shard_map.28.refs_0_.refs_4_), channel_id=1, source_target_pairs={{8,16},{12,20},{16,8},{20,12},{9,17},{13,21},{17,9},{21,13},{10,18... | collective-permute-start | bytes 12779528 | tf_op jit(solution)/shard_map/ppermute | solution.py:296
  11.7 94.5 %collective-permute-start.5 = (bf16[256,8320]{1,0:T(8,128)(2,1)}, bf16[256,8320]{1,0:T(8,128)(2,1)}, u32[]{:S(2)}, u32[]{:S(2)}) collective-permute-start(bf16[256,8320]{1,0:T(8,128)(2,1)} %shard_map.28.refs_0_.refs_4_), channel_id=1, source_target_pairs={{0,4},{4,0},{8,12},{12,8},{16,20},{20,16},{24,28},{28,24},{1,5},{5... | collective-permute-start | bytes 12779528 | tf_op jit(solution)/shard_map/ppermute | solution.py:296
  100.5 14.5 %collective-permute-start.2 = (bf16[256,8320]{1,0:T(8,128)(2,1)}, bf16[256,8320]{1,0:T(8,128)(2,1)}, u32[]{:S(2)}, u32[]{:S(2)}) collective-permute-start(bf16[256,8320]{1,0:T(8,128)(2,1)} %collective-permute-done.1.refs_2_), channel_id=1, source_target_pairs={{0,1},{1,0},{2,3},{3,2},{4,5},{5,4},{6,7},{7,6},{8,9},{9,8},{10,11... | collective-permute-start | bytes 12779528 | tf_op jit(solution)/shard_map/ppermute | solution.py:296
  102.0 15.1 %collective-permute-start.4 = (bf16[256,8320]{1,0:T(8,128)(2,1)}, bf16[256,8320]{1,0:T(8,128)(2,1)}, u32[]{:S(2)}, u32[]{:S(2)}) collective-permute-start(bf16[256,8320]{1,0:T(8,128)(2,1)} %collective-permute-done.3.refs_5_.refs_0_), channel_id=1, source_target_pairs={{8,16},{12,20},{16,8},{20,12},{9,17},{13,21},{17,9},{21,13},{10,18... | collective-permute-start | bytes 12779528 | tf_op jit(solution)/shard_map/ppermute | solution.py:296
  104.7 93.6 %collective-permute-start.9 = (bf16[256,8320]{1,0:T(8,128)(2,1)}, bf16[256,8320]{1,0:T(8,128)(2,1)}, u32[]{:S(2)}, u32[]{:S(2)}) collective-permute-start(bf16[256,8320]{1,0:T(8,128)(2,1)} %collective-permute-done.3.refs_5_.refs_0_), channel_id=1, source_target_pairs={{0,2},{1,3},{2,0},{3,1},{4,6},{5,7},{6,4},{7,5},{8,10},{9,11},{10,... | collective-permute-start | bytes 12779528 | tf_op jit(solution)/shard_map/ppermute | solution.py:296
  105.0 94.5 %collective-permute-start.8 = (bf16[256,8320]{1,0:T(8,128)(2,1)}, bf16[256,8320]{1,0:T(8,128)(2,1)}, u32[]{:S(2)}, u32[]{:S(2)}) collective-permute-start(bf16[256,8320]{1,0:T(8,128)(2,1)} %collective-permute-done.7.refs_7_), channel_id=1, source_target_pairs={{8,0},{12,4},{16,24},{20,28},{9,1},{13,5},{17,25},{21,29},{10,2},{... | collective-permute-start | bytes 12779528 | tf_op jit(solution)/shard_map/ppermute | solution.py:296
  106.3 95.8 %collective-permute-start.6 = (bf16[256,8320]{1,0:T(8,128)(2,1)}, bf16[256,8320]{1,0:T(8,128)(2,1)}, u32[]{:S(2)}, u32[]{:S(2)}) collective-permute-start(bf16[256,8320]{1,0:T(8,128)(2,1)} %collective-permute-done.5.refs_6_), channel_id=1, source_target_pairs={{0,8},{4,12},{24,16},{28,20},{1,9},{5,13},{25,17},{29,21},{2,10},{... | collective-permute-start | bytes 12779528 | tf_op jit(solution)/shard_map/ppermute | solution.py:296
  114.9 99.4 %collective-permute-start.15 = (bf16[256,8320]{1,0:T(8,128)(2,1)}, bf16[256,8320]{1,0:T(8,128)(2,1)}, u32[]{:S(2)}, u32[]{:S(2)}) collective-permute-start(bf16[256,8320]{1,0:T(8,128)(2,1)} %collective-permute-done.3.refs_5_.refs_0_), channel_id=1, source_target_pairs={{0,4},{4,0},{24,28},{28,24},{1,5},{5,1},{25,29},{29,25},{2,6},{6,2... | collective-permute-start | bytes 12779528 | tf_op jit(solution)/shard_map/ppermute | solution.py:296
  117.1 99.2 %collective-permute-start.14 = (bf16[256,8320]{1,0:T(8,128)(2,1)}, bf16[256,8320]{1,0:T(8,128)(2,1)}, u32[]{:S(2)}, u32[]{:S(2)}) collective-permute-start(bf16[256,8320]{1,0:T(8,128)(2,1)} %collective-permute-done.7.refs_7_), channel_id=1, source_target_pairs={{8,12},{12,8},{16,20},{20,16},{9,13},{13,9},{17,21},{21,17},{10,14... | collective-permute-start | bytes 12779528 | tf_op jit(solution)/shard_map/ppermute | solution.py:296
  198.3 45.8 %collective-permute-start.12 = (bf16[256,8320]{1,0:T(8,128)(2,1)}, bf16[256,8320]{1,0:T(8,128)(2,1)}, u32[]{:S(2)}, u32[]{:S(2)}) collective-permute-start(bf16[256,8320]{1,0:T(8,128)(2,1)} %collective-permute-done.3.refs_5_.refs_0_), channel_id=1, source_target_pairs={{0,1},{1,0},{2,3},{3,2},{4,5},{5,4},{6,7},{7,6},{8,9},{9,8},{10,11... | collective-permute-start | bytes 12779528 | tf_op jit(solution)/shard_map/ppermute | solution.py:296
  202.1 42.0 %collective-permute-start.13 = (bf16[256,8320]{1,0:T(8,128)(2,1)}, bf16[256,8320]{1,0:T(8,128)(2,1)}, u32[]{:S(2)}, u32[]{:S(2)}) collective-permute-start(bf16[256,8320]{1,0:T(8,128)(2,1)} %collective-permute-done.9.refs_2_), channel_id=1, source_target_pairs={{0,1},{1,0},{2,3},{3,2},{4,5},{5,4},{6,7},{7,6},{8,9},{9,8},{10,11... | collective-permute-start | bytes 12779528 | tf_op jit(solution)/shard_map/ppermute | solution.py:296
  210.3 51.8 %collective-permute-start.10 = (bf16[128,8320]{1,0:T(8,128)(2,1)}, bf16[128,8320]{1,0:T(8,128)(2,1)S(1)}, u32[]{:S(2)}, u32[]{:S(2)}) collective-permute-start(bf16[128,8320]{1,0:T(8,128)(2,1)} %slice.12), channel_id=1, source_target_pairs={{8,12},{12,8},{16,20},{20,16},{9,13},{13,9},{17,21},{21,17},{10,14... | collective-permute-start | bytes 6389768 | tf_op jit(solution)/shard_map/ppermute | solution.py:296
  214.3 47.8 %collective-permute-start.11 = (bf16[128,8320]{1,0:T(8,128)(2,1)}, bf16[128,8320]{1,0:T(8,128)(2,1)}, u32[]{:S(2)}, u32[]{:S(2)}) collective-permute-start(bf16[128,8320]{1,0:T(8,128)(2,1)} %slice.13), channel_id=1, source_target_pairs={{8,16},{12,20},{16,8},{20,12},{9,17},{13,21},{17,9},{21,13},{10,18... | collective-permute-start | bytes 6389768 | tf_op jit(solution)/shard_map/ppermute | solution.py:296
  216.3 173.4 %collective-permute-start.16 = (bf16[256,8320]{1,0:T(8,128)(2,1)}, bf16[256,8320]{1,0:T(8,128)(2,1)}, u32[]{:S(2)}, u32[]{:S(2)}) collective-permute-start(bf16[256,8320]{1,0:T(8,128)(2,1)} %collective-permute-done.8.refs_7_), channel_id=1, source_target_pairs={{0,4},{4,0},{24,28},{28,24},{1,5},{5,1},{25,29},{29,25},{2,6},{6,2... | collective-permute-start | bytes 12779528 | tf_op jit(solution)/shard_map/ppermute | solution.py:296
  260.6 81.2 %collective-permute-start.18 = (f32[4,8,128]{2,1,0:T(8,128)}, f32[4,8,128]{2,1,0:T(8,128)S(1)}, u32[]{:S(2)}, u32[]{:S(2)}) collective-permute-start(f32[4,8,128]{2,1,0:T(8,128)} %get-tuple-element.25), channel_id=1, source_target_pairs={{8,0},{12,4},{16,24},{20,28},{9,1},{13,5},{17,25},{21,29},{10,2},{... | collective-permute-start | bytes 49160 | tf_op jit(solution)/shard_map/ppermute | solution.py:296
  262.1 3.9 copy-start
  264.7 100.9 %collective-permute-start.17 = (f16[2,4,256,256]{3,2,1,0:T(8,128)(2,1)S(1)}, f16[2,4,256,256]{3,2,1,0:T(8,128)(2,1)}, u32[]{:S(2)}, u32[]{:S(2)}) collective-permute-start(f16[2,4,256,256]{3,2,1,0:T(8,128)(2,1)S(1)} %convert_element_type.12), channel_id=1, source_target_pairs={{8,0},{12,4},{16,24},{20,28},{9,1},{13,5},{17,25},{21,29},{10,2},{... | collective-permute-start | bytes 3145736 | tf_op jit(solution)/shard_map/ppermute | solution.py:296
  282.8 82.7 %collective-permute-start.20 = (f32[4,8,128]{2,1,0:T(8,128)}, f32[4,8,128]{2,1,0:T(8,128)S(1)}, u32[]{:S(2)}, u32[]{:S(2)}) collective-permute-start(f32[4,8,128]{2,1,0:T(8,128)} %get-tuple-element.29), channel_id=1, source_target_pairs={{8,0},{12,4},{16,24},{20,28},{9,1},{13,5},{17,25},{21,29},{10,2},{... | collective-permute-start | bytes 49160 | tf_op jit(solution)/shard_map/ppermute | solution.py:296
  285.8 102.3 %collective-permute-start.19 = (f16[2,4,256,256]{3,2,1,0:T(8,128)(2,1)S(1)}, f16[2,4,256,256]{3,2,1,0:T(8,128)(2,1)S(1)}, u32[]{:S(2)}, u32[]{:S(2)}) collective-permute-start(f16[2,4,256,256]{3,2,1,0:T(8,128)(2,1)S(1)} %convert_element_type.14), channel_id=1, source_target_pairs={{8,0},{12,4},{16,24},{20,28},{9,1},{13,5},{17,25},{21,29},{10,2},{... | collective-permute-start | bytes 3145736 | tf_op jit(solution)/shard_map/ppermute | solution.py:296

commit v4 on v3

v4 whole, which is shorter than its diff:
```python
import functools
import math

import jax
import jax.numpy as jnp
from jax import lax
from jax.experimental import pallas as pl
from jax.experimental.pallas import tpu as pltpu
from jax.sharding import PartitionSpec as P


NT = (((1,), (1,)), ((), ()))
LANES = 128
FLOOR = 1e-30


def tile_of(size, most):
    tile = 1
    while tile * 2 <= most and size % (tile * 2) == 0:
        tile *= 2
    return tile


def tied(*values):
    return lax.optimization_barrier(values)


def split_in_three(value):
    parts = []
    for _ in range(2):
        part = value.astype(jnp.bfloat16).astype(jnp.float32)
        parts.append(part)
        value = value - part
    return parts + [value]


def laid_out_body(per_piece, spectra_ref, flags_ref, whole_ref, *piece_refs):
    high, parts, bins, taps = spectra_ref.shape
    half_width = bins * taps

    def fill(out_ref):
        power = jnp.zeros((high, 1), jnp.float32)
        for part in range(parts):
            flat = spectra_ref[:, part].reshape(high, half_width)
            out_ref[:, part * half_width : (part + 1) * half_width] = flat
            widened = flat.astype(jnp.float32)
            power = power + jnp.sum(widened * widened, axis=1, keepdims=True)
        power_mean = power / (parts * half_width)
        factor = flags_ref[...].astype(jnp.float32) * lax.rsqrt(power_mean + 1e-06)
        norm = lax.rsqrt(jnp.maximum(power_mean, FLOOR))
        lane = lax.broadcasted_iota(jnp.int32, (high, LANES), 1)
        marks = jnp.zeros((high, LANES), jnp.float32)
        for index, value in enumerate(split_in_three(factor) + split_in_three(norm)):
            marks = jnp.where(lane == index, value, marks)
        out_ref[:, parts * half_width :] = marks.astype(jnp.bfloat16)

    fill(whole_ref)
    for piece, out_ref in enumerate(piece_refs):

        @pl.when(pl.program_id(0) // per_piece == piece)
        def _():
            out_ref[...] = whole_ref[...]


def laid_out(spectra, flags, pieces):
    rows, parts, bins, taps = spectra.shape
    width = parts * bins * taps + LANES
    high = tile_of(rows // pieces, 64)
    per_piece = rows // pieces // high

    def place(piece):
        first = piece * per_piece
        return lambda i: (jnp.clip(i - first, 0, per_piece - 1), 0)

    return pl.pallas_call(
        functools.partial(laid_out_body, per_piece),
        grid=(rows // high,),
        in_specs=[
            pl.BlockSpec((high, parts, bins, taps), lambda i: (i, 0, 0, 0)),
            pl.BlockSpec((high, 1), lambda i: (i, 0)),
        ],
        out_specs=[pl.BlockSpec((high, width), lambda i: (i, 0))]
        + [pl.BlockSpec((high, width), place(piece)) for piece in range(pieces)],
        out_shape=[jax.ShapeDtypeStruct((rows, width), spectra.dtype)]
        + [jax.ShapeDtypeStruct((rows // pieces, width), spectra.dtype)] * pieces,
    )(spectra, flags.reshape(rows, 1))


def products_body(sizes, scale_coef, raw, plan_ref, *refs):
    shapes, at_once, known, units = sizes
    refs = list(refs)
    rows, at = [], 0
    for shape in shapes:
        rows.append(refs[at : at + len(shape)])
        at += len(shape)
    columns = refs[at : at + known]
    held, right, col_marks, staged, row_sems, col_sems, out_sems = refs[-7:]
    outs = refs[-9:-7] if raw else refs[-8:-7]
    unit, part = pl.program_id(0), pl.program_id(1)
    parts = len(rows) // at_once
    now = unit * parts + part
    shard_rows = held.shape[1] // at_once
    cols, half_width = right.shape[1] // 2, right.shape[2] // 2
    half_cols = cols // 2

    def row_copies(index, row, slot):
        copies, top = [], row * shard_rows
        for number, piece in enumerate(rows[index]):
            where = held.at[slot, pl.ds(top, piece.shape[0])]
            copies.append(pltpu.make_async_copy(piece, where, row_sems.at[slot, row, number]))
            top += piece.shape[0]
        return copies

    def start_rows(which, slot):
        for index in range(parts):

            @pl.when(which == index)
            def _():
                for row in range(at_once):
                    for copy in row_copies(index * at_once + row, row, slot):
                        copy.start()

    def col_copies(source, half, slot):
        top = half * half_cols
        real = source.at[:, pl.ds(0, half_width)]
        imag = source.at[:, pl.ds(half_width, half_width)]
        marks = source.at[:, pl.ds(2 * half_width, LANES)]
        places = [
            (real, right.at[slot, pl.ds(top, half_cols), pl.ds(0, half_width)]),
            (imag, right.at[slot, pl.ds(top, half_cols), pl.ds(half_width, half_width)]),
            (real, right.at[slot, pl.ds(cols + top, half_cols), pl.ds(half_width, half_width)]),
            (marks, col_marks.at[slot, pl.ds(top, half_cols)]),
        ]
        return [
            pltpu.make_async_copy(start, end, col_sems.at[slot, half, kind])
            for kind, (start, end) in enumerate(places)
        ]

    def start_cols(which, slot):
        for half in range(2):
            for index in range(known):

                @pl.when(plan_ref[2 * which + half] == index)
                def _():
                    for copy in col_copies(columns[index], half, slot):
                        copy.start()

    def out_copies(slot):
        copies = []
        for row in range(at_once):
            group = plan_ref[4 * units + part * at_once + row]
            for half in range(2):
                start = plan_ref[2 * units + 2 * unit + half] * half_cols
                lanes = pl.ds(pl.multiple_of(start, half_cols), half_cols)
                source = staged.at[slot, :, row, :, pl.ds(half * half_cols, half_cols)]
                target = outs[0].at[:, group, :, lanes]
                copies.append(pltpu.make_async_copy(source, target, out_sems.at[slot, row, half]))
        return copies

    slot, col_slot = lax.rem(now, 2), lax.rem(unit, 2)

    @pl.when(now == 0)
    def _():
        start_rows(0, 0)
        start_cols(0, 0)

    @pl.when(now + 1 < units * parts)
    def _():
        start_rows(lax.rem(part + 1, parts), lax.rem(now + 1, 2))

    @pl.when(jnp.logical_and(part == 0, unit + 1 < units))
    def _():
        start_cols(unit + 1, lax.rem(unit + 1, 2))

    @pl.when(part == 0)
    def _():
        for half in range(2):
            for copy in col_copies(columns[0], half, col_slot):
                copy.wait()
        right[col_slot, cols:, :half_width] = -right[col_slot, :cols, half_width:]

    for row in range(at_once):
        for copy in row_copies(row, row, slot):
            copy.wait()

    left = held[slot, :, : 2 * half_width]
    product = lax.dot_general(left, right[col_slot], NT, preferred_element_type=jnp.float32)

    @pl.when(now >= 2)
    def _():
        for copy in out_copies(slot):
            copy.wait()

    def sums(values, axis):
        def one(first):
            take = [lax.slice_in_dim(values, i, i + 1, axis=axis) for i in range(first, first + 3)]
            return (take[2] + take[1]) + take[0]

        return one(0), one(3)

    col_factor, col_norm = sums(col_marks[col_slot].astype(jnp.float32).T, 0)
    for row in range(at_once):
        top = row * shard_rows
        marks = held[slot, pl.ds(top, shard_rows), pl.ds(2 * half_width, LANES)]
        row_factor, row_norm = sums(marks.astype(jnp.float32), 1)
        scaling = (row_factor * scale_coef) * col_factor
        if raw:
            bound = jnp.max(row_factor / row_norm, axis=0, keepdims=True)
            bound = bound * jnp.max(col_factor / col_norm, axis=1, keepdims=True)
            unit_size = jnp.maximum(bound * (2 * half_width * scale_coef), FLOOR) / 32768
            outs[1][row] = jnp.broadcast_to(unit_size, outs[1].shape[1:])
            scaling = scaling * (1 / unit_size)
        staged[slot, 0, row] = product[top : top + shard_rows, :cols] * scaling
        staged[slot, 1, row] = product[top : top + shard_rows, cols:] * scaling

    for copy in out_copies(slot):
        copy.start()

    @pl.when(now == units * parts - 1)
    def _():
        for copy in out_copies(lax.rem(now + 1, 2)) + out_copies(slot):
            copy.wait()


def products(out, rows, columns, choice, slots, mine, blocks, scale_coef, raw=False):
    shard_rows = sum(piece.shape[0] for piece in rows[0])
    width = rows[0][0].shape[1]
    half_width = (width - LANES) // 2
    units, count = len(choice) // 2, len(rows)
    at_once = 2 if units > 1 and count > 1 else 1
    parts = count // at_once
    cols = 2 * columns[0].shape[0]
    whole = pl.BlockSpec(memory_space=pl.ANY)
    operands = [piece for pieces in rows for piece in pieces] + list(columns)
    aliases = {}
    if out is not None:
        aliases = {1 + len(operands): 0}
        operands.append(out)
    groups = [mine ^ j for j in range(count)]
    plan = jnp.stack(list(choice) + list(slots) + groups).astype(jnp.int32)
    shape = (2, count, shard_rows, cols if raw else shard_rows * blocks)
    out_shape = [jax.ShapeDtypeStruct(shape, jnp.float32)]
    out_specs = [whole]
    if raw:
        out_shape.append(jax.ShapeDtypeStruct((count, 8, LANES), jnp.float32))
        out_specs.append(
            pl.BlockSpec((at_once, 8, LANES), lambda i, j, s: (s[4 * units + j], 0, 0))
        )
    shapes = [[piece.shape[0] for piece in pieces] for pieces in rows]
    most = max(len(pieces) for pieces in rows)
    given = pl.pallas_call(
        functools.partial(products_body, (shapes, at_once, len(columns), units), scale_coef, raw),
        grid_spec=pltpu.PrefetchScalarGridSpec(
            num_scalar_prefetch=1,
            grid=(units, parts),
            in_specs=[whole] * len(operands),
            out_specs=out_specs,
            scratch_shapes=[
                pltpu.VMEM((2, at_once * shard_rows, width), rows[0][0].dtype),
                pltpu.VMEM((2, 2 * cols, 2 * half_width), rows[0][0].dtype),
                pltpu.VMEM((2, cols, LANES), rows[0][0].dtype),
                pltpu.VMEM((2, 2, at_once, shard_rows, cols), jnp.float32),
                pltpu.SemaphoreType.DMA((2, at_once, most)),
                pltpu.SemaphoreType.DMA((2, 2, 4)),
                pltpu.SemaphoreType.DMA((2, at_once, 2)),
            ],
        ),
        out_shape=out_shape,
        input_output_aliases=aliases,
        cost_estimate=pl.CostEstimate(
            flops=8 * units * count * shard_rows * cols * half_width,
            bytes_accessed=4 * units * half_width * (count * shard_rows + cols),
            transcendentals=0,
        ),
        compiler_params=pltpu.CompilerParams(
            dimension_semantics=("arbitrary", "arbitrary"), vmem_limit_bytes=60 * 2**20
        ),
    )(plan, *operands)
    return given if raw else given[0]


def gathered(spectra, detector_valid, scale_coef):
    shard_rows = spectra.shape[1]
    half_width = spectra.shape[3] * spectra.shape[4]
    flattened = spectra.reshape(shard_rows, 2 * half_width)
    widened = flattened.astype(jnp.float32)
    power_mean = jnp.mean(widened * widened, axis=1) + 1e-06
    own_factor = detector_valid.reshape(shard_rows).astype(jnp.float32) * lax.rsqrt(power_mean)
    rows = lax.all_gather(flattened, "grp", axis=0, tiled=True)
    cols = lax.all_gather(flattened, "blk", axis=0, tiled=True)
    row_factor = lax.all_gather(own_factor, "grp", axis=0, tiled=True) * scale_coef
    col_factor = lax.all_gather(own_factor, "blk", axis=0, tiled=True)
    rotated = jnp.concatenate([-cols[:, half_width:], cols[:, :half_width]], axis=1)
    scaling = row_factor[:, None] * col_factor[None, :]
    parts = [
        lax.dot_general(rows, right, NT, preferred_element_type=jnp.float32) * scaling
        for right in (cols, rotated)
    ]
    return jnp.stack(parts)


def shards(spectra, detector_valid):
    shard_rows = spectra.shape[1]
    half_width = spectra.shape[3] * spectra.shape[4]
    blocks = lax.axis_size("blk")
    group_size = lax.axis_size("grp")
    scale_coef = 0.5 / math.sqrt(half_width)
    shape = (2, group_size, shard_rows, blocks * shard_rows)
    fits = shard_rows % 256 == 0 and half_width % 128 == 0 and group_size & (group_size - 1) == 0
    if blocks != 8 or group_size < 2 or not fits:
        return gathered(spectra, detector_valid, scale_coef).reshape(shape)

    devices = range(blocks)
    inner = [b for b in devices if 0 < b // 2 < blocks // 2 - 1]
    ends = [b for b in devices if b not in inner]
    me = lax.axis_index("blk")
    mine = lax.axis_index("grp")
    is_end = jnp.logical_or(me // 2 == 0, me // 2 == blocks // 2 - 1)

    def moved(value, axis, route):
        if isinstance(value, tuple):
            return tuple(moved(piece, axis, route) for piece in value)
        return lax.ppermute(value, axis, route)

    def swap(value, among, by):
        return moved(value, "blk", [(b, b ^ by) for b in among])

    def spread(value, by):
        return moved(value, "grp", [(g, g ^ by) for g in range(group_size)])

    def begun(value):
        return {0: value, group_size // 2: spread(value, group_size // 2)}

    def finished(arrays):
        by = group_size // 4
        while by:
            arrays = arrays | {key ^ by: spread(array, by) for key, array in arrays.items()}
            by //= 2
        return [arrays[key] for key in range(group_size)]

    def held_for(value, *after):
        return tied(value, *after)[0]

    def either(inner_value, end_value):
        return jnp.where(is_end, end_value, inner_value)

    def put(out, columns, units):
        halves = [half for column in columns for half in column]
        choice, slots = [], []
        for inner_half, end_half in units:
            choice.append(either(*(2 * c + h for c, h, _ in (inner_half, end_half))))
            slots.append(
                either(*(2 * (me ^ slot) + h for _, h, slot in (inner_half, end_half)))
            )
        return products(out, rows, halves, choice, slots, mine, blocks, scale_coef)

    def both(inner_column, inner_slot, end_column, end_slot):
        return [((inner_column, h, inner_slot), (end_column, h, end_slot)) for h in (0, 1)]

    whole, *own = laid_out(spectra[0], detector_valid[0], 2)
    own = tuple(own)
    near = swap(own, devices, 2)
    beside = swap(own, devices, 1)
    across = swap(own, inner, 6)
    rows = begun(whole)
    last = group_size // 2
    rows[last] = held_for(rows[last], *near, *beside, *across)
    rows = [(array,) for array in finished(rows)]

    far_end = swap(near, inner, 6)
    end_beside = swap(beside, ends, 2)
    far_inner = swap(across, inner, 2)
    across_beside = swap(across, inner, 1)
    near_beside = swap(near, ends, 1)
    client = begun(near)

    out = put(
        None,
        [own, near, beside, across],
        both(0, 0, 0, 0) + both(1, 2, 1, 2) + both(2, 1, 2, 1) + both(3, 6, 0, 5),
    )
    out = put(
        out,
        [far_end[:1] * 2, end_beside[:1] * 2, far_inner[:1] * 2, near_beside[:1] * 2],
        [((0, 0, 4), (2, 0, 4)), ((1, 0, 3), (3, 0, 3))],
    )
    *held, out = tied(
        far_end[0], end_beside[1], far_inner[0], across_beside[1], *client[last], out
    )
    client[last] = tuple(held[4:])
    low = swap(held[0], inner, 1)
    high = swap(held[1], inner, 6)
    low_beside = swap(held[2], ends, 1)
    high_beside = swap(held[3], inner, 2)
    client = finished(client)

    def serve(columns):
        zero = me * 0
        pick = [zero, zero + 1]
        return products(None, client, columns, pick, pick, mine, blocks, scale_coef, raw=True)

    def deliver(block, unit_size):
        return swap(block.astype(jnp.float16), inner, 2), swap(unit_size, inner, 2)

    def place(out, sent, end_slot):
        block, unit_size = sent
        block = block.astype(jnp.float32) * unit_size[None, :, :1, :1]
        start = (me ^ end_slot) * shard_rows
        starts = [jnp.zeros_like(start)] * 3 + [start]
        kept = lax.dynamic_slice(out, starts, block.shape)
        return lax.dynamic_update_slice(out, jnp.where(is_end, block, kept), starts)

    first = serve(far_end)
    sent_a = deliver(*first)
    out, _ = tied(out, first[1])
    out = put(
        out,
        [across_beside, far_end, end_beside, far_inner, near_beside],
        both(0, 7, 3, 6) + [((1, 1, 4), (3, 1, 4)), ((2, 1, 3), (4, 1, 3))],
    )
    low, high, low_beside, high_beside, out = tied(low, high, low_beside, high_beside, out)
    second = serve((low, high))
    sent_b = deliver(*second)
    out, _ = tied(out, second[1])
    out = put(out, [(low, high), (low_beside, high_beside)], both(0, 5, 1, 5))
    out = place(out, sent_a, 6)
    out = place(out, sent_b, 7)
    return out.reshape(shape)


def solution(mesh):
    return jax.shard_map(
        shards,
        mesh=mesh,
        in_specs=(P("grp", "blk", None, None, None), P("grp", "blk")),
        out_specs=P(None, None, "blk", "grp"),
        check_vma=False,
    )
```

time: 412 us -> 482 us (1.17)
  waiting for transfers between devices: 203 us -> 261 us
  starting transfers between devices: 37.2 us -> 50.4 us
  local copies, waits for them, and re-layouts: 11.2 us -> 4.93 us
  Pallas kernels: 146 us -> 152 us
    ppermute x21 -> x33, waiting for transfers between devices: 203 us -> 261 us  [moved(): return lax.ppermute(value, axis, route)]
    ppermute x21 -> x33, starting transfers between devices: 37.2 us -> 50.4 us  [moved(): return lax.ppermute(value, axis, route)]
    slice x2 -> x0, local copies, waits for them, and re-layouts: 6.2 us -> none  [the longest x1 3.15 us: shards(): high = swap(end_beside[half:], inner, 6)]
    pallas_call x7, Pallas kernels: 146 us -> 152 us  [the longest x6 145 us: products(): pl.pallas_call(functools.partial(products_body, (shapes, at_once, len(col...]
  transfers between devices with their start and end apart: 21 -> 33, of which waited for: 6 -> 9; matrix products, arithmetic and copies ran while one was open for 5% -> 2% of each run, Pallas kernels for 30% -> 30%
where the time goes in v4:
time: 482 us; the launch traced here: 477 us
  waiting for transfers between devices  261 us (54%)
  Pallas kernels  152 us (32%)
  starting transfers between devices  50.4 us (10%)
  other arithmetic  8.66 us (2%)
  local copies, waits for them, and re-layouts  4.93 us (1%)
    ppermute x33, waiting for transfers between devices, moved(): return lax.ppermute(value, axis, route)  261 us
    pallas_call x6, Pallas kernels, products(): pl.pallas_call(functools.partial(products_body, (shapes, at_once, len(col...  145 us
    ppermute x33, starting transfers between devices, moved(): return lax.ppermute(value, axis, route)  50.4 us
  transfers between devices with their start and end apart: 33, of which 9 were waited for; matrix products, arithmetic and copies ran while one was open for 2% of the time, Pallas kernels for 30%

profile of v4, /device:TPU:31, one launch (start us, length us, event | category | flops | bytes accessed | tf_op | source)
XLA Modules:
  0.0 477.2 jit_solution(9579601578034046049)
XLA Ops:
  1.5 6.9 %shard_map.28 = (bf16[256,8320]{1,0:T(8,128)(2,1)}, bf16[128,8320]{1,0:T(8,128)(2,1)}, bf16[128,8320]{1,0:T(8,128)(2,1)}) custom-call(bf16[256,2,16,256]{3,2,1,0:T(8,128)(2,1)} %bitcast.32, s32[256,1]{1,0:T(8,128)} %copy.6.flags_ref), custom_call_target="tpu_custom_call" | custom-call | tf_op jit(solution)/shard_map/pallas_call | solution.py:75
  9.8 2.0 collective-permute-start.6
  12.8 43.0 %collective-permute-done.2.refs_6_.refs_0_ = bf16[128,8320]{1,0:T(8,128)(2,1)} collective-permute-done((bf16[128,8320]{1,0:T(8,128)(2,1)}, bf16[128,8320]{1,0:T(8,128)(2,1)}, u32[]{:S(2)}, u32[]{:S(2)}) %collective-permute-start.2) | collective-permute-done | bytes 2129952 | tf_op jit(solution)/shard_map/ppermute | solution.py:323
  56.1 45.4 %collective-permute-done.3.refs_7_.refs_1_ = bf16[128,8320]{1,0:T(8,128)(2,1)} collective-permute-done((bf16[128,8320]{1,0:T(8,128)(2,1)}, bf16[128,8320]{1,0:T(8,128)(2,1)}, u32[]{:S(2)}, u32[]{:S(2)}) %collective-permute-start.3) | collective-permute-done | bytes 2129952 | tf_op jit(solution)/shard_map/ppermute | solution.py:323
  101.5 1.5 collective-permute-start
  104.1 3.1 collective-permute-start.16
  107.3 43.9 %collective-permute-done.5.refs_9_ = bf16[128,8320]{1,0:T(8,128)(2,1)S(1)} collective-permute-done((bf16[128,8320]{1,0:T(8,128)(2,1)}, bf16[128,8320]{1,0:T(8,128)(2,1)S(1)}, u32[]{:S(2)}, u32[]{:S(2)}) %collective-permute-start.5) | collective-permute-done | bytes 2129952 | tf_op jit(solution)/shard_map/ppermute | solution.py:323
  153.8 6.6 %collective-permute-start.15 = (bf16[128,8320]{1,0:T(8,128)(2,1)}, bf16[128,8320]{1,0:T(8,128)(2,1)}, u32[]{:S(2)}, u32[]{:S(2)}) collective-permute-start(bf16[128,8320]{1,0:T(8,128)(2,1)} %collective-permute-done.4.refs_8_), channel_id=1, source_target_pairs={{0,8},{4,12},{24,16},{28,20},{1,9},{5,13},{25,17},{29,21},{2,10},{... | collective-permute-start | bytes 6389768 | tf_op jit(solution)/shard_map/ppermute | solution.py:323
  160.7 36.2 %collective-permute-done.16.refs_10_.refs_11_.refs_12_ = bf16[128,8320]{1,0:T(8,128)(2,1)} collective-permute-done((bf16[128,8320]{1,0:T(8,128)(2,1)}, bf16[128,8320]{1,0:T(8,128)(2,1)}, u32[]{:S(2)}, u32[]{:S(2)}) %collective-permute-start.16) | collective-permute-done | bytes 2129952 | tf_op jit(solution)/shard_map/ppermute | solution.py:323
  198.5 4.1 collective-permute-done.11.refs_8_.refs_9_.refs_10_
  202.6 2.0 collective-permute-start.12
  204.8 5.4 %collective-permute-start.10 = (bf16[128,8320]{1,0:T(8,128)(2,1)}, bf16[128,8320]{1,0:T(8,128)(2,1)}, u32[]{:S(2)}, u32[]{:S(2)}) collective-permute-start(bf16[128,8320]{1,0:T(8,128)(2,1)} %copy-done.4), channel_id=1, source_target_pairs={{0,8},{4,12},{24,16},{28,20},{1,9},{5,13},{25,17},{29,21},{2,10},{... | collective-permute-start | bytes 6389768 | tf_op jit(solution)/shard_map/ppermute | solution.py:323
  210.2 2.0 collective-permute-start.22
  212.2 41.6 %collective-permute-done.14.refs_5_ = bf16[128,8320]{1,0:T(8,128)(2,1)} collective-permute-done((bf16[128,8320]{1,0:T(8,128)(2,1)}, bf16[128,8320]{1,0:T(8,128)(2,1)}, u32[]{:S(2)}, u32[]{:S(2)}) %collective-permute-start.14) | collective-permute-done | bytes 2129952 | tf_op jit(solution)/shard_map/ppermute | solution.py:323
  255.2 47.3 %shard_map.29.refs_12_ = f32[2,4,256,2048]{3,2,1,0:T(8,128)} custom-call(s32[20]{0:T(128)} %stack.156.plan_ref, bf16[256,8320]{1,0:T(8,128)(2,1)} %get-tuple-element.27.refs_0_, bf16[256,8320]{1,0:T(8,128)(2,1)} %collective-permute-done.refs_1_, bf16[256,8320]{1,0:T(8,128)(2,1)} %collective-permute-done.1.refs_2_, ...), custom_call_target="tpu_custom_call" | custom-call | flops 34359738368 | bytes 83886080 | tf_op jit(solution)/shard_map/pallas_call | solution.py:251
  302.5 16.3 %shard_map.30.refs_14_ = f32[2,4,256,2048]{3,2,1,0:T(8,128)} custom-call(s32[8]{0:T(128)} %stack.145.plan_ref, bf16[256,8320]{1,0:T(8,128)(2,1)} %get-tuple-element.27.refs_0_, bf16[256,8320]{1,0:T(8,128)(2,1)} %collective-permute-done.refs_1_, bf16[256,8320]{1,0:T(8,128)(2,1)} %collective-permute-done.1.refs_2_, ...), custom_call_target="tpu_custom_call", output_to_operand_aliasing={{}: (13, {})} | custom-call | flops 8589934592 | bytes 20971520 | tf_op jit(solution)/shard_map/pallas_call | solution.py:251
  318.8 2.1 collective-permute-start.24
  320.9 2.0 collective-permute-start.21
  327.0 41.4 %collective-permute-done.24.refs_13_ = bf16[128,8320]{1,0:T(8,128)(2,1)S(1)} collective-permute-done((bf16[128,8320]{1,0:T(8,128)(2,1)}, bf16[128,8320]{1,0:T(8,128)(2,1)S(1)}, u32[]{:S(2)}, u32[]{:S(2)}) %collective-permute-start.24) | collective-permute-done | bytes 2129952 | tf_op jit(solution)/shard_map/ppermute | solution.py:323
  368.4 2.0 collective-permute-start.17
  370.4 2.0 collective-permute-start.18
  372.4 2.1 collective-permute-start.19
  374.5 1.5 collective-permute-start.20
  376.0 19.1 %shard_map.31 = (f32[2,4,256,256]{3,2,1,0:T(8,128)}, f32[4,8,128]{2,1,0:T(8,128)}) custom-call(s32[8]{0:T(128)} %stack.166.plan_ref, bf16[128,8320]{1,0:T(8,128)(2,1)} %collective-permute-done.2.refs_6_.refs_0_, bf16[128,8320]{1,0:T(8,128)(2,1)} %collective-permute-done.3.refs_7_.refs_1_, bf16[128,8320]{1,0:T(8,128)(2,1)} %collective-permute-done.25.refs_2_, ...), custom_call_target="tpu_custom_call" | custom-call | flops 8589934592 | bytes 20971520 | tf_op jit(solution)/shard_map/pallas_call | solution.py:251
  396.5 27.1 %shard_map.32.refs_8_ = f32[2,4,256,2048]{3,2,1,0:T(8,128)} custom-call(s32[12]{0:T(128)} %stack.165.plan_ref, bf16[256,8320]{1,0:T(8,128)(2,1)} %get-tuple-element.27.refs_0_, bf16[256,8320]{1,0:T(8,128)(2,1)} %collective-permute-done.refs_1_, bf16[256,8320]{1,0:T(8,128)(2,1)} %collective-permute-done.1.refs_2_, ...), custom_call_target="tpu_custom_call", output_to_operand_aliasing={{}: (15, {})} | custom-call | flops 17179869184 | bytes 41943040 | tf_op jit(solution)/shard_map/pallas_call | solution.py:251
  425.2 19.0 %shard_map.33 = (f32[2,4,256,256]{3,2,1,0:T(8,128)}, f32[4,8,128]{2,1,0:T(8,128)}) custom-call(s32[8]{0:T(128)} %stack.166.plan_ref, bf16[128,8320]{1,0:T(8,128)(2,1)} %collective-permute-done.2.refs_6_.refs_0_, bf16[128,8320]{1,0:T(8,128)(2,1)} %collective-permute-done.3.refs_7_.refs_1_, bf16[128,8320]{1,0:T(8,128)(2,1)} %collective-permute-done.25.refs_2_, ...), custom_call_target="tpu_custom_call" | custom-call | flops 8589934592 | bytes 20971520 | tf_op jit(solution)/shard_map/pallas_call | solution.py:251
  445.5 1.8 convert_element_type.14
  447.3 1.5 collective-permute-start.31
  448.8 16.3 %shard_map.34 = f32[2,4,256,2048]{3,2,1,0:T(8,128)} custom-call(s32[8]{0:T(128)} %stack.140.plan_ref, bf16[256,8320]{1,0:T(8,128)(2,1)} %get-tuple-element.27.refs_0_, bf16[256,8320]{1,0:T(8,128)(2,1)} %collective-permute-done.refs_1_, bf16[256,8320]{1,0:T(8,128)(2,1)} %collective-permute-done.1.refs_2_, ...), custom_call_target="tpu_custom_call", output_to_operand_aliasing={{}: (9, {})} | custom-call | flops 8589934592 | bytes 20971520 | tf_op jit(solution)/shard_map/pallas_call | solution.py:251
  465.3 3.2 select_dynamic-update-slice_fusion.1
  468.6 5.2 %collective-permute-done.31 = f16[2,4,256,256]{3,2,1,0:T(8,128)(2,1)} collective-permute-done((f16[2,4,256,256]{3,2,1,0:T(8,128)(2,1)S(1)}, f16[2,4,256,256]{3,2,1,0:T(8,128)(2,1)}, u32[]{:S(2)}, u32[]{:S(2)}) %collective-permute-start.31) | collective-permute-done | bytes 1048608 | tf_op jit(solution)/shard_map/ppermute | solution.py:323
  473.7 3.5 select_dynamic-update-slice_fusion
  (63 shorter events, 19.8 us)
Async XLA Ops:
  8.3 47.5 %collective-permute-start.2 = (bf16[128,8320]{1,0:T(8,128)(2,1)}, bf16[128,8320]{1,0:T(8,128)(2,1)}, u32[]{:S(2)}, u32[]{:S(2)}) collective-permute-start(bf16[128,8320]{1,0:T(8,128)(2,1)} %get-tuple-element.28.refs_4_), channel_id=1, source_target_pairs={{0,8},{4,12},{8,0},{12,4},{16,24},{20,28},{24,16},{28,20},{1,9},{5... | collective-permute-start | bytes 6389768 | tf_op jit(solution)/shard_map/ppermute | solution.py:323
  8.5 93.0 %collective-permute-start.3 = (bf16[128,8320]{1,0:T(8,128)(2,1)}, bf16[128,8320]{1,0:T(8,128)(2,1)}, u32[]{:S(2)}, u32[]{:S(2)}) collective-permute-start(bf16[128,8320]{1,0:T(8,128)(2,1)} %get-tuple-element.29.refs_5_), channel_id=1, source_target_pairs={{0,8},{4,12},{8,0},{12,4},{16,24},{20,28},{24,16},{28,20},{1,9},{5... | collective-permute-start | bytes 6389768 | tf_op jit(solution)/shard_map/ppermute | solution.py:323
  9.8 93.2 %collective-permute-start.6 = (bf16[128,8320]{1,0:T(8,128)(2,1)}, bf16[128,8320]{1,0:T(8,128)(2,1)}, u32[]{:S(2)}, u32[]{:S(2)}) collective-permute-start(bf16[128,8320]{1,0:T(8,128)(2,1)} %get-tuple-element.28.refs_4_), channel_id=1, source_target_pairs={{8,16},{12,20},{16,8},{20,12},{9,17},{13,21},{17,9},{21,13},{10,18... | collective-permute-start | bytes 6389768 | tf_op jit(solution)/shard_map/ppermute | solution.py:323
  11.8 139.4 %collective-permute-start.1 = (bf16[256,8320]{1,0:T(8,128)(2,1)}, bf16[256,8320]{1,0:T(8,128)(2,1)}, u32[]{:S(2)}, u32[]{:S(2)}) collective-permute-start(bf16[256,8320]{1,0:T(8,128)(2,1)} %get-tuple-element.27.refs_0_), channel_id=1, source_target_pairs={{0,2},{1,3},{2,0},{3,1},{4,6},{5,7},{6,4},{7,5},{8,10},{9,11},{10,... | collective-permute-start | bytes 12779528 | tf_op jit(solution)/shard_map/ppermute | solution.py:323
  12.1 91.2 %collective-permute-start.7 = (bf16[128,8320]{1,0:T(8,128)(2,1)}, bf16[128,8320]{1,0:T(8,128)(2,1)S(1)}, u32[]{:S(2)}, u32[]{:S(2)}) collective-permute-start(bf16[128,8320]{1,0:T(8,128)(2,1)} %get-tuple-element.29.refs_5_), channel_id=1, source_target_pairs={{8,16},{12,20},{16,8},{20,12},{9,17},{13,21},{17,9},{21,13},{10,18... | collective-permute-start | bytes 6389768 | tf_op jit(solution)/shard_map/ppermute | solution.py:323
  55.9 48.2 %collective-permute-start.4 = (bf16[128,8320]{1,0:T(8,128)(2,1)}, bf16[128,8320]{1,0:T(8,128)(2,1)}, u32[]{:S(2)}, u32[]{:S(2)}) collective-permute-start(bf16[128,8320]{1,0:T(8,128)(2,1)} %get-tuple-element.28.refs_4_), channel_id=1, source_target_pairs={{0,4},{4,0},{8,12},{12,8},{16,20},{20,16},{24,28},{28,24},{1,5},{5... | collective-permute-start | bytes 6389768 | tf_op jit(solution)/shard_map/ppermute | solution.py:323
  101.5 52.3 %collective-permute-start = (bf16[256,8320]{1,0:T(8,128)(2,1)}, bf16[256,8320]{1,0:T(8,128)(2,1)}, u32[]{:S(2)}, u32[]{:S(2)}) collective-permute-start(bf16[256,8320]{1,0:T(8,128)(2,1)} %get-tuple-element.27.refs_0_), channel_id=1, source_target_pairs={{0,1},{1,0},{2,3},{3,2},{4,5},{5,4},{6,7},{7,6},{8,9},{9,8},{10,11... | collective-permute-start | bytes 12779528 | tf_op jit(solution)/shard_map/ppermute | solution.py:323
  103.1 48.1 %collective-permute-start.5 = (bf16[128,8320]{1,0:T(8,128)(2,1)}, bf16[128,8320]{1,0:T(8,128)(2,1)S(1)}, u32[]{:S(2)}, u32[]{:S(2)}) collective-permute-start(bf16[128,8320]{1,0:T(8,128)(2,1)} %get-tuple-element.29.refs_5_), channel_id=1, source_target_pairs={{0,4},{4,0},{8,12},{12,8},{16,20},{20,16},{24,28},{28,24},{1,5},{5... | collective-permute-start | bytes 6389768 | tf_op jit(solution)/shard_map/ppermute | solution.py:323
  103.3 57.1 %collective-permute-start.9 = (bf16[128,8320]{1,0:T(8,128)(2,1)}, bf16[128,8320]{1,0:T(8,128)(2,1)S(1)}, u32[]{:S(2)}, u32[]{:S(2)}) collective-permute-start(bf16[128,8320]{1,0:T(8,128)(2,1)} %collective-permute-done.2.refs_6_.refs_0_), channel_id=1, source_target_pairs={{8,16},{12,20},{16,8},{20,12},{9,17},{13,21},{17,9},{21,13},{10,18... | collective-permute-start | bytes 6389768 | tf_op jit(solution)/shard_map/ppermute | solution.py:323
  104.1 92.8 %collective-permute-start.16 = (bf16[128,8320]{1,0:T(8,128)(2,1)}, bf16[128,8320]{1,0:T(8,128)(2,1)}, u32[]{:S(2)}, u32[]{:S(2)}) collective-permute-start(bf16[128,8320]{1,0:T(8,128)(2,1)} %collective-permute-done.2.refs_6_.refs_0_), channel_id=1, source_target_pairs={{0,4},{4,0},{24,28},{28,24},{1,5},{5,1},{25,29},{29,25},{2,6},{6,2... | collective-permute-start | bytes 6389768 | tf_op jit(solution)/shard_map/ppermute | solution.py:323
  151.2 104.0 %collective-permute-start.8 = (bf16[256,8320]{1,0:T(8,128)(2,1)}, bf16[256,8320]{1,0:T(8,128)(2,1)}, u32[]{:S(2)}, u32[]{:S(2)}) collective-permute-start(bf16[256,8320]{1,0:T(8,128)(2,1)} %collective-permute-done.1.refs_2_), channel_id=1, source_target_pairs={{0,1},{1,0},{2,3},{3,2},{4,5},{5,4},{6,7},{7,6},{8,9},{9,8},{10,11... | collective-permute-start | bytes 12779528 | tf_op jit(solution)/shard_map/ppermute | solution.py:323
  152.5 50.1 %collective-permute-start.11 = (bf16[128,8320]{1,0:T(8,128)(2,1)}, bf16[128,8320]{1,0:T(8,128)(2,1)}, u32[]{:S(2)}, u32[]{:S(2)}) collective-permute-start(bf16[128,8320]{1,0:T(8,128)(2,1)} %collective-permute-done.6.refs_10_), channel_id=1, source_target_pairs={{8,0},{12,4},{16,24},{20,28},{9,1},{13,5},{17,25},{21,29},{10,2},{... | collective-permute-start | bytes 6389768 | tf_op jit(solution)/shard_map/ppermute | solution.py:323
  153.8 51.0 %collective-permute-start.15 = (bf16[128,8320]{1,0:T(8,128)(2,1)}, bf16[128,8320]{1,0:T(8,128)(2,1)}, u32[]{:S(2)}, u32[]{:S(2)}) collective-permute-start(bf16[128,8320]{1,0:T(8,128)(2,1)} %collective-permute-done.4.refs_8_), channel_id=1, source_target_pairs={{0,8},{4,12},{24,16},{28,20},{1,9},{5,13},{25,17},{29,21},{2,10},{... | collective-permute-start | bytes 6389768 | tf_op jit(solution)/shard_map/ppermute | solution.py:323
  160.4 49.8 %collective-permute-start.13 = (bf16[128,8320]{1,0:T(8,128)(2,1)}, bf16[128,8320]{1,0:T(8,128)(2,1)}, u32[]{:S(2)}, u32[]{:S(2)}) collective-permute-start(bf16[128,8320]{1,0:T(8,128)(2,1)} %collective-permute-done.2.refs_6_.refs_0_), channel_id=1, source_target_pairs={{0,2},{1,3},{2,0},{3,1},{4,6},{5,7},{6,4},{7,5},{8,10},{9,11},{10,... | collective-permute-start | bytes 6389768 | tf_op jit(solution)/shard_map/ppermute | solution.py:323
  196.9 56.8 %collective-permute-start.14 = (bf16[128,8320]{1,0:T(8,128)(2,1)}, bf16[128,8320]{1,0:T(8,128)(2,1)}, u32[]{:S(2)}, u32[]{:S(2)}) collective-permute-start(bf16[128,8320]{1,0:T(8,128)(2,1)} %collective-permute-done.3.refs_7_.refs_1_), channel_id=1, source_target_pairs={{0,2},{1,3},{2,0},{3,1},{4,6},{5,7},{6,4},{7,5},{8,10},{9,11},{10,... | collective-permute-start | bytes 6389768 | tf_op jit(solution)/shard_map/ppermute | solution.py:323
  202.6 116.2 %collective-permute-start.12 = (bf16[128,8320]{1,0:T(8,128)(2,1)}, bf16[128,8320]{1,0:T(8,128)(2,1)}, u32[]{:S(2)}, u32[]{:S(2)}) collective-permute-start(bf16[128,8320]{1,0:T(8,128)(2,1)} %copy-done.3), channel_id=1, source_target_pairs={{8,12},{12,8},{16,20},{20,16},{9,13},{13,9},{17,21},{21,17},{10,14... | collective-permute-start | bytes 6389768 | tf_op jit(solution)/shard_map/ppermute | solution.py:323
  204.8 116.1 %collective-permute-start.10 = (bf16[128,8320]{1,0:T(8,128)(2,1)}, bf16[128,8320]{1,0:T(8,128)(2,1)}, u32[]{:S(2)}, u32[]{:S(2)}) collective-permute-start(bf16[128,8320]{1,0:T(8,128)(2,1)} %copy-done.4), channel_id=1, source_target_pairs={{0,8},{4,12},{24,16},{28,20},{1,9},{5,13},{25,17},{29,21},{2,10},{... | collective-permute-start | bytes 6389768 | tf_op jit(solution)/shard_map/ppermute | solution.py:323
  210.2 112.7 %collective-permute-start.22 = (bf16[128,8320]{1,0:T(8,128)(2,1)}, bf16[128,8320]{1,0:T(8,128)(2,1)}, u32[]{:S(2)}, u32[]{:S(2)}) collective-permute-start(bf16[128,8320]{1,0:T(8,128)(2,1)} %collective-permute-done.3.refs_7_.refs_1_), channel_id=1, source_target_pairs={{8,16},{12,20},{16,8},{20,12},{9,17},{13,21},{17,9},{21,13},{10,18... | collective-permute-start | bytes 6389768 | tf_op jit(solution)/shard_map/ppermute | solution.py:323
  253.7 70.0 %collective-permute-start.25 = (bf16[128,8320]{1,0:T(8,128)(2,1)}, bf16[128,8320]{1,0:T(8,128)(2,1)}, u32[]{:S(2)}, u32[]{:S(2)}) collective-permute-start(bf16[128,8320]{1,0:T(8,128)(2,1)} %collective-permute-done.2.refs_6_.refs_0_), channel_id=1, source_target_pairs={{0,1},{1,0},{2,3},{3,2},{4,5},{5,4},{6,7},{7,6},{8,9},{9,8},{10,11... | collective-permute-start | bytes 6389768 | tf_op jit(solution)/shard_map/ppermute | solution.py:323
  255.2 68.7 %collective-permute-start.26 = (bf16[128,8320]{1,0:T(8,128)(2,1)}, bf16[128,8320]{1,0:T(8,128)(2,1)}, u32[]{:S(2)}, u32[]{:S(2)}) collective-permute-start(bf16[128,8320]{1,0:T(8,128)(2,1)} %collective-permute-done.3.refs_7_.refs_1_), channel_id=1, source_target_pairs={{0,1},{1,0},{2,3},{3,2},{4,5},{5,4},{6,7},{7,6},{8,9},{9,8},{10,11... | collective-permute-start | bytes 6389768 | tf_op jit(solution)/shard_map/ppermute | solution.py:323
  318.8 49.6 %collective-permute-start.24 = (bf16[128,8320]{1,0:T(8,128)(2,1)}, bf16[128,8320]{1,0:T(8,128)(2,1)S(1)}, u32[]{:S(2)}, u32[]{:S(2)}) collective-permute-start(bf16[128,8320]{1,0:T(8,128)(2,1)} %collective-permute-done.3.refs_7_.refs_1_), channel_id=1, source_target_pairs={{0,4},{4,0},{24,28},{28,24},{1,5},{5,1},{25,29},{29,25},{2,6},{6,2... | collective-permute-start | bytes 6389768 | tf_op jit(solution)/shard_map/ppermute | solution.py:323
  320.9 49.5 %collective-permute-start.21 = (bf16[128,8320]{1,0:T(8,128)(2,1)}, bf16[128,8320]{1,0:T(8,128)(2,1)}, u32[]{:S(2)}, u32[]{:S(2)}) collective-permute-start(bf16[128,8320]{1,0:T(8,128)(2,1)} %collective-permute-done.6.refs_10_), channel_id=1, source_target_pairs={{8,12},{12,8},{16,20},{20,16},{9,13},{13,9},{17,21},{21,17},{10,14... | collective-permute-start | bytes 6389768 | tf_op jit(solution)/shard_map/ppermute | solution.py:323
  322.9 49.5 %collective-permute-start.27 = (bf16[128,8320]{1,0:T(8,128)(2,1)}, bf16[128,8320]{1,0:T(8,128)(2,1)}, u32[]{:S(2)}, u32[]{:S(2)}) collective-permute-start(bf16[128,8320]{1,0:T(8,128)(2,1)} %collective-permute-done.13.refs_4_), channel_id=1, source_target_pairs={{0,1},{1,0},{2,3},{3,2},{4,5},{5,4},{6,7},{7,6},{8,9},{9,8},{10,11... | collective-permute-start | bytes 6389768 | tf_op jit(solution)/shard_map/ppermute | solution.py:323
  323.7 50.8 %collective-permute-start.28 = (bf16[128,8320]{1,0:T(8,128)(2,1)}, bf16[128,8320]{1,0:T(8,128)(2,1)}, u32[]{:S(2)}, u32[]{:S(2)}) collective-permute-start(bf16[128,8320]{1,0:T(8,128)(2,1)} %collective-permute-done.14.refs_5_), channel_id=1, source_target_pairs={{0,1},{1,0},{2,3},{3,2},{4,5},{5,4},{6,7},{7,6},{8,9},{9,8},{10,11... | collective-permute-start | bytes 6389768 | tf_op jit(solution)/shard_map/ppermute | solution.py:323
  323.8 71.3 %collective-permute-start.23 = (bf16[128,8320]{1,0:T(8,128)(2,1)}, bf16[128,8320]{1,0:T(8,128)(2,1)}, u32[]{:S(2)}, u32[]{:S(2)}) collective-permute-start(bf16[128,8320]{1,0:T(8,128)(2,1)} %copy-done.3), channel_id=1, source_target_pairs={{8,0},{12,4},{16,24},{20,28},{9,1},{13,5},{17,25},{21,29},{10,2},{... | collective-permute-start | bytes 6389768 | tf_op jit(solution)/shard_map/ppermute | solution.py:323
  368.4 55.3 %collective-permute-start.17 = (bf16[128,8320]{1,0:T(8,128)(2,1)}, bf16[128,8320]{1,0:T(8,128)(2,1)}, u32[]{:S(2)}, u32[]{:S(2)}) collective-permute-start(bf16[128,8320]{1,0:T(8,128)(2,1)} %copy-done), channel_id=1, source_target_pairs={{8,12},{12,8},{16,20},{20,16},{9,13},{13,9},{17,21},{21,17},{10,14... | collective-permute-start | bytes 6389768 | tf_op jit(solution)/shard_map/ppermute | solution.py:323
  370.4 53.3 %collective-permute-start.18 = (bf16[128,8320]{1,0:T(8,128)(2,1)}, bf16[128,8320]{1,0:T(8,128)(2,1)}, u32[]{:S(2)}, u32[]{:S(2)}) collective-permute-start(bf16[128,8320]{1,0:T(8,128)(2,1)} %collective-permute-done.10.refs_9_), channel_id=1, source_target_pairs={{8,16},{12,20},{16,8},{20,12},{9,17},{13,21},{17,9},{21,13},{10,18... | collective-permute-start | bytes 6389768 | tf_op jit(solution)/shard_map/ppermute | solution.py:323
  372.4 51.3 %collective-permute-start.19 = (bf16[128,8320]{1,0:T(8,128)(2,1)}, bf16[128,8320]{1,0:T(8,128)(2,1)}, u32[]{:S(2)}, u32[]{:S(2)}) collective-permute-start(bf16[128,8320]{1,0:T(8,128)(2,1)} %collective-permute-done.11.refs_8_.refs_9_.refs_10_), channel_id=1, source_target_pairs={{0,4},{4,0},{24,28},{28,24},{1,5},{5,1},{25,29},{29,25},{2,6},{6,2... | collective-permute-start | bytes 6389768 | tf_op jit(solution)/shard_map/ppermute | solution.py:323
  374.5 49.2 %collective-permute-start.20 = (bf16[128,8320]{1,0:T(8,128)(2,1)}, bf16[128,8320]{1,0:T(8,128)(2,1)}, u32[]{:S(2)}, u32[]{:S(2)}) collective-permute-start(bf16[128,8320]{1,0:T(8,128)(2,1)} %collective-permute-done.12.refs_5_), channel_id=1, source_target_pairs={{8,0},{12,4},{16,24},{20,28},{9,1},{13,5},{17,25},{21,29},{10,2},{... | collective-permute-start | bytes 6389768 | tf_op jit(solution)/shard_map/ppermute | solution.py:323
  395.1 70.0 %collective-permute-start.30 = (f32[4,8,128]{2,1,0:T(8,128)}, f32[4,8,128]{2,1,0:T(8,128)S(1)}, u32[]{:S(2)}, u32[]{:S(2)}) collective-permute-start(f32[4,8,128]{2,1,0:T(8,128)} %get-tuple-element.38), channel_id=1, source_target_pairs={{8,0},{12,4},{16,24},{20,28},{9,1},{13,5},{17,25},{21,29},{10,2},{... | collective-permute-start | bytes 49160 | tf_op jit(solution)/shard_map/ppermute | solution.py:323
  423.9 41.5 %collective-permute-start.29 = (f16[2,4,256,256]{3,2,1,0:T(8,128)(2,1)S(1)}, f16[2,4,256,256]{3,2,1,0:T(8,128)(2,1)S(1)}, u32[]{:S(2)}, u32[]{:S(2)}) collective-permute-start(f16[2,4,256,256]{3,2,1,0:T(8,128)(2,1)S(1)} %convert_element_type.12), channel_id=1, source_target_pairs={{8,0},{12,4},{16,24},{20,28},{9,1},{13,5},{17,25},{21,29},{10,2},{... | collective-permute-start | bytes 3145736 | tf_op jit(solution)/shard_map/ppermute | solution.py:323
  447.3 26.4 %collective-permute-start.31 = (f16[2,4,256,256]{3,2,1,0:T(8,128)(2,1)S(1)}, f16[2,4,256,256]{3,2,1,0:T(8,128)(2,1)}, u32[]{:S(2)}, u32[]{:S(2)}) collective-permute-start(f16[2,4,256,256]{3,2,1,0:T(8,128)(2,1)S(1)} %convert_element_type.14), channel_id=1, source_target_pairs={{8,0},{12,4},{16,24},{20,28},{9,1},{13,5},{17,25},{21,29},{10,2},{... | collective-permute-start | bytes 3145736 | tf_op jit(solution)/shard_map/ppermute | solution.py:323
  (6 other events, 285.0 us)

commit v5 on v4

--- a/solution.py
+++ b/solution.py
@@ -19,6 +19,16 @@
     while tile * 2 <= most and size % (tile * 2) == 0:
         tile *= 2
     return tile
+
+
+def passed_body(value_ref, out_ref):
+    out_ref[...] = value_ref[...]
+
+
+def passed(number):
+    block = jnp.broadcast_to(number, (8, LANES)).astype(jnp.int32)
+    out = pl.pallas_call(passed_body, out_shape=jax.ShapeDtypeStruct(block.shape, jnp.int32))(block)
+    return out[0, 0]
 
 
 def tied(*values):
@@ -208,7 +218,8 @@
             bound = jnp.max(row_factor / row_norm, axis=0, keepdims=True)
             bound = bound * jnp.max(col_factor / col_norm, axis=1, keepdims=True)
             unit_size = jnp.maximum(bound * (2 * half_width * scale_coef), FLOOR) / 32768
-            outs[1][row] = jnp.broadcast_to(unit_size, outs[1].shape[1:])
+            group = plan_ref[4 * units + part * at_once + row]
+            outs[1][group] = jnp.broadcast_to(unit_size, outs[1].shape[1:])
             scaling = scaling * (1 / unit_size)
         staged[slot, 0, row] = product[top : top + shard_rows, :cols] * scaling
         staged[slot, 1, row] = product[top : top + shard_rows, cols:] * scaling
@@ -244,7 +255,7 @@
     if raw:
         out_shape.append(jax.ShapeDtypeStruct((count, 8, LANES), jnp.float32))
         out_specs.append(
-            pl.BlockSpec((at_once, 8, LANES), lambda i, j, s: (s[4 * units + j], 0, 0))
+            pl.BlockSpec((count, 8, LANES), lambda i, j, s: (0, 0, 0))
         )
     shapes = [[piece.shape[0] for piece in pieces] for pieces in rows]
     most = max(len(pieces) for pieces in rows)
@@ -318,9 +329,12 @@
     is_end = jnp.logical_or(me // 2 == 0, me // 2 == blocks // 2 - 1)
 
     def moved(value, axis, route):
-        if isinstance(value, tuple):
-            return tuple(moved(piece, axis, route) for piece in value)
-        return lax.ppermute(value, axis, route)
+        if not isinstance(value, tuple):
+            return lax.ppermute(value, axis, route)
+        pieces = []
+        for piece in value:
+            pieces.append(lax.ppermute(piece, axis, route))
+        return tuple(pieces)
 
     def swap(value, among, by):
         return moved(value, "blk", [(b, b ^ by) for b in among])
@@ -344,7 +358,7 @@
     def either(inner_value, end_value):
         return jnp.where(is_end, end_value, inner_value)
 
-    def put(out, columns, units):
+    def put(out, columns, units, me=me):
         halves = [half for column in columns for half in column]
         choice, slots = [], []
         for inner_half, end_half in units:
@@ -374,25 +388,27 @@
     near_beside = swap(near, ends, 1)
     client = begun(near)
 
+    marked = passed(me)
     out = put(
         None,
         [own, near, beside, across],
         both(0, 0, 0, 0) + both(1, 2, 1, 2) + both(2, 1, 2, 1) + both(3, 6, 0, 5),
+        marked,
     )
+    *held, first_out = tied(far_end[0], far_inner[0], client[last][0], out)
+    low = swap(held[0], inner, 1)
+    low_beside = swap(held[1], ends, 1)
+    firsts = finished({0: near[0], last: held[2]})
     out = put(
-        out,
+        first_out,
         [far_end[:1] * 2, end_beside[:1] * 2, far_inner[:1] * 2, near_beside[:1] * 2],
         [((0, 0, 4), (2, 0, 4)), ((1, 0, 3), (3, 0, 3))],
     )
-    *held, out = tied(
-        far_end[0], end_beside[1], far_inner[0], across_beside[1], *client[last], out
-    )
-    client[last] = tuple(held[4:])
-    low = swap(held[0], inner, 1)
-    high = swap(held[1], inner, 6)
-    low_beside = swap(held[2], ends, 1)
-    high_beside = swap(held[3], inner, 2)
-    client = finished(client)
+    *held, out = tied(end_beside[1], across_beside[1], client[last][1], out)
+    high = swap(held[0], inner, 6)
+    high_beside = swap(held[1], inner, 2)
+    seconds = finished({0: near[1], last: held[2]})
+    client = list(zip(firsts, seconds))
 
     def serve(columns):
         zero = me * 0

time: 482 us -> 439 us (0.911)
  waiting for transfers between devices: 261 us -> 215 us
    ppermute x33 -> x15, waiting for transfers between devices: 261 us -> 5.26 us  [moved(): return lax.ppermute(value, axis, route)]
    ppermute x0 -> x18, waiting for transfers between devices: none -> 210 us  [moved(): pieces.append(lax.ppermute(piece, axis, route))]
    ppermute x33 -> x15, starting transfers between devices: 50.4 us -> 18.1 us  [moved(): return lax.ppermute(value, axis, route)]
    ppermute x0 -> x18, starting transfers between devices: none -> 28.1 us  [moved(): pieces.append(lax.ppermute(piece, axis, route))]
  transfers between devices with their start and end apart: 33 -> 33, of which waited for: 9 -> 7; matrix products, arithmetic and copies ran while one was open for 2% -> 2% of each run, Pallas kernels for 30% -> 34%
where the time goes in v5:
time: 439 us; the launch traced here: 433 us
  waiting for transfers between devices  215 us (49%)
  Pallas kernels  153 us (35%)
  starting transfers between devices  46.3 us (11%)
  other arithmetic  8.66 us (2%)
  local copies, waits for them, and re-layouts  6.73 us (2%)
    ppermute x18, waiting for transfers between devices, moved(): pieces.append(lax.ppermute(piece, axis, route))  210 us
    pallas_call x6, Pallas kernels, products(): pl.pallas_call(functools.partial(products_body, (shapes, at_once, len(col...  145 us
    ppermute x18, starting transfers between devices, moved(): pieces.append(lax.ppermute(piece, axis, route))  28.1 us
    ppermute x15, starting transfers between devices, moved(): return lax.ppermute(value, axis, route)  18.1 us
  transfers between devices with their start and end apart: 33, of which 7 were waited for; matrix products, arithmetic and copies ran while one was open for 2% of the time, Pallas kernels for 34%

profile of v5, /device:TPU:31, one launch (start us, length us, event | category | flops | bytes accessed | tf_op | source)
XLA Modules:
  0.0 433.3 jit_solution(5589254678379191794)
XLA Ops:
  0.0 1.5 copy.6.flags_ref
  1.5 6.9 %shard_map.28 = (bf16[256,8320]{1,0:T(8,128)(2,1)}, bf16[128,8320]{1,0:T(8,128)(2,1)}, bf16[128,8320]{1,0:T(8,128)(2,1)}) custom-call(bf16[256,2,16,256]{3,2,1,0:T(8,128)(2,1)} %bitcast.34, s32[256,1]{1,0:T(8,128)} %copy.6.flags_ref), custom_call_target="tpu_custom_call" | custom-call | tf_op jit(solution)/shard_map/pallas_call | solution.py:85
  9.8 2.0 collective-permute-start.6
  12.8 43.0 %collective-permute-done.2.refs_6_.refs_0_ = bf16[128,8320]{1,0:T(8,128)(2,1)} collective-permute-done((bf16[128,8320]{1,0:T(8,128)(2,1)}, bf16[128,8320]{1,0:T(8,128)(2,1)}, u32[]{:S(2)}, u32[]{:S(2)}) %collective-permute-start.2) | collective-permute-done | bytes 2129952 | tf_op jit(solution)/shard_map/ppermute | solution.py:336
  56.1 45.4 %collective-permute-done.3.refs_7_.refs_1_ = bf16[128,8320]{1,0:T(8,128)(2,1)} collective-permute-done((bf16[128,8320]{1,0:T(8,128)(2,1)}, bf16[128,8320]{1,0:T(8,128)(2,1)}, u32[]{:S(2)}, u32[]{:S(2)}) %collective-permute-start.3) | collective-permute-done | bytes 2129952 | tf_op jit(solution)/shard_map/ppermute | solution.py:336
  101.5 1.5 collective-permute-start
  104.4 46.8 %collective-permute-done.5.refs_9_ = bf16[128,8320]{1,0:T(8,128)(2,1)S(1)} collective-permute-done((bf16[128,8320]{1,0:T(8,128)(2,1)}, bf16[128,8320]{1,0:T(8,128)(2,1)S(1)}, u32[]{:S(2)}, u32[]{:S(2)}) %collective-permute-start.5) | collective-permute-done | bytes 2129952 | tf_op jit(solution)/shard_map/ppermute | solution.py:336
  153.3 2.1 collective-permute-start.17
  155.5 6.5 %collective-permute-start.16 = (bf16[128,8320]{1,0:T(8,128)(2,1)}, bf16[128,8320]{1,0:T(8,128)(2,1)}, u32[]{:S(2)}, u32[]{:S(2)}) collective-permute-start(bf16[128,8320]{1,0:T(8,128)(2,1)} %collective-permute-done.4.refs_8_), channel_id=1, source_target_pairs={{0,8},{4,12},{24,16},{28,20},{1,9},{5,13},{25,17},{29,21},{2,10},{... | collective-permute-start | bytes 6389768 | tf_op jit(solution)/shard_map/ppermute | solution.py:336
  169.5 32.6 %collective-permute-done.10.refs_8_.refs_9_.refs_10_ = bf16[128,8320]{1,0:T(8,128)(2,1)} collective-permute-done((bf16[128,8320]{1,0:T(8,128)(2,1)}, bf16[128,8320]{1,0:T(8,128)(2,1)}, u32[]{:S(2)}, u32[]{:S(2)}) %collective-permute-start.10) | collective-permute-done | bytes 2129952 | tf_op jit(solution)/shard_map/ppermute | solution.py:336
  202.1 2.0 collective-permute-start.14
  204.1 2.7 collective-permute-start.13
  206.7 2.0 collective-permute-start.22
  209.6 1.4 collective-permute-start.25
  211.0 47.3 %shard_map.30.refs_12_ = f32[2,4,256,2048]{3,2,1,0:T(8,128)} custom-call(s32[20]{0:T(128)} %stack.151.plan_ref, bf16[256,8320]{1,0:T(8,128)(2,1)} %get-tuple-element.28.refs_0_, bf16[256,8320]{1,0:T(8,128)(2,1)} %collective-permute-done.refs_1_, bf16[256,8320]{1,0:T(8,128)(2,1)} %collective-permute-done.1.refs_2_, ...), custom_call_target="tpu_custom_call" | custom-call | flops 34359738368 | bytes 83886080 | tf_op jit(solution)/shard_map/pallas_call | solution.py:262
  258.4 16.3 %shard_map.31.refs_14_ = f32[2,4,256,2048]{3,2,1,0:T(8,128)} custom-call(s32[8]{0:T(128)} %stack.156.plan_ref, bf16[256,8320]{1,0:T(8,128)(2,1)} %get-tuple-element.28.refs_0_, bf16[256,8320]{1,0:T(8,128)(2,1)} %collective-permute-done.refs_1_, bf16[256,8320]{1,0:T(8,128)(2,1)} %collective-permute-done.1.refs_2_, ...), custom_call_target="tpu_custom_call", output_to_operand_aliasing={{}: (13, {})} | custom-call | flops 8589934592 | bytes 20971520 | tf_op jit(solution)/shard_map/pallas_call | solution.py:262
  274.7 2.3 collective-permute-start.24
  277.0 2.0 collective-permute-start.21
  283.0 41.3 %collective-permute-done.24.refs_13_ = bf16[128,8320]{1,0:T(8,128)(2,1)S(1)} collective-permute-done((bf16[128,8320]{1,0:T(8,128)(2,1)}, bf16[128,8320]{1,0:T(8,128)(2,1)S(1)}, u32[]{:S(2)}, u32[]{:S(2)}) %collective-permute-start.24) | collective-permute-done | bytes 2129952 | tf_op jit(solution)/shard_map/ppermute | solution.py:336
  324.3 2.0 collective-permute-start.18
  327.6 2.0 collective-permute-start.12
  329.6 2.6 collective-permute-start.19
  332.1 19.0 %shard_map.32 = (f32[2,4,256,256]{3,2,1,0:T(8,128)}, f32[4,8,128]{2,1,0:T(8,128)}) custom-call(s32[8]{0:T(128)} %stack.166.plan_ref, bf16[128,8320]{1,0:T(8,128)(2,1)} %collective-permute-done.2.refs_6_.refs_0_, bf16[128,8320]{1,0:T(8,128)(2,1)} %collective-permute-done.3.refs_7_.refs_1_, bf16[128,8320]{1,0:T(8,128)(2,1)} %collective-permute-done.25.refs_2_, ...), custom_call_target="tpu_custom_call" | custom-call | flops 8589934592 | bytes 20971520 | tf_op jit(solution)/shard_map/pallas_call | solution.py:262
  351.2 1.4 collective-permute-start.30
  352.6 27.1 %shard_map.33.refs_8_ = f32[2,4,256,2048]{3,2,1,0:T(8,128)} custom-call(s32[12]{0:T(128)} %stack.165.plan_ref, bf16[256,8320]{1,0:T(8,128)(2,1)} %get-tuple-element.28.refs_0_, bf16[256,8320]{1,0:T(8,128)(2,1)} %collective-permute-done.refs_1_, bf16[256,8320]{1,0:T(8,128)(2,1)} %collective-permute-done.1.refs_2_, ...), custom_call_target="tpu_custom_call", output_to_operand_aliasing={{}: (15, {})} | custom-call | flops 17179869184 | bytes 41943040 | tf_op jit(solution)/shard_map/pallas_call | solution.py:262
  381.3 19.0 %shard_map.34 = (f32[2,4,256,256]{3,2,1,0:T(8,128)}, f32[4,8,128]{2,1,0:T(8,128)}) custom-call(s32[8]{0:T(128)} %stack.166.plan_ref, bf16[128,8320]{1,0:T(8,128)(2,1)} %collective-permute-done.2.refs_6_.refs_0_, bf16[128,8320]{1,0:T(8,128)(2,1)} %collective-permute-done.3.refs_7_.refs_1_, bf16[128,8320]{1,0:T(8,128)(2,1)} %collective-permute-done.25.refs_2_, ...), custom_call_target="tpu_custom_call" | custom-call | flops 8589934592 | bytes 20971520 | tf_op jit(solution)/shard_map/pallas_call | solution.py:262
  401.6 1.8 convert_element_type.14
  403.4 1.5 collective-permute-start.31
  404.9 16.3 %shard_map.35 = f32[2,4,256,2048]{3,2,1,0:T(8,128)} custom-call(s32[8]{0:T(128)} %stack.140.plan_ref, bf16[256,8320]{1,0:T(8,128)(2,1)} %get-tuple-element.28.refs_0_, bf16[256,8320]{1,0:T(8,128)(2,1)} %collective-permute-done.refs_1_, bf16[256,8320]{1,0:T(8,128)(2,1)} %collective-permute-done.1.refs_2_, ...), custom_call_target="tpu_custom_call", output_to_operand_aliasing={{}: (9, {})} | custom-call | flops 8589934592 | bytes 20971520 | tf_op jit(solution)/shard_map/pallas_call | solution.py:262
  421.4 3.2 select_dynamic-update-slice_fusion.1
  424.6 5.2 %collective-permute-done.31 = f16[2,4,256,256]{3,2,1,0:T(8,128)(2,1)} collective-permute-done((f16[2,4,256,256]{3,2,1,0:T(8,128)(2,1)S(1)}, f16[2,4,256,256]{3,2,1,0:T(8,128)(2,1)}, u32[]{:S(2)}, u32[]{:S(2)}) %collective-permute-start.31) | collective-permute-done | bytes 1048608 | tf_op jit(solution)/shard_map/ppermute | solution.py:333
  429.8 3.5 select_dynamic-update-slice_fusion
  (66 shorter events, 20.0 us)
Async XLA Ops:
  8.3 47.5 %collective-permute-start.2 = (bf16[128,8320]{1,0:T(8,128)(2,1)}, bf16[128,8320]{1,0:T(8,128)(2,1)}, u32[]{:S(2)}, u32[]{:S(2)}) collective-permute-start(bf16[128,8320]{1,0:T(8,128)(2,1)} %get-tuple-element.29.refs_4_), channel_id=1, source_target_pairs={{0,8},{4,12},{8,0},{12,4},{16,24},{20,28},{24,16},{28,20},{1,9},{5... | collective-permute-start | bytes 6389768 | tf_op jit(solution)/shard_map/ppermute | solution.py:336
  8.5 93.0 %collective-permute-start.3 = (bf16[128,8320]{1,0:T(8,128)(2,1)}, bf16[128,8320]{1,0:T(8,128)(2,1)}, u32[]{:S(2)}, u32[]{:S(2)}) collective-permute-start(bf16[128,8320]{1,0:T(8,128)(2,1)} %get-tuple-element.30.refs_5_), channel_id=1, source_target_pairs={{0,8},{4,12},{8,0},{12,4},{16,24},{20,28},{24,16},{28,20},{1,9},{5... | collective-permute-start | bytes 6389768 | tf_op jit(solution)/shard_map/ppermute | solution.py:336
  9.8 93.2 %collective-permute-start.6 = (bf16[128,8320]{1,0:T(8,128)(2,1)}, bf16[128,8320]{1,0:T(8,128)(2,1)}, u32[]{:S(2)}, u32[]{:S(2)}) collective-permute-start(bf16[128,8320]{1,0:T(8,128)(2,1)} %get-tuple-element.29.refs_4_), channel_id=1, source_target_pairs={{8,16},{12,20},{16,8},{20,12},{9,17},{13,21},{17,9},{21,13},{10,18... | collective-permute-start | bytes 6389768 | tf_op jit(solution)/shard_map/ppermute | solution.py:336
  11.8 139.5 %collective-permute-start.1 = (bf16[256,8320]{1,0:T(8,128)(2,1)}, bf16[256,8320]{1,0:T(8,128)(2,1)}, u32[]{:S(2)}, u32[]{:S(2)}) collective-permute-start(bf16[256,8320]{1,0:T(8,128)(2,1)} %get-tuple-element.28.refs_0_), channel_id=1, source_target_pairs={{0,2},{1,3},{2,0},{3,1},{4,6},{5,7},{6,4},{7,5},{8,10},{9,11},{10,... | collective-permute-start | bytes 12779528 | tf_op jit(solution)/shard_map/ppermute | solution.py:333
  12.0 91.2 %collective-permute-start.7 = (bf16[128,8320]{1,0:T(8,128)(2,1)}, bf16[128,8320]{1,0:T(8,128)(2,1)S(1)}, u32[]{:S(2)}, u32[]{:S(2)}) collective-permute-start(bf16[128,8320]{1,0:T(8,128)(2,1)} %get-tuple-element.30.refs_5_), channel_id=1, source_target_pairs={{8,16},{12,20},{16,8},{20,12},{9,17},{13,21},{17,9},{21,13},{10,18... | collective-permute-start | bytes 6389768 | tf_op jit(solution)/shard_map/ppermute | solution.py:336
  55.9 48.2 %collective-permute-start.4 = (bf16[128,8320]{1,0:T(8,128)(2,1)}, bf16[128,8320]{1,0:T(8,128)(2,1)}, u32[]{:S(2)}, u32[]{:S(2)}) collective-permute-start(bf16[128,8320]{1,0:T(8,128)(2,1)} %get-tuple-element.29.refs_4_), channel_id=1, source_target_pairs={{0,4},{4,0},{8,12},{12,8},{16,20},{20,16},{24,28},{28,24},{1,5},{5... | collective-permute-start | bytes 6389768 | tf_op jit(solution)/shard_map/ppermute | solution.py:336
  101.5 51.8 %collective-permute-start = (bf16[256,8320]{1,0:T(8,128)(2,1)}, bf16[256,8320]{1,0:T(8,128)(2,1)}, u32[]{:S(2)}, u32[]{:S(2)}) collective-permute-start(bf16[256,8320]{1,0:T(8,128)(2,1)} %get-tuple-element.28.refs_0_), channel_id=1, source_target_pairs={{0,1},{1,0},{2,3},{3,2},{4,5},{5,4},{6,7},{7,6},{8,9},{9,8},{10,11... | collective-permute-start | bytes 12779528 | tf_op jit(solution)/shard_map/ppermute | solution.py:333
  103.1 48.2 %collective-permute-start.5 = (bf16[128,8320]{1,0:T(8,128)(2,1)}, bf16[128,8320]{1,0:T(8,128)(2,1)S(1)}, u32[]{:S(2)}, u32[]{:S(2)}) collective-permute-start(bf16[128,8320]{1,0:T(8,128)(2,1)} %get-tuple-element.30.refs_5_), channel_id=1, source_target_pairs={{0,4},{4,0},{8,12},{12,8},{16,20},{20,16},{24,28},{28,24},{1,5},{5... | collective-permute-start | bytes 6389768 | tf_op jit(solution)/shard_map/ppermute | solution.py:336
  103.3 52.2 %collective-permute-start.9 = (bf16[128,8320]{1,0:T(8,128)(2,1)}, bf16[128,8320]{1,0:T(8,128)(2,1)S(1)}, u32[]{:S(2)}, u32[]{:S(2)}) collective-permute-start(bf16[128,8320]{1,0:T(8,128)(2,1)} %collective-permute-done.2.refs_6_.refs_0_), channel_id=1, source_target_pairs={{8,16},{12,20},{16,8},{20,12},{9,17},{13,21},{17,9},{21,13},{10,18... | collective-permute-start | bytes 6389768 | tf_op jit(solution)/shard_map/ppermute | solution.py:336
  104.1 57.9 %collective-permute-start.11 = (bf16[128,8320]{1,0:T(8,128)(2,1)}, bf16[128,8320]{1,0:T(8,128)(2,1)}, u32[]{:S(2)}, u32[]{:S(2)}) collective-permute-start(bf16[128,8320]{1,0:T(8,128)(2,1)} %collective-permute-done.2.refs_6_.refs_0_), channel_id=1, source_target_pairs={{0,2},{1,3},{2,0},{3,1},{4,6},{5,7},{6,4},{7,5},{8,10},{9,11},{10,... | collective-permute-start | bytes 6389768 | tf_op jit(solution)/shard_map/ppermute | solution.py:336
  151.3 59.8 %collective-permute-start.8 = (bf16[256,8320]{1,0:T(8,128)(2,1)}, bf16[256,8320]{1,0:T(8,128)(2,1)}, u32[]{:S(2)}, u32[]{:S(2)}) collective-permute-start(bf16[256,8320]{1,0:T(8,128)(2,1)} %collective-permute-done.1.refs_2_), channel_id=1, source_target_pairs={{0,1},{1,0},{2,3},{3,2},{4,5},{5,4},{6,7},{7,6},{8,9},{9,8},{10,11... | collective-permute-start | bytes 12779528 | tf_op jit(solution)/shard_map/ppermute | solution.py:333
  152.0 50.1 %collective-permute-start.10 = (bf16[128,8320]{1,0:T(8,128)(2,1)}, bf16[128,8320]{1,0:T(8,128)(2,1)}, u32[]{:S(2)}, u32[]{:S(2)}) collective-permute-start(bf16[128,8320]{1,0:T(8,128)(2,1)} %collective-permute-done.6.refs_10_), channel_id=1, source_target_pairs={{8,0},{12,4},{16,24},{20,28},{9,1},{13,5},{17,25},{21,29},{10,2},{... | collective-permute-start | bytes 6389768 | tf_op jit(solution)/shard_map/ppermute | solution.py:336
  153.3 50.8 %collective-permute-start.17 = (bf16[128,8320]{1,0:T(8,128)(2,1)}, bf16[128,8320]{1,0:T(8,128)(2,1)}, u32[]{:S(2)}, u32[]{:S(2)}) collective-permute-start(bf16[128,8320]{1,0:T(8,128)(2,1)} %collective-permute-done.2.refs_6_.refs_0_), channel_id=1, source_target_pairs={{0,4},{4,0},{24,28},{28,24},{1,5},{5,1},{25,29},{29,25},{2,6},{6,2... | collective-permute-start | bytes 6389768 | tf_op jit(solution)/shard_map/ppermute | solution.py:336
  155.5 51.2 %collective-permute-start.16 = (bf16[128,8320]{1,0:T(8,128)(2,1)}, bf16[128,8320]{1,0:T(8,128)(2,1)}, u32[]{:S(2)}, u32[]{:S(2)}) collective-permute-start(bf16[128,8320]{1,0:T(8,128)(2,1)} %collective-permute-done.4.refs_8_), channel_id=1, source_target_pairs={{0,8},{4,12},{24,16},{28,20},{1,9},{5,13},{25,17},{29,21},{2,10},{... | collective-permute-start | bytes 6389768 | tf_op jit(solution)/shard_map/ppermute | solution.py:336
  162.0 47.6 %collective-permute-start.15 = (bf16[128,8320]{1,0:T(8,128)(2,1)}, bf16[128,8320]{1,0:T(8,128)(2,1)}, u32[]{:S(2)}, u32[]{:S(2)}) collective-permute-start(bf16[128,8320]{1,0:T(8,128)(2,1)} %collective-permute-done.3.refs_7_.refs_1_), channel_id=1, source_target_pairs={{0,2},{1,3},{2,0},{3,1},{4,6},{5,7},{6,4},{7,5},{8,10},{9,11},{10,... | collective-permute-start | bytes 6389768 | tf_op jit(solution)/shard_map/ppermute | solution.py:336
  202.1 72.6 %collective-permute-start.14 = (bf16[128,8320]{1,0:T(8,128)(2,1)}, bf16[128,8320]{1,0:T(8,128)(2,1)}, u32[]{:S(2)}, u32[]{:S(2)}) collective-permute-start(bf16[128,8320]{1,0:T(8,128)(2,1)} %copy-done.3), channel_id=1, source_target_pairs={{8,12},{12,8},{16,20},{20,16},{9,13},{13,9},{17,21},{21,17},{10,14... | collective-permute-start | bytes 6389768 | tf_op jit(solution)/shard_map/ppermute | solution.py:336
  204.1 72.9 %collective-permute-start.13 = (bf16[128,8320]{1,0:T(8,128)(2,1)}, bf16[128,8320]{1,0:T(8,128)(2,1)}, u32[]{:S(2)}, u32[]{:S(2)}) collective-permute-start(bf16[128,8320]{1,0:T(8,128)(2,1)} %copy-done.4), channel_id=1, source_target_pairs={{0,8},{4,12},{24,16},{28,20},{1,9},{5,13},{25,17},{29,21},{2,10},{... | collective-permute-start | bytes 6389768 | tf_op jit(solution)/shard_map/ppermute | solution.py:336
  206.7 72.3 %collective-permute-start.22 = (bf16[128,8320]{1,0:T(8,128)(2,1)}, bf16[128,8320]{1,0:T(8,128)(2,1)}, u32[]{:S(2)}, u32[]{:S(2)}) collective-permute-start(bf16[128,8320]{1,0:T(8,128)(2,1)} %collective-permute-done.3.refs_7_.refs_1_), channel_id=1, source_target_pairs={{8,16},{12,20},{16,8},{20,12},{9,17},{13,21},{17,9},{21,13},{10,18... | collective-permute-start | bytes 6389768 | tf_op jit(solution)/shard_map/ppermute | solution.py:336
  209.6 70.1 %collective-permute-start.25 = (bf16[128,8320]{1,0:T(8,128)(2,1)}, bf16[128,8320]{1,0:T(8,128)(2,1)}, u32[]{:S(2)}, u32[]{:S(2)}) collective-permute-start(bf16[128,8320]{1,0:T(8,128)(2,1)} %collective-permute-done.2.refs_6_.refs_0_), channel_id=1, source_target_pairs={{0,1},{1,0},{2,3},{3,2},{4,5},{5,4},{6,7},{7,6},{8,9},{9,8},{10,11... | collective-permute-start | bytes 6389768 | tf_op jit(solution)/shard_map/ppermute | solution.py:333
  211.0 68.8 %collective-permute-start.26 = (bf16[128,8320]{1,0:T(8,128)(2,1)}, bf16[128,8320]{1,0:T(8,128)(2,1)}, u32[]{:S(2)}, u32[]{:S(2)}) collective-permute-start(bf16[128,8320]{1,0:T(8,128)(2,1)} %collective-permute-done.3.refs_7_.refs_1_), channel_id=1, source_target_pairs={{0,1},{1,0},{2,3},{3,2},{4,5},{5,4},{6,7},{7,6},{8,9},{9,8},{10,11... | collective-permute-start | bytes 6389768 | tf_op jit(solution)/shard_map/ppermute | solution.py:333
  274.7 49.6 %collective-permute-start.24 = (bf16[128,8320]{1,0:T(8,128)(2,1)}, bf16[128,8320]{1,0:T(8,128)(2,1)S(1)}, u32[]{:S(2)}, u32[]{:S(2)}) collective-permute-start(bf16[128,8320]{1,0:T(8,128)(2,1)} %collective-permute-done.3.refs_7_.refs_1_), channel_id=1, source_target_pairs={{0,4},{4,0},{24,28},{28,24},{1,5},{5,1},{25,29},{29,25},{2,6},{6,2... | collective-permute-start | bytes 6389768 | tf_op jit(solution)/shard_map/ppermute | solution.py:336
  277.0 49.3 %collective-permute-start.21 = (bf16[128,8320]{1,0:T(8,128)(2,1)}, bf16[128,8320]{1,0:T(8,128)(2,1)}, u32[]{:S(2)}, u32[]{:S(2)}) collective-permute-start(bf16[128,8320]{1,0:T(8,128)(2,1)} %collective-permute-done.6.refs_10_), channel_id=1, source_target_pairs={{8,12},{12,8},{16,20},{20,16},{9,13},{13,9},{17,21},{21,17},{10,14... | collective-permute-start | bytes 6389768 | tf_op jit(solution)/shard_map/ppermute | solution.py:336
  279.0 48.6 %collective-permute-start.28 = (bf16[128,8320]{1,0:T(8,128)(2,1)}, bf16[128,8320]{1,0:T(8,128)(2,1)}, u32[]{:S(2)}, u32[]{:S(2)}) collective-permute-start(bf16[128,8320]{1,0:T(8,128)(2,1)} %collective-permute-done.15.refs_5_), channel_id=1, source_target_pairs={{0,1},{1,0},{2,3},{3,2},{4,5},{5,4},{6,7},{7,6},{8,9},{9,8},{10,11... | collective-permute-start | bytes 6389768 | tf_op jit(solution)/shard_map/ppermute | solution.py:333
  279.7 49.8 %collective-permute-start.27 = (bf16[128,8320]{1,0:T(8,128)(2,1)}, bf16[128,8320]{1,0:T(8,128)(2,1)}, u32[]{:S(2)}, u32[]{:S(2)}) collective-permute-start(bf16[128,8320]{1,0:T(8,128)(2,1)} %collective-permute-done.11.refs_4_), channel_id=1, source_target_pairs={{0,1},{1,0},{2,3},{3,2},{4,5},{5,4},{6,7},{7,6},{8,9},{9,8},{10,11... | collective-permute-start | bytes 6389768 | tf_op jit(solution)/shard_map/ppermute | solution.py:333
  279.8 71.4 %collective-permute-start.23 = (bf16[128,8320]{1,0:T(8,128)(2,1)}, bf16[128,8320]{1,0:T(8,128)(2,1)}, u32[]{:S(2)}, u32[]{:S(2)}) collective-permute-start(bf16[128,8320]{1,0:T(8,128)(2,1)} %copy-done.3), channel_id=1, source_target_pairs={{8,0},{12,4},{16,24},{20,28},{9,1},{13,5},{17,25},{21,29},{10,2},{... | collective-permute-start | bytes 6389768 | tf_op jit(solution)/shard_map/ppermute | solution.py:336
  324.3 55.5 %collective-permute-start.18 = (bf16[128,8320]{1,0:T(8,128)(2,1)}, bf16[128,8320]{1,0:T(8,128)(2,1)}, u32[]{:S(2)}, u32[]{:S(2)}) collective-permute-start(bf16[128,8320]{1,0:T(8,128)(2,1)} %collective-permute-done.13.refs_9_), channel_id=1, source_target_pairs={{8,16},{12,20},{16,8},{20,12},{9,17},{13,21},{17,9},{21,13},{10,18... | collective-permute-start | bytes 6389768 | tf_op jit(solution)/shard_map/ppermute | solution.py:333
  326.3 53.5 %collective-permute-start.20 = (bf16[128,8320]{1,0:T(8,128)(2,1)}, bf16[128,8320]{1,0:T(8,128)(2,1)}, u32[]{:S(2)}, u32[]{:S(2)}) collective-permute-start(bf16[128,8320]{1,0:T(8,128)(2,1)} %collective-permute-done.14.refs_5_), channel_id=1, source_target_pairs={{8,0},{12,4},{16,24},{20,28},{9,1},{13,5},{17,25},{21,29},{10,2},{... | collective-permute-start | bytes 6389768 | tf_op jit(solution)/shard_map/ppermute | solution.py:333
  327.6 52.2 %collective-permute-start.12 = (bf16[128,8320]{1,0:T(8,128)(2,1)}, bf16[128,8320]{1,0:T(8,128)(2,1)}, u32[]{:S(2)}, u32[]{:S(2)}) collective-permute-start(bf16[128,8320]{1,0:T(8,128)(2,1)} %copy-done), channel_id=1, source_target_pairs={{8,12},{12,8},{16,20},{20,16},{9,13},{13,9},{17,21},{21,17},{10,14... | collective-permute-start | bytes 6389768 | tf_op jit(solution)/shard_map/ppermute | solution.py:333
  329.6 50.2 %collective-permute-start.19 = (bf16[128,8320]{1,0:T(8,128)(2,1)}, bf16[128,8320]{1,0:T(8,128)(2,1)}, u32[]{:S(2)}, u32[]{:S(2)}) collective-permute-start(bf16[128,8320]{1,0:T(8,128)(2,1)} %collective-permute-done.10.refs_8_.refs_9_.refs_10_), channel_id=1, source_target_pairs={{0,4},{4,0},{24,28},{28,24},{1,5},{5,1},{25,29},{29,25},{2,6},{6,2... | collective-permute-start | bytes 6389768 | tf_op jit(solution)/shard_map/ppermute | solution.py:333
  351.2 69.9 %collective-permute-start.30 = (f32[4,8,128]{2,1,0:T(8,128)}, f32[4,8,128]{2,1,0:T(8,128)S(1)}, u32[]{:S(2)}, u32[]{:S(2)}) collective-permute-start(f32[4,8,128]{2,1,0:T(8,128)} %get-tuple-element.40), channel_id=1, source_target_pairs={{8,0},{12,4},{16,24},{20,28},{9,1},{13,5},{17,25},{21,29},{10,2},{... | collective-permute-start | bytes 49160 | tf_op jit(solution)/shard_map/ppermute | solution.py:333
  380.0 41.4 %collective-permute-start.29 = (f16[2,4,256,256]{3,2,1,0:T(8,128)(2,1)S(1)}, f16[2,4,256,256]{3,2,1,0:T(8,128)(2,1)S(1)}, u32[]{:S(2)}, u32[]{:S(2)}) collective-permute-start(f16[2,4,256,256]{3,2,1,0:T(8,128)(2,1)S(1)} %convert_element_type.12), channel_id=1, source_target_pairs={{8,0},{12,4},{16,24},{20,28},{9,1},{13,5},{17,25},{21,29},{10,2},{... | collective-permute-start | bytes 3145736 | tf_op jit(solution)/shard_map/ppermute | solution.py:333
  403.4 26.5 %collective-permute-start.31 = (f16[2,4,256,256]{3,2,1,0:T(8,128)(2,1)S(1)}, f16[2,4,256,256]{3,2,1,0:T(8,128)(2,1)}, u32[]{:S(2)}, u32[]{:S(2)}) collective-permute-start(f16[2,4,256,256]{3,2,1,0:T(8,128)(2,1)S(1)} %convert_element_type.14), channel_id=1, source_target_pairs={{8,0},{12,4},{16,24},{20,28},{9,1},{13,5},{17,25},{21,29},{10,2},{... | collective-permute-start | bytes 3145736 | tf_op jit(solution)/shard_map/ppermute | solution.py:333
  (6 other events, 242.3 us)

commit v6 on v5

--- a/solution.py
+++ b/solution.py
@@ -21,14 +21,16 @@
     return tile
 
 
-def passed_body(value_ref, out_ref):
-    out_ref[...] = value_ref[...]
-
-
-def passed(number):
-    block = jnp.broadcast_to(number, (8, LANES)).astype(jnp.int32)
-    out = pl.pallas_call(passed_body, out_shape=jax.ShapeDtypeStruct(block.shape, jnp.int32))(block)
-    return out[0, 0]
+def passed_body(count, *refs):
+    for value_ref, out_ref in zip(refs[:count], refs[count:]):
+        out_ref[...] = value_ref[...]
+
+
+def passed(values):
+    return pl.pallas_call(
+        functools.partial(passed_body, len(values)),
+        out_shape=[jax.ShapeDtypeStruct(value.shape, value.dtype) for value in values],
+    )(*values)
 
 
 def tied(*values):
@@ -233,11 +235,16 @@
             copy.wait()
 
 
-def products(out, rows, columns, choice, slots, mine, blocks, scale_coef, raw=False):
+def plan_of(choice, slots, groups):
+    return jnp.stack(list(choice) + list(slots) + list(groups)).astype(jnp.int32)
+
+
+def products(out, rows, columns, plan, blocks, scale_coef, raw=False):
     shard_rows = sum(piece.shape[0] for piece in rows[0])
     width = rows[0][0].shape[1]
     half_width = (width - LANES) // 2
-    units, count = len(choice) // 2, len(rows)
+    count = len(rows)
+    units = (plan.shape[0] - count) // 4
     at_once = 2 if units > 1 and count > 1 else 1
     parts = count // at_once
     cols = 2 * columns[0].shape[0]
@@ -247,8 +254,6 @@
     if out is not None:
         aliases = {1 + len(operands): 0}
         operands.append(out)
-    groups = [mine ^ j for j in range(count)]
-    plan = jnp.stack(list(choice) + list(slots) + groups).astype(jnp.int32)
     shape = (2, count, shard_rows, cols if raw else shard_rows * blocks)
     out_shape = [jax.ShapeDtypeStruct(shape, jnp.float32)]
     out_specs = [whole]
@@ -358,15 +363,18 @@
     def either(inner_value, end_value):
         return jnp.where(is_end, end_value, inner_value)
 
-    def put(out, columns, units, me=me):
-        halves = [half for column in columns for half in column]
+    groups = [mine ^ j for j in range(group_size)]
+
+    def planned(units):
         choice, slots = [], []
         for inner_half, end_half in units:
             choice.append(either(*(2 * c + h for c, h, _ in (inner_half, end_half))))
-            slots.append(
-                either(*(2 * (me ^ slot) + h for _, h, slot in (inner_half, end_half)))
-            )
-        return products(out, rows, halves, choice, slots, mine, blocks, scale_coef)
+            slots.append(either(*(2 * (me ^ slot) + h for _, h, slot in (inner_half, end_half))))
+        return plan_of(choice, slots, groups)
+
+    def put(out, columns, plan):
+        halves = [half for column in columns for half in column]
+        return products(out, rows, halves, plan, blocks, scale_coef)
 
     def both(inner_column, inner_slot, end_column, end_slot):
         return [((inner_column, h, inner_slot), (end_column, h, end_slot)) for h in (0, 1)]
@@ -388,12 +396,19 @@
     near_beside = swap(near, ends, 1)
     client = begun(near)
 
-    marked = passed(me)
+    zero = me * 0
+    plans = [
+        planned(both(0, 0, 0, 0) + both(1, 2, 1, 2) + both(2, 1, 2, 1) + both(3, 6, 0, 5)),
+        planned([((0, 0, 4), (2, 0, 4)), ((1, 0, 3), (3, 0, 3))]),
+        planned(both(0, 7, 3, 6) + [((1, 1, 4), (3, 1, 4)), ((2, 1, 3), (4, 1, 3))]),
+        planned(both(0, 5, 1, 5)),
+        plan_of([zero, zero + 1], [zero, zero + 1], groups),
+    ]
+    plan_a, plan_b, plan_c, plan_d, plan_served = passed(plans)
     out = put(
         None,
         [own, near, beside, across],
-        both(0, 0, 0, 0) + both(1, 2, 1, 2) + both(2, 1, 2, 1) + both(3, 6, 0, 5),
-        marked,
+        plan_a,
     )
     *held, first_out = tied(far_end[0], far_inner[0], client[last][0], out)
     low = swap(held[0], inner, 1)
@@ -402,7 +417,7 @@
     out = put(
         first_out,
         [far_end[:1] * 2, end_beside[:1] * 2, far_inner[:1] * 2, near_beside[:1] * 2],
-        [((0, 0, 4), (2, 0, 4)), ((1, 0, 3), (3, 0, 3))],
+        plan_b,
     )
     *held, out = tied(end_beside[1], across_beside[1], client[last][1], out)
     high = swap(held[0], inner, 6)
@@ -411,9 +426,7 @@
     client = list(zip(firsts, seconds))
 
     def serve(columns):
-        zero = me * 0
-        pick = [zero, zero + 1]
-        return products(None, client, columns, pick, pick, mine, blocks, scale_coef, raw=True)
+        return products(None, client, columns, plan_served, blocks, scale_coef, raw=True)
 
     def deliver(block, unit_size):
         return swap(block.astype(jnp.float16), inner, 2), swap(unit_size, inner, 2)
@@ -432,13 +445,13 @@
     out = put(
         out,
         [across_beside, far_end, end_beside, far_inner, near_beside],
-        both(0, 7, 3, 6) + [((1, 1, 4), (3, 1, 4)), ((2, 1, 3), (4, 1, 3))],
+        plan_c,
     )
     low, high, low_beside, high_beside, out = tied(low, high, low_beside, high_beside, out)
     second = serve((low, high))
     sent_b = deliver(*second)
     out, _ = tied(out, second[1])
-    out = put(out, [(low, high), (low_beside, high_beside)], both(0, 5, 1, 5))
+    out = put(out, [(low, high), (low_beside, high_beside)], plan_d)
     out = place(out, sent_a, 6)
     out = place(out, sent_b, 7)
     return out.reshape(shape)

time: 439 us -> 442 us (level)
  no operation moved by 1% of the time
where the time goes in v6:
time: 442 us; the launch traced here: 435 us
  waiting for transfers between devices  218 us (49%)
  Pallas kernels  153 us (35%)
  starting transfers between devices  47.6 us (11%)
  other arithmetic  10.3 us (2%)
  local copies, waits for them, and re-layouts  4.93 us (1%)
    ppermute x18, waiting for transfers between devices, moved(): pieces.append(lax.ppermute(piece, axis, route))  213 us
    pallas_call x6, Pallas kernels, products(): pl.pallas_call(functools.partial(products_body, (shapes, at_once, len(col...  145 us
    ppermute x18, starting transfers between devices, moved(): pieces.append(lax.ppermute(piece, axis, route))  29.6 us
    ppermute x15, starting transfers between devices, moved(): return lax.ppermute(value, axis, route)  18 us
  transfers between devices with their start and end apart: 33, of which 7 were waited for; matrix products, arithmetic and copies ran while one was open for 2% of the time, Pallas kernels for 34%

profile of v6, /device:TPU:31, one launch (start us, length us, event | category | flops | bytes accessed | tf_op | source)
XLA Modules:
  0.0 434.8 jit_solution(12909446334512573446)
XLA Ops:
  0.0 1.5 copy.6.flags_ref
  1.5 6.9 %shard_map.29 = (bf16[256,8320]{1,0:T(8,128)(2,1)}, bf16[128,8320]{1,0:T(8,128)(2,1)}, bf16[128,8320]{1,0:T(8,128)(2,1)}) custom-call(bf16[256,2,16,256]{3,2,1,0:T(8,128)(2,1)} %bitcast.32, s32[256,1]{1,0:T(8,128)} %copy.6.flags_ref), custom_call_target="tpu_custom_call" | custom-call | tf_op jit(solution)/shard_map/pallas_call | solution.py:87
  9.8 2.0 collective-permute-start.6
  12.1 2.1 collective-permute-start.7
  14.1 41.7 %collective-permute-done.2.refs_6_.refs_0_ = bf16[128,8320]{1,0:T(8,128)(2,1)} collective-permute-done((bf16[128,8320]{1,0:T(8,128)(2,1)}, bf16[128,8320]{1,0:T(8,128)(2,1)}, u32[]{:S(2)}, u32[]{:S(2)}) %collective-permute-start.2) | collective-permute-done | bytes 2129952 | tf_op jit(solution)/shard_map/ppermute | solution.py:341
  56.1 45.4 %collective-permute-done.3.refs_7_.refs_1_ = bf16[128,8320]{1,0:T(8,128)(2,1)} collective-permute-done((bf16[128,8320]{1,0:T(8,128)(2,1)}, bf16[128,8320]{1,0:T(8,128)(2,1)}, u32[]{:S(2)}, u32[]{:S(2)}) %collective-permute-start.3) | collective-permute-done | bytes 2129952 | tf_op jit(solution)/shard_map/ppermute | solution.py:341
  101.5 1.5 collective-permute-start
  104.4 46.8 %collective-permute-done.5.refs_9_ = bf16[128,8320]{1,0:T(8,128)(2,1)S(1)} collective-permute-done((bf16[128,8320]{1,0:T(8,128)(2,1)}, bf16[128,8320]{1,0:T(8,128)(2,1)S(1)}, u32[]{:S(2)}, u32[]{:S(2)}) %collective-permute-start.5) | collective-permute-done | bytes 2129952 | tf_op jit(solution)/shard_map/ppermute | solution.py:341
  153.3 2.1 collective-permute-start.17
  155.5 6.5 %collective-permute-start.16 = (bf16[128,8320]{1,0:T(8,128)(2,1)}, bf16[128,8320]{1,0:T(8,128)(2,1)}, u32[]{:S(2)}, u32[]{:S(2)}) collective-permute-start(bf16[128,8320]{1,0:T(8,128)(2,1)} %collective-permute-done.4.refs_8_), channel_id=1, source_target_pairs={{0,8},{4,12},{24,16},{28,20},{1,9},{5,13},{25,17},{29,21},{2,10},{... | collective-permute-start | bytes 6389768 | tf_op jit(solution)/shard_map/ppermute | solution.py:341
  166.8 35.4 %collective-permute-done.10.refs_8_.refs_9_.refs_10_ = bf16[128,8320]{1,0:T(8,128)(2,1)} collective-permute-done((bf16[128,8320]{1,0:T(8,128)(2,1)}, bf16[128,8320]{1,0:T(8,128)(2,1)}, u32[]{:S(2)}, u32[]{:S(2)}) %collective-permute-start.10) | collective-permute-done | bytes 2129952 | tf_op jit(solution)/shard_map/ppermute | solution.py:341
  202.1 2.0 collective-permute-start.14
  204.1 2.7 collective-permute-start.13
  206.7 2.0 collective-permute-start.22
  211.0 47.3 %shard_map.30.refs_12_ = f32[2,4,256,2048]{3,2,1,0:T(8,128)} custom-call(s32[20]{0:T(128)} %get-tuple-element.38.plan_ref, bf16[256,8320]{1,0:T(8,128)(2,1)} %get-tuple-element.34.refs_0_, bf16[256,8320]{1,0:T(8,128)(2,1)} %collective-permute-done.refs_1_, bf16[256,8320]{1,0:T(8,128)(2,1)} %collective-permute-done.1.refs_2_, ...), custom_call_target="tpu_custom_call" | custom-call | flops 34359738368 | bytes 83886080 | tf_op jit(solution)/shard_map/pallas_call | solution.py:267
  258.4 16.4 %shard_map.31.refs_14_ = f32[2,4,256,2048]{3,2,1,0:T(8,128)} custom-call(s32[8]{0:T(128)} %get-tuple-element.40.plan_ref, bf16[256,8320]{1,0:T(8,128)(2,1)} %get-tuple-element.34.refs_0_, bf16[256,8320]{1,0:T(8,128)(2,1)} %collective-permute-done.refs_1_, bf16[256,8320]{1,0:T(8,128)(2,1)} %collective-permute-done.1.refs_2_, ...), custom_call_target="tpu_custom_call", output_to_operand_aliasing={{}: (13, {})} | custom-call | flops 8589934592 | bytes 20971520 | tf_op jit(solution)/shard_map/pallas_call | solution.py:267
  274.8 2.4 collective-permute-start.24
  277.2 2.1 collective-permute-start.21
  281.4 43.1 %collective-permute-done.24.refs_13_ = bf16[128,8320]{1,0:T(8,128)(2,1)} collective-permute-done((bf16[128,8320]{1,0:T(8,128)(2,1)}, bf16[128,8320]{1,0:T(8,128)(2,1)}, u32[]{:S(2)}, u32[]{:S(2)}) %collective-permute-start.24) | collective-permute-done | bytes 2129952 | tf_op jit(solution)/shard_map/ppermute | solution.py:341
  324.4 2.0 collective-permute-start.18
  327.7 2.0 collective-permute-start.12
  329.7 2.6 collective-permute-start.19
  332.3 19.0 %shard_map.32 = (f32[2,4,256,256]{3,2,1,0:T(8,128)}, f32[4,8,128]{2,1,0:T(8,128)}) custom-call(s32[8]{0:T(128)} %get-tuple-element.47.plan_ref, bf16[128,8320]{1,0:T(8,128)(2,1)} %collective-permute-done.2.refs_6_.refs_0_, bf16[128,8320]{1,0:T(8,128)(2,1)} %collective-permute-done.3.refs_7_.refs_1_, bf16[128,8320]{1,0:T(8,128)(2,1)} %collective-permute-done.25.refs_2_, ...), custom_call_target="tpu_custom_call" | custom-call | flops 8589934592 | bytes 20971520 | tf_op jit(solution)/shard_map/pallas_call | solution.py:267
  352.6 27.1 %shard_map.33.refs_8_ = f32[2,4,256,2048]{3,2,1,0:T(8,128)} custom-call(s32[12]{0:T(128)} %get-tuple-element.45.plan_ref, bf16[256,8320]{1,0:T(8,128)(2,1)} %get-tuple-element.34.refs_0_, bf16[256,8320]{1,0:T(8,128)(2,1)} %collective-permute-done.refs_1_, bf16[256,8320]{1,0:T(8,128)(2,1)} %collective-permute-done.1.refs_2_, ...), custom_call_target="tpu_custom_call", output_to_operand_aliasing={{}: (15, {})} | custom-call | flops 17179869184 | bytes 41943040 | tf_op jit(solution)/shard_map/pallas_call | solution.py:267
  379.8 1.8 convert_element_type.12
  382.8 19.0 %shard_map.34 = (f32[2,4,256,256]{3,2,1,0:T(8,128)}, f32[4,8,128]{2,1,0:T(8,128)}) custom-call(s32[8]{0:T(128)} %get-tuple-element.47.plan_ref, bf16[128,8320]{1,0:T(8,128)(2,1)} %collective-permute-done.2.refs_6_.refs_0_, bf16[128,8320]{1,0:T(8,128)(2,1)} %collective-permute-done.3.refs_7_.refs_1_, bf16[128,8320]{1,0:T(8,128)(2,1)} %collective-permute-done.25.refs_2_, ...), custom_call_target="tpu_custom_call" | custom-call | flops 8589934592 | bytes 20971520 | tf_op jit(solution)/shard_map/pallas_call | solution.py:267
  403.1 1.8 convert_element_type.14
  404.9 1.5 collective-permute-start.31
  406.4 16.3 %shard_map.35 = f32[2,4,256,2048]{3,2,1,0:T(8,128)} custom-call(s32[8]{0:T(128)} %get-tuple-element.33.plan_ref, bf16[256,8320]{1,0:T(8,128)(2,1)} %get-tuple-element.34.refs_0_, bf16[256,8320]{1,0:T(8,128)(2,1)} %collective-permute-done.refs_1_, bf16[256,8320]{1,0:T(8,128)(2,1)} %collective-permute-done.1.refs_2_, ...), custom_call_target="tpu_custom_call", output_to_operand_aliasing={{}: (9, {})} | custom-call | flops 8589934592 | bytes 20971520 | tf_op jit(solution)/shard_map/pallas_call | solution.py:267
  422.9 3.2 select_dynamic-update-slice_fusion.1
  426.1 5.1 %collective-permute-done.31 = f16[2,4,256,256]{3,2,1,0:T(8,128)(2,1)} collective-permute-done((f16[2,4,256,256]{3,2,1,0:T(8,128)(2,1)S(1)}, f16[2,4,256,256]{3,2,1,0:T(8,128)(2,1)}, u32[]{:S(2)}, u32[]{:S(2)}) %collective-permute-start.31) | collective-permute-done | bytes 1048608 | tf_op jit(solution)/shard_map/ppermute | solution.py:338
  431.3 3.5 select_dynamic-update-slice_fusion
  (60 shorter events, 19.9 us)
Async XLA Ops:
  8.4 47.5 %collective-permute-start.2 = (bf16[128,8320]{1,0:T(8,128)(2,1)}, bf16[128,8320]{1,0:T(8,128)(2,1)}, u32[]{:S(2)}, u32[]{:S(2)}) collective-permute-start(bf16[128,8320]{1,0:T(8,128)(2,1)} %get-tuple-element.35.refs_4_), channel_id=1, source_target_pairs={{0,8},{4,12},{8,0},{12,4},{16,24},{20,28},{24,16},{28,20},{1,9},{5... | collective-permute-start | bytes 6389768 | tf_op jit(solution)/shard_map/ppermute | solution.py:341
  8.5 93.0 %collective-permute-start.3 = (bf16[128,8320]{1,0:T(8,128)(2,1)}, bf16[128,8320]{1,0:T(8,128)(2,1)}, u32[]{:S(2)}, u32[]{:S(2)}) collective-permute-start(bf16[128,8320]{1,0:T(8,128)(2,1)} %get-tuple-element.36.refs_5_), channel_id=1, source_target_pairs={{0,8},{4,12},{8,0},{12,4},{16,24},{20,28},{24,16},{28,20},{1,9},{5... | collective-permute-start | bytes 6389768 | tf_op jit(solution)/shard_map/ppermute | solution.py:341
  9.8 93.2 %collective-permute-start.6 = (bf16[128,8320]{1,0:T(8,128)(2,1)}, bf16[128,8320]{1,0:T(8,128)(2,1)}, u32[]{:S(2)}, u32[]{:S(2)}) collective-permute-start(bf16[128,8320]{1,0:T(8,128)(2,1)} %get-tuple-element.35.refs_4_), channel_id=1, source_target_pairs={{8,16},{12,20},{16,8},{20,12},{9,17},{13,21},{17,9},{21,13},{10,18... | collective-permute-start | bytes 6389768 | tf_op jit(solution)/shard_map/ppermute | solution.py:341
  11.8 139.5 %collective-permute-start.1 = (bf16[256,8320]{1,0:T(8,128)(2,1)}, bf16[256,8320]{1,0:T(8,128)(2,1)}, u32[]{:S(2)}, u32[]{:S(2)}) collective-permute-start(bf16[256,8320]{1,0:T(8,128)(2,1)} %get-tuple-element.34.refs_0_), channel_id=1, source_target_pairs={{0,2},{1,3},{2,0},{3,1},{4,6},{5,7},{6,4},{7,5},{8,10},{9,11},{10,... | collective-permute-start | bytes 12779528 | tf_op jit(solution)/shard_map/ppermute | solution.py:338
  12.1 91.2 %collective-permute-start.7 = (bf16[128,8320]{1,0:T(8,128)(2,1)}, bf16[128,8320]{1,0:T(8,128)(2,1)}, u32[]{:S(2)}, u32[]{:S(2)}) collective-permute-start(bf16[128,8320]{1,0:T(8,128)(2,1)} %get-tuple-element.36.refs_5_), channel_id=1, source_target_pairs={{8,16},{12,20},{16,8},{20,12},{9,17},{13,21},{17,9},{21,13},{10,18... | collective-permute-start | bytes 6389768 | tf_op jit(solution)/shard_map/ppermute | solution.py:341
  55.9 48.2 %collective-permute-start.4 = (bf16[128,8320]{1,0:T(8,128)(2,1)}, bf16[128,8320]{1,0:T(8,128)(2,1)}, u32[]{:S(2)}, u32[]{:S(2)}) collective-permute-start(bf16[128,8320]{1,0:T(8,128)(2,1)} %get-tuple-element.35.refs_4_), channel_id=1, source_target_pairs={{0,4},{4,0},{8,12},{12,8},{16,20},{20,16},{24,28},{28,24},{1,5},{5... | collective-permute-start | bytes 6389768 | tf_op jit(solution)/shard_map/ppermute | solution.py:341
  101.5 51.8 %collective-permute-start = (bf16[256,8320]{1,0:T(8,128)(2,1)}, bf16[256,8320]{1,0:T(8,128)(2,1)}, u32[]{:S(2)}, u32[]{:S(2)}) collective-permute-start(bf16[256,8320]{1,0:T(8,128)(2,1)} %get-tuple-element.34.refs_0_), channel_id=1, source_target_pairs={{0,1},{1,0},{2,3},{3,2},{4,5},{5,4},{6,7},{7,6},{8,9},{9,8},{10,11... | collective-permute-start | bytes 12779528 | tf_op jit(solution)/shard_map/ppermute | solution.py:338
  103.1 48.2 %collective-permute-start.5 = (bf16[128,8320]{1,0:T(8,128)(2,1)}, bf16[128,8320]{1,0:T(8,128)(2,1)S(1)}, u32[]{:S(2)}, u32[]{:S(2)}) collective-permute-start(bf16[128,8320]{1,0:T(8,128)(2,1)} %get-tuple-element.36.refs_5_), channel_id=1, source_target_pairs={{0,4},{4,0},{8,12},{12,8},{16,20},{20,16},{24,28},{28,24},{1,5},{5... | collective-permute-start | bytes 6389768 | tf_op jit(solution)/shard_map/ppermute | solution.py:341
  103.3 52.2 %collective-permute-start.9 = (bf16[128,8320]{1,0:T(8,128)(2,1)}, bf16[128,8320]{1,0:T(8,128)(2,1)S(1)}, u32[]{:S(2)}, u32[]{:S(2)}) collective-permute-start(bf16[128,8320]{1,0:T(8,128)(2,1)} %collective-permute-done.2.refs_6_.refs_0_), channel_id=1, source_target_pairs={{8,16},{12,20},{16,8},{20,12},{9,17},{13,21},{17,9},{21,13},{10,18... | collective-permute-start | bytes 6389768 | tf_op jit(solution)/shard_map/ppermute | solution.py:341
  104.1 57.9 %collective-permute-start.11 = (bf16[128,8320]{1,0:T(8,128)(2,1)}, bf16[128,8320]{1,0:T(8,128)(2,1)}, u32[]{:S(2)}, u32[]{:S(2)}) collective-permute-start(bf16[128,8320]{1,0:T(8,128)(2,1)} %collective-permute-done.2.refs_6_.refs_0_), channel_id=1, source_target_pairs={{0,2},{1,3},{2,0},{3,1},{4,6},{5,7},{6,4},{7,5},{8,10},{9,11},{10,... | collective-permute-start | bytes 6389768 | tf_op jit(solution)/shard_map/ppermute | solution.py:341
  151.3 59.8 %collective-permute-start.8 = (bf16[256,8320]{1,0:T(8,128)(2,1)}, bf16[256,8320]{1,0:T(8,128)(2,1)}, u32[]{:S(2)}, u32[]{:S(2)}) collective-permute-start(bf16[256,8320]{1,0:T(8,128)(2,1)} %collective-permute-done.1.refs_2_), channel_id=1, source_target_pairs={{0,1},{1,0},{2,3},{3,2},{4,5},{5,4},{6,7},{7,6},{8,9},{9,8},{10,11... | collective-permute-start | bytes 12779528 | tf_op jit(solution)/shard_map/ppermute | solution.py:338
  152.0 50.1 %collective-permute-start.10 = (bf16[128,8320]{1,0:T(8,128)(2,1)}, bf16[128,8320]{1,0:T(8,128)(2,1)}, u32[]{:S(2)}, u32[]{:S(2)}) collective-permute-start(bf16[128,8320]{1,0:T(8,128)(2,1)} %collective-permute-done.6.refs_10_), channel_id=1, source_target_pairs={{8,0},{12,4},{16,24},{20,28},{9,1},{13,5},{17,25},{21,29},{10,2},{... | collective-permute-start | bytes 6389768 | tf_op jit(solution)/shard_map/ppermute | solution.py:341
  153.3 50.8 %collective-permute-start.17 = (bf16[128,8320]{1,0:T(8,128)(2,1)}, bf16[128,8320]{1,0:T(8,128)(2,1)}, u32[]{:S(2)}, u32[]{:S(2)}) collective-permute-start(bf16[128,8320]{1,0:T(8,128)(2,1)} %collective-permute-done.2.refs_6_.refs_0_), channel_id=1, source_target_pairs={{0,4},{4,0},{24,28},{28,24},{1,5},{5,1},{25,29},{29,25},{2,6},{6,2... | collective-permute-start | bytes 6389768 | tf_op jit(solution)/shard_map/ppermute | solution.py:341
  155.5 51.2 %collective-permute-start.16 = (bf16[128,8320]{1,0:T(8,128)(2,1)}, bf16[128,8320]{1,0:T(8,128)(2,1)}, u32[]{:S(2)}, u32[]{:S(2)}) collective-permute-start(bf16[128,8320]{1,0:T(8,128)(2,1)} %collective-permute-done.4.refs_8_), channel_id=1, source_target_pairs={{0,8},{4,12},{24,16},{28,20},{1,9},{5,13},{25,17},{29,21},{2,10},{... | collective-permute-start | bytes 6389768 | tf_op jit(solution)/shard_map/ppermute | solution.py:341
  162.0 47.6 %collective-permute-start.15 = (bf16[128,8320]{1,0:T(8,128)(2,1)}, bf16[128,8320]{1,0:T(8,128)(2,1)}, u32[]{:S(2)}, u32[]{:S(2)}) collective-permute-start(bf16[128,8320]{1,0:T(8,128)(2,1)} %collective-permute-done.3.refs_7_.refs_1_), channel_id=1, source_target_pairs={{0,2},{1,3},{2,0},{3,1},{4,6},{5,7},{6,4},{7,5},{8,10},{9,11},{10,... | collective-permute-start | bytes 6389768 | tf_op jit(solution)/shard_map/ppermute | solution.py:341
  202.1 72.7 %collective-permute-start.14 = (bf16[128,8320]{1,0:T(8,128)(2,1)}, bf16[128,8320]{1,0:T(8,128)(2,1)}, u32[]{:S(2)}, u32[]{:S(2)}) collective-permute-start(bf16[128,8320]{1,0:T(8,128)(2,1)} %collective-permute-done.7.refs_11_), channel_id=1, source_target_pairs={{8,12},{12,8},{16,20},{20,16},{9,13},{13,9},{17,21},{21,17},{10,14... | collective-permute-start | bytes 6389768 | tf_op jit(solution)/shard_map/ppermute | solution.py:341
  204.1 73.1 %collective-permute-start.13 = (bf16[128,8320]{1,0:T(8,128)(2,1)}, bf16[128,8320]{1,0:T(8,128)(2,1)}, u32[]{:S(2)}, u32[]{:S(2)}) collective-permute-start(bf16[128,8320]{1,0:T(8,128)(2,1)} %copy-done.2), channel_id=1, source_target_pairs={{0,8},{4,12},{24,16},{28,20},{1,9},{5,13},{25,17},{29,21},{2,10},{... | collective-permute-start | bytes 6389768 | tf_op jit(solution)/shard_map/ppermute | solution.py:341
  206.7 72.5 %collective-permute-start.22 = (bf16[128,8320]{1,0:T(8,128)(2,1)}, bf16[128,8320]{1,0:T(8,128)(2,1)}, u32[]{:S(2)}, u32[]{:S(2)}) collective-permute-start(bf16[128,8320]{1,0:T(8,128)(2,1)} %collective-permute-done.3.refs_7_.refs_1_), channel_id=1, source_target_pairs={{8,16},{12,20},{16,8},{20,12},{9,17},{13,21},{17,9},{21,13},{10,18... | collective-permute-start | bytes 6389768 | tf_op jit(solution)/shard_map/ppermute | solution.py:341
  209.6 70.4 %collective-permute-start.25 = (bf16[128,8320]{1,0:T(8,128)(2,1)}, bf16[128,8320]{1,0:T(8,128)(2,1)}, u32[]{:S(2)}, u32[]{:S(2)}) collective-permute-start(bf16[128,8320]{1,0:T(8,128)(2,1)} %collective-permute-done.2.refs_6_.refs_0_), channel_id=1, source_target_pairs={{0,1},{1,0},{2,3},{3,2},{4,5},{5,4},{6,7},{7,6},{8,9},{9,8},{10,11... | collective-permute-start | bytes 6389768 | tf_op jit(solution)/shard_map/ppermute | solution.py:338
  211.0 69.0 %collective-permute-start.26 = (bf16[128,8320]{1,0:T(8,128)(2,1)}, bf16[128,8320]{1,0:T(8,128)(2,1)}, u32[]{:S(2)}, u32[]{:S(2)}) collective-permute-start(bf16[128,8320]{1,0:T(8,128)(2,1)} %collective-permute-done.3.refs_7_.refs_1_), channel_id=1, source_target_pairs={{0,1},{1,0},{2,3},{3,2},{4,5},{5,4},{6,7},{7,6},{8,9},{9,8},{10,11... | collective-permute-start | bytes 6389768 | tf_op jit(solution)/shard_map/ppermute | solution.py:338
  274.8 49.6 %collective-permute-start.24 = (bf16[128,8320]{1,0:T(8,128)(2,1)}, bf16[128,8320]{1,0:T(8,128)(2,1)}, u32[]{:S(2)}, u32[]{:S(2)}) collective-permute-start(bf16[128,8320]{1,0:T(8,128)(2,1)} %collective-permute-done.3.refs_7_.refs_1_), channel_id=1, source_target_pairs={{0,4},{4,0},{24,28},{28,24},{1,5},{5,1},{25,29},{29,25},{2,6},{6,2... | collective-permute-start | bytes 6389768 | tf_op jit(solution)/shard_map/ppermute | solution.py:341
  277.2 49.2 %collective-permute-start.21 = (bf16[128,8320]{1,0:T(8,128)(2,1)}, bf16[128,8320]{1,0:T(8,128)(2,1)}, u32[]{:S(2)}, u32[]{:S(2)}) collective-permute-start(bf16[128,8320]{1,0:T(8,128)(2,1)} %collective-permute-done.6.refs_10_), channel_id=1, source_target_pairs={{8,12},{12,8},{16,20},{20,16},{9,13},{13,9},{17,21},{21,17},{10,14... | collective-permute-start | bytes 6389768 | tf_op jit(solution)/shard_map/ppermute | solution.py:341
  279.3 48.4 %collective-permute-start.28 = (bf16[128,8320]{1,0:T(8,128)(2,1)}, bf16[128,8320]{1,0:T(8,128)(2,1)}, u32[]{:S(2)}, u32[]{:S(2)}) collective-permute-start(bf16[128,8320]{1,0:T(8,128)(2,1)} %collective-permute-done.15.refs_5_), channel_id=1, source_target_pairs={{0,1},{1,0},{2,3},{3,2},{4,5},{5,4},{6,7},{7,6},{8,9},{9,8},{10,11... | collective-permute-start | bytes 6389768 | tf_op jit(solution)/shard_map/ppermute | solution.py:338
  280.0 49.7 %collective-permute-start.27 = (bf16[128,8320]{1,0:T(8,128)(2,1)}, bf16[128,8320]{1,0:T(8,128)(2,1)}, u32[]{:S(2)}, u32[]{:S(2)}) collective-permute-start(bf16[128,8320]{1,0:T(8,128)(2,1)} %collective-permute-done.11.refs_4_), channel_id=1, source_target_pairs={{0,1},{1,0},{2,3},{3,2},{4,5},{5,4},{6,7},{7,6},{8,9},{9,8},{10,11... | collective-permute-start | bytes 6389768 | tf_op jit(solution)/shard_map/ppermute | solution.py:338
  280.0 71.2 %collective-permute-start.23 = (bf16[128,8320]{1,0:T(8,128)(2,1)}, bf16[128,8320]{1,0:T(8,128)(2,1)}, u32[]{:S(2)}, u32[]{:S(2)}) collective-permute-start(bf16[128,8320]{1,0:T(8,128)(2,1)} %collective-permute-done.7.refs_11_), channel_id=1, source_target_pairs={{8,0},{12,4},{16,24},{20,28},{9,1},{13,5},{17,25},{21,29},{10,2},{... | collective-permute-start | bytes 6389768 | tf_op jit(solution)/shard_map/ppermute | solution.py:341
  324.4 55.3 %collective-permute-start.18 = (bf16[128,8320]{1,0:T(8,128)(2,1)}, bf16[128,8320]{1,0:T(8,128)(2,1)}, u32[]{:S(2)}, u32[]{:S(2)}) collective-permute-start(bf16[128,8320]{1,0:T(8,128)(2,1)} %collective-permute-done.13.refs_9_), channel_id=1, source_target_pairs={{8,16},{12,20},{16,8},{20,12},{9,17},{13,21},{17,9},{21,13},{10,18... | collective-permute-start | bytes 6389768 | tf_op jit(solution)/shard_map/ppermute | solution.py:338
  326.4 53.3 %collective-permute-start.20 = (bf16[128,8320]{1,0:T(8,128)(2,1)}, bf16[128,8320]{1,0:T(8,128)(2,1)}, u32[]{:S(2)}, u32[]{:S(2)}) collective-permute-start(bf16[128,8320]{1,0:T(8,128)(2,1)} %collective-permute-done.14.refs_5_), channel_id=1, source_target_pairs={{8,0},{12,4},{16,24},{20,28},{9,1},{13,5},{17,25},{21,29},{10,2},{... | collective-permute-start | bytes 6389768 | tf_op jit(solution)/shard_map/ppermute | solution.py:338
  327.7 52.0 %collective-permute-start.12 = (bf16[128,8320]{1,0:T(8,128)(2,1)S(1)}, bf16[128,8320]{1,0:T(8,128)(2,1)}, u32[]{:S(2)}, u32[]{:S(2)}) collective-permute-start(bf16[128,8320]{1,0:T(8,128)(2,1)S(1)} %copy-done.1), channel_id=1, source_target_pairs={{8,12},{12,8},{16,20},{20,16},{9,13},{13,9},{17,21},{21,17},{10,14... | collective-permute-start | bytes 6389768 | tf_op jit(solution)/shard_map/ppermute | solution.py:338
  329.7 50.0 %collective-permute-start.19 = (bf16[128,8320]{1,0:T(8,128)(2,1)}, bf16[128,8320]{1,0:T(8,128)(2,1)}, u32[]{:S(2)}, u32[]{:S(2)}) collective-permute-start(bf16[128,8320]{1,0:T(8,128)(2,1)} %collective-permute-done.10.refs_8_.refs_9_.refs_10_), channel_id=1, source_target_pairs={{0,4},{4,0},{24,28},{28,24},{1,5},{5,1},{25,29},{29,25},{2,6},{6,2... | collective-permute-start | bytes 6389768 | tf_op jit(solution)/shard_map/ppermute | solution.py:338
  351.3 71.4 %collective-permute-start.30 = (f32[4,8,128]{2,1,0:T(8,128)}, f32[4,8,128]{2,1,0:T(8,128)S(1)}, u32[]{:S(2)}, u32[]{:S(2)}) collective-permute-start(f32[4,8,128]{2,1,0:T(8,128)} %get-tuple-element.50), channel_id=1, source_target_pairs={{8,0},{12,4},{16,24},{20,28},{9,1},{13,5},{17,25},{21,29},{10,2},{... | collective-permute-start | bytes 49160 | tf_op jit(solution)/shard_map/ppermute | solution.py:338
  381.5 41.4 %collective-permute-start.29 = (f16[2,4,256,256]{3,2,1,0:T(8,128)(2,1)S(1)}, f16[2,4,256,256]{3,2,1,0:T(8,128)(2,1)S(1)}, u32[]{:S(2)}, u32[]{:S(2)}) collective-permute-start(f16[2,4,256,256]{3,2,1,0:T(8,128)(2,1)S(1)} %convert_element_type.12), channel_id=1, source_target_pairs={{8,0},{12,4},{16,24},{20,28},{9,1},{13,5},{17,25},{21,29},{10,2},{... | collective-permute-start | bytes 3145736 | tf_op jit(solution)/shard_map/ppermute | solution.py:338
  404.9 26.4 %collective-permute-start.31 = (f16[2,4,256,256]{3,2,1,0:T(8,128)(2,1)S(1)}, f16[2,4,256,256]{3,2,1,0:T(8,128)(2,1)}, u32[]{:S(2)}, u32[]{:S(2)}) collective-permute-start(f16[2,4,256,256]{3,2,1,0:T(8,128)(2,1)S(1)} %convert_element_type.14), channel_id=1, source_target_pairs={{8,0},{12,4},{16,24},{20,28},{9,1},{13,5},{17,25},{21,29},{10,2},{... | collective-permute-start | bytes 3145736 | tf_op jit(solution)/shard_map/ppermute | solution.py:338
  (4 other events, 197.4 us)

commit v7 on v6

--- a/solution.py
+++ b/solution.py
@@ -98,39 +98,58 @@
     )(spectra, flags.reshape(rows, 1))
 
 
-def products_body(sizes, scale_coef, raw, plan_ref, *refs):
-    shapes, at_once, known, units = sizes
+def products_body(sizes, scale_coef, plan_ref, *refs):
+    sets, at_once, known, units, served, given = sizes
     refs = list(refs)
-    rows, at = [], 0
-    for shape in shapes:
-        rows.append(refs[at : at + len(shape)])
-        at += len(shape)
+    row_sets, at = [], 0
+    for shapes in sets:
+        rows = []
+        for shape in shapes:
+            rows.append(refs[at : at + len(shape)])
+            at += len(shape)
+        row_sets.append(rows)
     columns = refs[at : at + known]
-    held, right, col_marks, staged, row_sems, col_sems, out_sems = refs[-7:]
-    outs = refs[-9:-7] if raw else refs[-8:-7]
+    held, right, col_marks, staged, inverse, row_sems, col_sems, out_sems = refs[-8:]
+    main = [] if served == units else [refs[at + known + given]]
+    extra = refs[-10:-8] if served else []
     unit, part = pl.program_id(0), pl.program_id(1)
-    parts = len(rows) // at_once
+    parts = len(row_sets[0]) // at_once
     now = unit * parts + part
     shard_rows = held.shape[1] // at_once
     cols, half_width = right.shape[1] // 2, right.shape[2] // 2
     half_cols = cols // 2
 
-    def row_copies(index, row, slot):
+    def for_set(which_unit, body):
+        if len(row_sets) == 1:
+            body(row_sets[0])
+        else:
+            pl.when(which_unit < served)(lambda: body(row_sets[1]))
+            pl.when(which_unit >= served)(lambda: body(row_sets[0]))
+
+    def row_copies(pieces, row, slot):
         copies, top = [], row * shard_rows
-        for number, piece in enumerate(rows[index]):
+        for number, piece in enumerate(pieces):
             where = held.at[slot, pl.ds(top, piece.shape[0])]
             copies.append(pltpu.make_async_copy(piece, where, row_sems.at[slot, row, number]))
             top += piece.shape[0]
         return copies
 
-    def start_rows(which, slot):
-        for index in range(parts):
-
-            @pl.when(which == index)
-            def _():
-                for row in range(at_once):
-                    for copy in row_copies(index * at_once + row, row, slot):
-                        copy.start()
+    def start_rows(which_unit, which, slot):
+        def start(rows):
+            for index in range(parts):
+
+                @pl.when(which == index)
+                def _():
+                    for row in range(at_once):
+                        for copy in row_copies(rows[index * at_once + row], row, slot):
+                            copy.start()
+
+        for_set(which_unit, start)
+
+    def wait_rows(rows):
+        for row in range(at_once):
+            for copy in row_copies(rows[row], row, slot):
+                copy.wait()
 
     def col_copies(source, half, slot):
         top = half * half_cols
@@ -157,7 +176,8 @@
                     for copy in col_copies(columns[index], half, slot):
                         copy.start()
 
-    def out_copies(slot):
+    def out_copies(slot, target_ref=None):
+        target_ref = (main + extra)[0] if target_ref is None else target_ref
         copies = []
         for row in range(at_once):
             group = plan_ref[4 * units + part * at_once + row]
@@ -165,7 +185,7 @@
                 start = plan_ref[2 * units + 2 * unit + half] * half_cols
                 lanes = pl.ds(pl.multiple_of(start, half_cols), half_cols)
                 source = staged.at[slot, :, row, :, pl.ds(half * half_cols, half_cols)]
-                target = outs[0].at[:, group, :, lanes]
+                target = target_ref.at[:, group, :, lanes]
                 copies.append(pltpu.make_async_copy(source, target, out_sems.at[slot, row, half]))
         return copies
 
@@ -173,12 +193,12 @@
 
     @pl.when(now == 0)
     def _():
-        start_rows(0, 0)
+        start_rows(0, 0, 0)
         start_cols(0, 0)
 
     @pl.when(now + 1 < units * parts)
     def _():
-        start_rows(lax.rem(part + 1, parts), lax.rem(now + 1, 2))
+        start_rows(lax.div(now + 1, parts), lax.rem(part + 1, parts), lax.rem(now + 1, 2))
 
     @pl.when(jnp.logical_and(part == 0, unit + 1 < units))
     def _():
@@ -191,10 +211,7 @@
                 copy.wait()
         right[col_slot, cols:, :half_width] = -right[col_slot, :cols, half_width:]
 
-    for row in range(at_once):
-        for copy in row_copies(row, row, slot):
-            copy.wait()
-
+    for_set(unit, wait_rows)
     left = held[slot, :, : 2 * half_width]
     product = lax.dot_general(left, right[col_slot], NT, preferred_element_type=jnp.float32)
 
@@ -216,18 +233,36 @@
         marks = held[slot, pl.ds(top, shard_rows), pl.ds(2 * half_width, LANES)]
         row_factor, row_norm = sums(marks.astype(jnp.float32), 1)
         scaling = (row_factor * scale_coef) * col_factor
-        if raw:
-            bound = jnp.max(row_factor / row_norm, axis=0, keepdims=True)
-            bound = bound * jnp.max(col_factor / col_norm, axis=1, keepdims=True)
-            unit_size = jnp.maximum(bound * (2 * half_width * scale_coef), FLOOR) / 32768
-            group = plan_ref[4 * units + part * at_once + row]
-            outs[1][group] = jnp.broadcast_to(unit_size, outs[1].shape[1:])
-            scaling = scaling * (1 / unit_size)
+        if served:
+
+            @pl.when(unit < served)
+            def _():
+                bound = jnp.max(row_factor / row_norm, axis=0, keepdims=True)
+                bound = bound * jnp.max(col_factor / col_norm, axis=1, keepdims=True)
+                unit_size = jnp.maximum(bound * (2 * half_width * scale_coef), FLOOR) / 32768
+                group = plan_ref[4 * units + part * at_once + row]
+                extra[1][group] = jnp.broadcast_to(unit_size, extra[1].shape[1:])
+                inverse[...] = jnp.broadcast_to(1 / unit_size, inverse.shape)
+
+            if main:
+
+                @pl.when(unit >= served)
+                def _():
+                    inverse[...] = jnp.ones_like(inverse)
+
+            scaling = scaling * inverse[0:1, 0:1]
         staged[slot, 0, row] = product[top : top + shard_rows, :cols] * scaling
         staged[slot, 1, row] = product[top : top + shard_rows, cols:] * scaling
 
-    for copy in out_copies(slot):
-        copy.start()
+    def start_out(target_ref):
+        for copy in out_copies(slot, target_ref):
+            copy.start()
+
+    if served and main:
+        pl.when(unit < served)(lambda: start_out(extra[0]))
+        pl.when(unit >= served)(lambda: start_out(main[0]))
+    else:
+        start_out((main + extra)[0])
 
     @pl.when(now == units * parts - 1)
     def _():
@@ -239,43 +274,49 @@
     return jnp.stack(list(choice) + list(slots) + list(groups)).astype(jnp.int32)
 
 
-def products(out, rows, columns, plan, blocks, scale_coef, raw=False):
-    shard_rows = sum(piece.shape[0] for piece in rows[0])
-    width = rows[0][0].shape[1]
+def products(out, row_sets, columns, plan, blocks, scale_coef, served=0):
+    count = len(row_sets[0])
+    units = (plan.shape[0] - count) // 4
+    shard_rows = sum(piece.shape[0] for piece in row_sets[0][0])
+    width = row_sets[0][0][0].shape[1]
+    kind = row_sets[0][0][0].dtype
     half_width = (width - LANES) // 2
-    count = len(rows)
-    units = (plan.shape[0] - count) // 4
     at_once = 2 if units > 1 and count > 1 else 1
     parts = count // at_once
     cols = 2 * columns[0].shape[0]
     whole = pl.BlockSpec(memory_space=pl.ANY)
-    operands = [piece for pieces in rows for piece in pieces] + list(columns)
+    operands = [piece for rows in row_sets for pieces in rows for piece in pieces]
+    operands += list(columns)
     aliases = {}
     if out is not None:
         aliases = {1 + len(operands): 0}
         operands.append(out)
-    shape = (2, count, shard_rows, cols if raw else shard_rows * blocks)
-    out_shape = [jax.ShapeDtypeStruct(shape, jnp.float32)]
-    out_specs = [whole]
-    if raw:
-        out_shape.append(jax.ShapeDtypeStruct((count, 8, LANES), jnp.float32))
-        out_specs.append(
-            pl.BlockSpec((count, 8, LANES), lambda i, j, s: (0, 0, 0))
-        )
-    shapes = [[piece.shape[0] for piece in pieces] for pieces in rows]
-    most = max(len(pieces) for pieces in rows)
-    given = pl.pallas_call(
-        functools.partial(products_body, (shapes, at_once, len(columns), units), scale_coef, raw),
+    out_shape, out_specs = [], []
+    if served < units:
+        shape = (2, count, shard_rows, shard_rows * blocks)
+        out_shape.append(jax.ShapeDtypeStruct(shape, jnp.float32))
+        out_specs.append(whole)
+    if served:
+        sizes = (count, 8, LANES)
+        out_shape.append(jax.ShapeDtypeStruct((2, count, shard_rows, cols), jnp.float32))
+        out_shape.append(jax.ShapeDtypeStruct(sizes, jnp.float32))
+        out_specs += [whole, pl.BlockSpec(sizes, lambda i, j, s: (0, 0, 0))]
+    sets = [[[piece.shape[0] for piece in pieces] for pieces in rows] for rows in row_sets]
+    most = max(len(pieces) for rows in row_sets for pieces in rows)
+    sizes = (sets, at_once, len(columns), units, served, int(out is not None))
+    return pl.pallas_call(
+        functools.partial(products_body, sizes, scale_coef),
         grid_spec=pltpu.PrefetchScalarGridSpec(
             num_scalar_prefetch=1,
             grid=(units, parts),
             in_specs=[whole] * len(operands),
             out_specs=out_specs,
             scratch_shapes=[
-                pltpu.VMEM((2, at_once * shard_rows, width), rows[0][0].dtype),
-                pltpu.VMEM((2, 2 * cols, 2 * half_width), rows[0][0].dtype),
-                pltpu.VMEM((2, cols, LANES), rows[0][0].dtype),
+                pltpu.VMEM((2, at_once * shard_rows, width), kind),
+                pltpu.VMEM((2, 2 * cols, 2 * half_width), kind),
+                pltpu.VMEM((2, cols, LANES), kind),
                 pltpu.VMEM((2, 2, at_once, shard_rows, cols), jnp.float32),
+                pltpu.VMEM((8, LANES), jnp.float32),
                 pltpu.SemaphoreType.DMA((2, at_once, most)),
                 pltpu.SemaphoreType.DMA((2, 2, 4)),
                 pltpu.SemaphoreType.DMA((2, at_once, 2)),
@@ -292,7 +333,6 @@
             dimension_semantics=("arbitrary", "arbitrary"), vmem_limit_bytes=60 * 2**20
         ),
     )(plan, *operands)
-    return given if raw else given[0]
 
 
 def gathered(spectra, detector_valid, scale_coef):
@@ -365,8 +405,8 @@
 
     groups = [mine ^ j for j in range(group_size)]
 
-    def planned(units):
-        choice, slots = [], []
+    def planned(units, served=()):
+        choice, slots = list(served), [me * 0, me * 0 + 1][: len(served)]
         for inner_half, end_half in units:
             choice.append(either(*(2 * c + h for c, h, _ in (inner_half, end_half))))
             slots.append(either(*(2 * (me ^ slot) + h for _, h, slot in (inner_half, end_half))))
@@ -374,7 +414,7 @@
 
     def put(out, columns, plan):
         halves = [half for column in columns for half in column]
-        return products(out, rows, halves, plan, blocks, scale_coef)
+        return products(out, [rows], halves, plan, blocks, scale_coef)[0]
 
     def both(inner_column, inner_slot, end_column, end_slot):
         return [((inner_column, h, inner_slot), (end_column, h, end_slot)) for h in (0, 1)]
@@ -396,13 +436,15 @@
     near_beside = swap(near, ends, 1)
     client = begun(near)
 
-    zero = me * 0
+    zero, one = me * 0, me * 0 + 1
+    units_c = both(0, 7, 3, 6) + [((1, 1, 4), (3, 1, 4)), ((2, 1, 3), (4, 1, 3))]
+    plan_c = planned(units_c, [zero + 2, zero + 3])
     plans = [
         planned(both(0, 0, 0, 0) + both(1, 2, 1, 2) + both(2, 1, 2, 1) + both(3, 6, 0, 5)),
         planned([((0, 0, 4), (2, 0, 4)), ((1, 0, 3), (3, 0, 3))]),
-        planned(both(0, 7, 3, 6) + [((1, 1, 4), (3, 1, 4)), ((2, 1, 3), (4, 1, 3))]),
+        plan_c,
         planned(both(0, 5, 1, 5)),
-        plan_of([zero, zero + 1], [zero, zero + 1], groups),
+        plan_of([zero, one], [zero, one], groups),
     ]
     plan_a, plan_b, plan_c, plan_d, plan_served = passed(plans)
     out = put(
@@ -425,9 +467,6 @@
     seconds = finished({0: near[1], last: held[2]})
     client = list(zip(firsts, seconds))
 
-    def serve(columns):
-        return products(None, client, columns, plan_served, blocks, scale_coef, raw=True)
-
     def deliver(block, unit_size):
         return swap(block.astype(jnp.float16), inner, 2), swap(unit_size, inner, 2)
 
@@ -439,16 +478,19 @@
         kept = lax.dynamic_slice(out, starts, block.shape)
         return lax.dynamic_update_slice(out, jnp.where(is_end, block, kept), starts)
 
-    first = serve(far_end)
+    columns = [across_beside, far_end, end_beside, far_inner, near_beside]
+    out, *first = products(
+        out,
+        [rows, client],
+        [half for column in columns for half in column],
+        plan_c,
+        blocks,
+        scale_coef,
+        served=1,
+    )
     sent_a = deliver(*first)
-    out, _ = tied(out, first[1])
-    out = put(
-        out,
-        [across_beside, far_end, end_beside, far_inner, near_beside],
-        plan_c,
-    )
     low, high, low_beside, high_beside, out = tied(low, high, low_beside, high_beside, out)
-    second = serve((low, high))
+    second = products(None, [client], [low, high], plan_served, blocks, scale_coef, served=1)
     sent_b = deliver(*second)
     out, _ = tied(out, second[1])
     out = put(out, [(low, high), (low_beside, high_beside)], plan_d)

time: 442 us -> 441 us (level)
  waiting for transfers between devices: 218 us -> 225 us
  Pallas kernels: 153 us -> 147 us
    pallas_call x6 -> x5, Pallas kernels: 145 us -> 139 us  [products(): pl.pallas_call(functools.partial(products_body, sizes, scale_coef), grid_...]
  transfers between devices with their start and end apart: 33 -> 33, of which waited for: 7 -> 10; matrix products, arithmetic and copies ran while one was open for 2% -> 2% of each run, Pallas kernels for 34% -> 32%
where the time goes in v7:
time: 441 us; the launch traced here: 437 us
  waiting for transfers between devices  225 us (51%)
  Pallas kernels  147 us (33%)
  starting transfers between devices  49 us (11%)
  other arithmetic  10.3 us (2%)
  local copies, waits for them, and re-layouts  4.96 us (1%)
    ppermute x18, waiting for transfers between devices, moved(): pieces.append(lax.ppermute(piece, axis, route))  215 us
    pallas_call x5, Pallas kernels, products(): pl.pallas_call(functools.partial(products_body, sizes, scale_coef), grid_...  139 us
    ppermute x18, starting transfers between devices, moved(): pieces.append(lax.ppermute(piece, axis, route))  29.2 us
    ppermute x15, starting transfers between devices, moved(): return lax.ppermute(value, axis, route)  19.7 us
    ppermute x15, waiting for transfers between devices, moved(): return lax.ppermute(value, axis, route)  9.15 us
  transfers between devices with their start and end apart: 33, of which 10 were waited for; matrix products, arithmetic and copies ran while one was open for 2% of the time, Pallas kernels for 32%

profile of v7, /device:TPU:31, one launch (start us, length us, event | category | flops | bytes accessed | tf_op | source)
XLA Modules:
  0.0 436.5 jit_solution(15196201364672499770)
XLA Ops:
  1.5 6.9 %shard_map.29 = (bf16[256,8320]{1,0:T(8,128)(2,1)}, bf16[128,8320]{1,0:T(8,128)(2,1)}, bf16[128,8320]{1,0:T(8,128)(2,1)}) custom-call(bf16[256,2,16,256]{3,2,1,0:T(8,128)(2,1)} %bitcast.32, s32[256,1]{1,0:T(8,128)} %copy.6.flags_ref), custom_call_target="tpu_custom_call" | custom-call | tf_op jit(solution)/shard_map/pallas_call | solution.py:87
  9.8 2.1 collective-permute-start.6
  12.2 2.0 collective-permute-start.7
  14.1 41.8 %collective-permute-done.2.refs_6_.refs_4_.refs_0_ = bf16[128,8320]{1,0:T(8,128)(2,1)} collective-permute-done((bf16[128,8320]{1,0:T(8,128)(2,1)}, bf16[128,8320]{1,0:T(8,128)(2,1)}, u32[]{:S(2)}, u32[]{:S(2)}) %collective-permute-start.2) | collective-permute-done | bytes 2129952 | tf_op jit(solution)/shard_map/ppermute | solution.py:381
  56.1 45.4 %collective-permute-done.3.refs_7_.refs_5_.refs_1_ = bf16[128,8320]{1,0:T(8,128)(2,1)} collective-permute-done((bf16[128,8320]{1,0:T(8,128)(2,1)}, bf16[128,8320]{1,0:T(8,128)(2,1)}, u32[]{:S(2)}, u32[]{:S(2)}) %collective-permute-start.3) | collective-permute-done | bytes 2129952 | tf_op jit(solution)/shard_map/ppermute | solution.py:381
  101.5 1.5 collective-permute-start
  104.4 46.8 %collective-permute-done.5.refs_9_ = bf16[128,8320]{1,0:T(8,128)(2,1)S(1)} collective-permute-done((bf16[128,8320]{1,0:T(8,128)(2,1)}, bf16[128,8320]{1,0:T(8,128)(2,1)S(1)}, u32[]{:S(2)}, u32[]{:S(2)}) %collective-permute-start.5) | collective-permute-done | bytes 2129952 | tf_op jit(solution)/shard_map/ppermute | solution.py:381
  153.3 2.1 collective-permute-start.17
  155.5 6.5 %collective-permute-start.16 = (bf16[128,8320]{1,0:T(8,128)(2,1)}, bf16[128,8320]{1,0:T(8,128)(2,1)}, u32[]{:S(2)}, u32[]{:S(2)}) collective-permute-start(bf16[128,8320]{1,0:T(8,128)(2,1)} %collective-permute-done.4.refs_8_), channel_id=1, source_target_pairs={{0,8},{4,12},{24,16},{28,20},{1,9},{5,13},{25,17},{29,21},{2,10},{... | collective-permute-start | bytes 6389768 | tf_op jit(solution)/shard_map/ppermute | solution.py:381
  166.8 35.3 %collective-permute-done.10.refs_8_.refs_9_.refs_18_ = bf16[128,8320]{1,0:T(8,128)(2,1)} collective-permute-done((bf16[128,8320]{1,0:T(8,128)(2,1)}, bf16[128,8320]{1,0:T(8,128)(2,1)}, u32[]{:S(2)}, u32[]{:S(2)}) %collective-permute-start.10) | collective-permute-done | bytes 2129952 | tf_op jit(solution)/shard_map/ppermute | solution.py:381
  202.1 2.0 collective-permute-start.14
  204.1 2.7 collective-permute-start.13
  206.8 1.5 collective-permute-start.21
  211.0 2.0 collective-permute-start.26
  213.0 47.3 %shard_map.30.refs_12_ = f32[2,4,256,2048]{3,2,1,0:T(8,128)} custom-call(s32[20]{0:T(128)} %get-tuple-element.38.plan_ref, bf16[256,8320]{1,0:T(8,128)(2,1)} %get-tuple-element.34.refs_0_, bf16[256,8320]{1,0:T(8,128)(2,1)} %collective-permute-done.refs_1_, bf16[256,8320]{1,0:T(8,128)(2,1)} %collective-permute-done.1.refs_2_, ...), custom_call_target="tpu_custom_call" | custom-call | flops 34359738368 | bytes 83886080 | tf_op jit(solution)/shard_map/pallas_call | solution.py:307
  260.4 16.4 %shard_map.31.refs_22_ = f32[2,4,256,2048]{3,2,1,0:T(8,128)} custom-call(s32[8]{0:T(128)} %get-tuple-element.40.plan_ref, bf16[256,8320]{1,0:T(8,128)(2,1)} %get-tuple-element.34.refs_0_, bf16[256,8320]{1,0:T(8,128)(2,1)} %collective-permute-done.refs_1_, bf16[256,8320]{1,0:T(8,128)(2,1)} %collective-permute-done.1.refs_2_, ...), custom_call_target="tpu_custom_call", output_to_operand_aliasing={{}: (13, {})} | custom-call | flops 8589934592 | bytes 20971520 | tf_op jit(solution)/shard_map/pallas_call | solution.py:307
  276.8 2.1 collective-permute-start.28
  278.9 2.0 collective-permute-start.25
  282.8 44.1 %collective-permute-done.28.refs_21_ = bf16[128,8320]{1,0:T(8,128)(2,1)} collective-permute-done((bf16[128,8320]{1,0:T(8,128)(2,1)}, bf16[128,8320]{1,0:T(8,128)(2,1)}, u32[]{:S(2)}, u32[]{:S(2)}) %collective-permute-start.28) | collective-permute-done | bytes 2129952 | tf_op jit(solution)/shard_map/ppermute | solution.py:381
  326.9 2.0 collective-permute-start.18
  330.7 2.0 collective-permute-start.12
  332.7 3.3 collective-permute-start.19
  336.0 40.1 %shard_map.32 = (f32[2,4,256,2048]{3,2,1,0:T(8,128)}, f32[2,4,256,256]{3,2,1,0:T(8,128)}, f32[4,8,128]{2,1,0:T(8,128)}) custom-call(s32[16]{0:T(128)} %get-tuple-element.45.plan_ref, bf16[256,8320]{1,0:T(8,128)(2,1)} %get-tuple-element.34.refs_0_, bf16[256,8320]{1,0:T(8,128)(2,1)} %collective-permute-done.refs_1_, ...), custom_call_target="tpu_custom_call", output_to_operand_aliasing={{0}: (23, {})} | custom-call | flops 25769803776 | bytes 62914560 | tf_op jit(solution)/shard_map/pallas_call | solution.py:307
  376.2 1.9 collective-permute-done.20.refs_7_
  378.1 3.5 collective-permute-done.19.refs_6_
  381.6 1.8 convert_element_type.12
  384.7 19.1 %shard_map.33 = (f32[2,4,256,256]{3,2,1,0:T(8,128)}, f32[4,8,128]{2,1,0:T(8,128)}) custom-call(s32[8]{0:T(128)} %get-tuple-element.55.plan_ref, bf16[128,8320]{1,0:T(8,128)(2,1)} %collective-permute-done.2.refs_6_.refs_4_.refs_0_, bf16[128,8320]{1,0:T(8,128)(2,1)} %collective-permute-done.3.refs_7_.refs_5_.refs_1_, ...), custom_call_target="tpu_custom_call" | custom-call | flops 8589934592 | bytes 20971520 | tf_op jit(solution)/shard_map/pallas_call | solution.py:307
  406.4 1.8 convert_element_type.14
  409.5 16.4 %shard_map.34 = f32[2,4,256,2048]{3,2,1,0:T(8,128)} custom-call(s32[8]{0:T(128)} %get-tuple-element.33.plan_ref, bf16[256,8320]{1,0:T(8,128)(2,1)} %get-tuple-element.34.refs_0_, bf16[256,8320]{1,0:T(8,128)(2,1)} %collective-permute-done.refs_1_, bf16[256,8320]{1,0:T(8,128)(2,1)} %collective-permute-done.1.refs_2_, ...), custom_call_target="tpu_custom_call", output_to_operand_aliasing={{}: (9, {})} | custom-call | flops 8589934592 | bytes 20971520 | tf_op jit(solution)/shard_map/pallas_call | solution.py:307
  426.2 3.2 select_dynamic-update-slice_fusion.1
  429.4 3.7 collective-permute-done.31
  433.0 3.5 select_dynamic-update-slice_fusion
  (61 shorter events, 23.5 us)
Async XLA Ops:
  8.3 47.5 %collective-permute-start.2 = (bf16[128,8320]{1,0:T(8,128)(2,1)}, bf16[128,8320]{1,0:T(8,128)(2,1)}, u32[]{:S(2)}, u32[]{:S(2)}) collective-permute-start(bf16[128,8320]{1,0:T(8,128)(2,1)} %get-tuple-element.35.refs_4_), channel_id=1, source_target_pairs={{0,8},{4,12},{8,0},{12,4},{16,24},{20,28},{24,16},{28,20},{1,9},{5... | collective-permute-start | bytes 6389768 | tf_op jit(solution)/shard_map/ppermute | solution.py:381
  8.5 93.0 %collective-permute-start.3 = (bf16[128,8320]{1,0:T(8,128)(2,1)}, bf16[128,8320]{1,0:T(8,128)(2,1)}, u32[]{:S(2)}, u32[]{:S(2)}) collective-permute-start(bf16[128,8320]{1,0:T(8,128)(2,1)} %get-tuple-element.36.refs_5_), channel_id=1, source_target_pairs={{0,8},{4,12},{8,0},{12,4},{16,24},{20,28},{24,16},{28,20},{1,9},{5... | collective-permute-start | bytes 6389768 | tf_op jit(solution)/shard_map/ppermute | solution.py:381
  9.8 93.2 %collective-permute-start.6 = (bf16[128,8320]{1,0:T(8,128)(2,1)}, bf16[128,8320]{1,0:T(8,128)(2,1)}, u32[]{:S(2)}, u32[]{:S(2)}) collective-permute-start(bf16[128,8320]{1,0:T(8,128)(2,1)} %get-tuple-element.35.refs_4_), channel_id=1, source_target_pairs={{8,16},{12,20},{16,8},{20,12},{9,17},{13,21},{17,9},{21,13},{10,18... | collective-permute-start | bytes 6389768 | tf_op jit(solution)/shard_map/ppermute | solution.py:381
  11.9 139.4 %collective-permute-start.1 = (bf16[256,8320]{1,0:T(8,128)(2,1)}, bf16[256,8320]{1,0:T(8,128)(2,1)}, u32[]{:S(2)}, u32[]{:S(2)}) collective-permute-start(bf16[256,8320]{1,0:T(8,128)(2,1)} %get-tuple-element.34.refs_0_), channel_id=1, source_target_pairs={{0,2},{1,3},{2,0},{3,1},{4,6},{5,7},{6,4},{7,5},{8,10},{9,11},{10,... | collective-permute-start | bytes 12779528 | tf_op jit(solution)/shard_map/ppermute | solution.py:378
  12.2 91.1 %collective-permute-start.7 = (bf16[128,8320]{1,0:T(8,128)(2,1)}, bf16[128,8320]{1,0:T(8,128)(2,1)}, u32[]{:S(2)}, u32[]{:S(2)}) collective-permute-start(bf16[128,8320]{1,0:T(8,128)(2,1)} %get-tuple-element.36.refs_5_), channel_id=1, source_target_pairs={{8,16},{12,20},{16,8},{20,12},{9,17},{13,21},{17,9},{21,13},{10,18... | collective-permute-start | bytes 6389768 | tf_op jit(solution)/shard_map/ppermute | solution.py:381
  55.9 48.2 %collective-permute-start.4 = (bf16[128,8320]{1,0:T(8,128)(2,1)}, bf16[128,8320]{1,0:T(8,128)(2,1)}, u32[]{:S(2)}, u32[]{:S(2)}) collective-permute-start(bf16[128,8320]{1,0:T(8,128)(2,1)} %get-tuple-element.35.refs_4_), channel_id=1, source_target_pairs={{0,4},{4,0},{8,12},{12,8},{16,20},{20,16},{24,28},{28,24},{1,5},{5... | collective-permute-start | bytes 6389768 | tf_op jit(solution)/shard_map/ppermute | solution.py:381
  101.5 51.8 %collective-permute-start = (bf16[256,8320]{1,0:T(8,128)(2,1)}, bf16[256,8320]{1,0:T(8,128)(2,1)}, u32[]{:S(2)}, u32[]{:S(2)}) collective-permute-start(bf16[256,8320]{1,0:T(8,128)(2,1)} %get-tuple-element.34.refs_0_), channel_id=1, source_target_pairs={{0,1},{1,0},{2,3},{3,2},{4,5},{5,4},{6,7},{7,6},{8,9},{9,8},{10,11... | collective-permute-start | bytes 12779528 | tf_op jit(solution)/shard_map/ppermute | solution.py:378
  103.1 48.2 %collective-permute-start.5 = (bf16[128,8320]{1,0:T(8,128)(2,1)}, bf16[128,8320]{1,0:T(8,128)(2,1)S(1)}, u32[]{:S(2)}, u32[]{:S(2)}) collective-permute-start(bf16[128,8320]{1,0:T(8,128)(2,1)} %get-tuple-element.36.refs_5_), channel_id=1, source_target_pairs={{0,4},{4,0},{8,12},{12,8},{16,20},{20,16},{24,28},{28,24},{1,5},{5... | collective-permute-start | bytes 6389768 | tf_op jit(solution)/shard_map/ppermute | solution.py:381
  103.3 52.2 %collective-permute-start.9 = (bf16[128,8320]{1,0:T(8,128)(2,1)}, bf16[128,8320]{1,0:T(8,128)(2,1)S(1)}, u32[]{:S(2)}, u32[]{:S(2)}) collective-permute-start(bf16[128,8320]{1,0:T(8,128)(2,1)} %collective-permute-done.2.refs_6_.refs_4_.refs_0_), channel_id=1, source_target_pairs={{8,16},{12,20},{16,8},{20,12},{9,17},{13,21},{17,9},{21,13},{10,18... | collective-permute-start | bytes 6389768 | tf_op jit(solution)/shard_map/ppermute | solution.py:381
  104.1 57.9 %collective-permute-start.11 = (bf16[128,8320]{1,0:T(8,128)(2,1)}, bf16[128,8320]{1,0:T(8,128)(2,1)}, u32[]{:S(2)}, u32[]{:S(2)}) collective-permute-start(bf16[128,8320]{1,0:T(8,128)(2,1)} %collective-permute-done.2.refs_6_.refs_4_.refs_0_), channel_id=1, source_target_pairs={{0,2},{1,3},{2,0},{3,1},{4,6},{5,7},{6,4},{7,5},{8,10},{9,11},{10,... | collective-permute-start | bytes 6389768 | tf_op jit(solution)/shard_map/ppermute | solution.py:381
  151.3 59.8 %collective-permute-start.8 = (bf16[256,8320]{1,0:T(8,128)(2,1)}, bf16[256,8320]{1,0:T(8,128)(2,1)}, u32[]{:S(2)}, u32[]{:S(2)}) collective-permute-start(bf16[256,8320]{1,0:T(8,128)(2,1)} %collective-permute-done.1.refs_2_), channel_id=1, source_target_pairs={{0,1},{1,0},{2,3},{3,2},{4,5},{5,4},{6,7},{7,6},{8,9},{9,8},{10,11... | collective-permute-start | bytes 12779528 | tf_op jit(solution)/shard_map/ppermute | solution.py:378
  152.0 50.1 %collective-permute-start.10 = (bf16[128,8320]{1,0:T(8,128)(2,1)}, bf16[128,8320]{1,0:T(8,128)(2,1)}, u32[]{:S(2)}, u32[]{:S(2)}) collective-permute-start(bf16[128,8320]{1,0:T(8,128)(2,1)} %collective-permute-done.6.refs_10_), channel_id=1, source_target_pairs={{8,0},{12,4},{16,24},{20,28},{9,1},{13,5},{17,25},{21,29},{10,2},{... | collective-permute-start | bytes 6389768 | tf_op jit(solution)/shard_map/ppermute | solution.py:381
  153.3 50.7 %collective-permute-start.17 = (bf16[128,8320]{1,0:T(8,128)(2,1)}, bf16[128,8320]{1,0:T(8,128)(2,1)}, u32[]{:S(2)}, u32[]{:S(2)}) collective-permute-start(bf16[128,8320]{1,0:T(8,128)(2,1)} %collective-permute-done.2.refs_6_.refs_4_.refs_0_), channel_id=1, source_target_pairs={{0,4},{4,0},{24,28},{28,24},{1,5},{5,1},{25,29},{29,25},{2,6},{6,2... | collective-permute-start | bytes 6389768 | tf_op jit(solution)/shard_map/ppermute | solution.py:381
  155.5 51.3 %collective-permute-start.16 = (bf16[128,8320]{1,0:T(8,128)(2,1)}, bf16[128,8320]{1,0:T(8,128)(2,1)}, u32[]{:S(2)}, u32[]{:S(2)}) collective-permute-start(bf16[128,8320]{1,0:T(8,128)(2,1)} %collective-permute-done.4.refs_8_), channel_id=1, source_target_pairs={{0,8},{4,12},{24,16},{28,20},{1,9},{5,13},{25,17},{29,21},{2,10},{... | collective-permute-start | bytes 6389768 | tf_op jit(solution)/shard_map/ppermute | solution.py:381
  162.0 47.6 %collective-permute-start.15 = (bf16[128,8320]{1,0:T(8,128)(2,1)}, bf16[128,8320]{1,0:T(8,128)(2,1)}, u32[]{:S(2)}, u32[]{:S(2)}) collective-permute-start(bf16[128,8320]{1,0:T(8,128)(2,1)} %collective-permute-done.3.refs_7_.refs_5_.refs_1_), channel_id=1, source_target_pairs={{0,2},{1,3},{2,0},{3,1},{4,6},{5,7},{6,4},{7,5},{8,10},{9,11},{10,... | collective-permute-start | bytes 6389768 | tf_op jit(solution)/shard_map/ppermute | solution.py:381
  202.1 74.7 %collective-permute-start.14 = (bf16[128,8320]{1,0:T(8,128)(2,1)}, bf16[128,8320]{1,0:T(8,128)(2,1)}, u32[]{:S(2)}, u32[]{:S(2)}) collective-permute-start(bf16[128,8320]{1,0:T(8,128)(2,1)} %collective-permute-done.7.refs_11_), channel_id=1, source_target_pairs={{8,12},{12,8},{16,20},{20,16},{9,13},{13,9},{17,21},{21,17},{10,14... | collective-permute-start | bytes 6389768 | tf_op jit(solution)/shard_map/ppermute | solution.py:381
  204.1 74.9 %collective-permute-start.13 = (bf16[128,8320]{1,0:T(8,128)(2,1)}, bf16[128,8320]{1,0:T(8,128)(2,1)}, u32[]{:S(2)}, u32[]{:S(2)}) collective-permute-start(bf16[128,8320]{1,0:T(8,128)(2,1)} %copy-done.2), channel_id=1, source_target_pairs={{0,8},{4,12},{24,16},{28,20},{1,9},{5,13},{25,17},{29,21},{2,10},{... | collective-permute-start | bytes 6389768 | tf_op jit(solution)/shard_map/ppermute | solution.py:381
  206.8 74.1 %collective-permute-start.21 = (bf16[128,8320]{1,0:T(8,128)(2,1)}, bf16[128,8320]{1,0:T(8,128)(2,1)}, u32[]{:S(2)}, u32[]{:S(2)}) collective-permute-start(bf16[128,8320]{1,0:T(8,128)(2,1)} %collective-permute-done.2.refs_6_.refs_4_.refs_0_), channel_id=1, source_target_pairs={{0,1},{1,0},{2,3},{3,2},{4,5},{5,4},{6,7},{7,6},{8,9},{9,8},{10,11... | collective-permute-start | bytes 6389768 | tf_op jit(solution)/shard_map/ppermute | solution.py:378
  209.6 72.6 %collective-permute-start.22 = (bf16[128,8320]{1,0:T(8,128)(2,1)}, bf16[128,8320]{1,0:T(8,128)(2,1)}, u32[]{:S(2)}, u32[]{:S(2)}) collective-permute-start(bf16[128,8320]{1,0:T(8,128)(2,1)} %collective-permute-done.3.refs_7_.refs_5_.refs_1_), channel_id=1, source_target_pairs={{0,1},{1,0},{2,3},{3,2},{4,5},{5,4},{6,7},{7,6},{8,9},{9,8},{10,11... | collective-permute-start | bytes 6389768 | tf_op jit(solution)/shard_map/ppermute | solution.py:378
  211.0 71.5 %collective-permute-start.26 = (bf16[128,8320]{1,0:T(8,128)(2,1)}, bf16[128,8320]{1,0:T(8,128)(2,1)}, u32[]{:S(2)}, u32[]{:S(2)}) collective-permute-start(bf16[128,8320]{1,0:T(8,128)(2,1)} %collective-permute-done.3.refs_7_.refs_5_.refs_1_), channel_id=1, source_target_pairs={{8,16},{12,20},{16,8},{20,12},{9,17},{13,21},{17,9},{21,13},{10,18... | collective-permute-start | bytes 6389768 | tf_op jit(solution)/shard_map/ppermute | solution.py:381
  276.8 50.1 %collective-permute-start.28 = (bf16[128,8320]{1,0:T(8,128)(2,1)}, bf16[128,8320]{1,0:T(8,128)(2,1)}, u32[]{:S(2)}, u32[]{:S(2)}) collective-permute-start(bf16[128,8320]{1,0:T(8,128)(2,1)} %collective-permute-done.3.refs_7_.refs_5_.refs_1_), channel_id=1, source_target_pairs={{0,4},{4,0},{24,28},{28,24},{1,5},{5,1},{25,29},{29,25},{2,6},{6,2... | collective-permute-start | bytes 6389768 | tf_op jit(solution)/shard_map/ppermute | solution.py:381
  278.9 49.9 %collective-permute-start.25 = (bf16[128,8320]{1,0:T(8,128)(2,1)}, bf16[128,8320]{1,0:T(8,128)(2,1)}, u32[]{:S(2)}, u32[]{:S(2)}) collective-permute-start(bf16[128,8320]{1,0:T(8,128)(2,1)} %collective-permute-done.6.refs_10_), channel_id=1, source_target_pairs={{8,12},{12,8},{16,20},{20,16},{9,13},{13,9},{17,21},{21,17},{10,14... | collective-permute-start | bytes 6389768 | tf_op jit(solution)/shard_map/ppermute | solution.py:381
  280.9 49.8 %collective-permute-start.27 = (bf16[128,8320]{1,0:T(8,128)(2,1)}, bf16[128,8320]{1,0:T(8,128)(2,1)}, u32[]{:S(2)}, u32[]{:S(2)}) collective-permute-start(bf16[128,8320]{1,0:T(8,128)(2,1)} %collective-permute-done.7.refs_11_), channel_id=1, source_target_pairs={{8,0},{12,4},{16,24},{20,28},{9,1},{13,5},{17,25},{21,29},{10,2},{... | collective-permute-start | bytes 6389768 | tf_op jit(solution)/shard_map/ppermute | solution.py:381
  282.2 50.5 %collective-permute-start.24 = (bf16[128,8320]{1,0:T(8,128)(2,1)}, bf16[128,8320]{1,0:T(8,128)(2,1)}, u32[]{:S(2)}, u32[]{:S(2)}) collective-permute-start(bf16[128,8320]{1,0:T(8,128)(2,1)} %collective-permute-done.15.refs_9_.refs_5_), channel_id=1, source_target_pairs={{0,1},{1,0},{2,3},{3,2},{4,5},{5,4},{6,7},{7,6},{8,9},{9,8},{10,11... | collective-permute-start | bytes 6389768 | tf_op jit(solution)/shard_map/ppermute | solution.py:378
  282.6 53.5 %collective-permute-start.23 = (bf16[128,8320]{1,0:T(8,128)(2,1)}, bf16[128,8320]{1,0:T(8,128)(2,1)}, u32[]{:S(2)}, u32[]{:S(2)}) collective-permute-start(bf16[128,8320]{1,0:T(8,128)(2,1)} %collective-permute-done.11.refs_8_.refs_4_), channel_id=1, source_target_pairs={{0,1},{1,0},{2,3},{3,2},{4,5},{5,4},{6,7},{7,6},{8,9},{9,8},{10,11... | collective-permute-start | bytes 6389768 | tf_op jit(solution)/shard_map/ppermute | solution.py:378
  326.9 49.3 %collective-permute-start.18 = (bf16[128,8320]{1,0:T(8,128)(2,1)}, bf16[128,8320]{1,0:T(8,128)(2,1)}, u32[]{:S(2)}, u32[]{:S(2)}) collective-permute-start(bf16[128,8320]{1,0:T(8,128)(2,1)} %collective-permute-done.13.refs_17_), channel_id=1, source_target_pairs={{8,16},{12,20},{16,8},{20,12},{9,17},{13,21},{17,9},{21,13},{10,18... | collective-permute-start | bytes 6389768 | tf_op jit(solution)/shard_map/ppermute | solution.py:378
  328.9 49.2 %collective-permute-start.20 = (bf16[128,8320]{1,0:T(8,128)(2,1)}, bf16[128,8320]{1,0:T(8,128)(2,1)}, u32[]{:S(2)}, u32[]{:S(2)}) collective-permute-start(bf16[128,8320]{1,0:T(8,128)(2,1)} %collective-permute-done.14.refs_13_), channel_id=1, source_target_pairs={{8,0},{12,4},{16,24},{20,28},{9,1},{13,5},{17,25},{21,29},{10,2},{... | collective-permute-start | bytes 6389768 | tf_op jit(solution)/shard_map/ppermute | solution.py:378
  330.7 47.4 %collective-permute-start.12 = (bf16[128,8320]{1,0:T(8,128)(2,1)S(1)}, bf16[128,8320]{1,0:T(8,128)(2,1)}, u32[]{:S(2)}, u32[]{:S(2)}) collective-permute-start(bf16[128,8320]{1,0:T(8,128)(2,1)S(1)} %copy-done.1), channel_id=1, source_target_pairs={{8,12},{12,8},{16,20},{20,16},{9,13},{13,9},{17,21},{21,17},{10,14... | collective-permute-start | bytes 6389768 | tf_op jit(solution)/shard_map/ppermute | solution.py:378
  332.7 49.0 %collective-permute-start.19 = (bf16[128,8320]{1,0:T(8,128)(2,1)}, bf16[128,8320]{1,0:T(8,128)(2,1)}, u32[]{:S(2)}, u32[]{:S(2)}) collective-permute-start(bf16[128,8320]{1,0:T(8,128)(2,1)} %collective-permute-done.10.refs_8_.refs_9_.refs_18_), channel_id=1, source_target_pairs={{0,4},{4,0},{24,28},{28,24},{1,5},{5,1},{25,29},{29,25},{2,6},{6,2... | collective-permute-start | bytes 6389768 | tf_op jit(solution)/shard_map/ppermute | solution.py:378
  383.4 42.7 %collective-permute-start.29 = (f16[2,4,256,256]{3,2,1,0:T(8,128)(2,1)S(1)}, f16[2,4,256,256]{3,2,1,0:T(8,128)(2,1)S(1)}, u32[]{:S(2)}, u32[]{:S(2)}) collective-permute-start(f16[2,4,256,256]{3,2,1,0:T(8,128)(2,1)S(1)} %convert_element_type.12), channel_id=1, source_target_pairs={{8,0},{12,4},{16,24},{20,28},{9,1},{13,5},{17,25},{21,29},{10,2},{... | collective-permute-start | bytes 3145736 | tf_op jit(solution)/shard_map/ppermute | solution.py:378
  403.8 22.2 %collective-permute-start.32 = (f32[4,8,128]{2,1,0:T(8,128)}, f32[4,8,128]{2,1,0:T(8,128)S(1)}, u32[]{:S(2)}, u32[]{:S(2)}) collective-permute-start(f32[4,8,128]{2,1,0:T(8,128)} %get-tuple-element.56), channel_id=1, source_target_pairs={{8,0},{12,4},{16,24},{20,28},{9,1},{13,5},{17,25},{21,29},{10,2},{... | collective-permute-start | bytes 49160 | tf_op jit(solution)/shard_map/ppermute | solution.py:378
  408.2 24.8 %collective-permute-start.31 = (f16[2,4,256,256]{3,2,1,0:T(8,128)(2,1)S(1)}, f16[2,4,256,256]{3,2,1,0:T(8,128)(2,1)}, u32[]{:S(2)}, u32[]{:S(2)}) collective-permute-start(f16[2,4,256,256]{3,2,1,0:T(8,128)(2,1)S(1)} %convert_element_type.14), channel_id=1, source_target_pairs={{8,0},{12,4},{16,24},{20,28},{9,1},{13,5},{17,25},{21,29},{10,2},{... | collective-permute-start | bytes 3145736 | tf_op jit(solution)/shard_map/ppermute | solution.py:378
  (5 other events, 220.6 us)

commit v8 on v7

--- a/solution.py
+++ b/solution.py
@@ -468,7 +468,8 @@
     client = list(zip(firsts, seconds))
 
     def deliver(block, unit_size):
-        return swap(block.astype(jnp.float16), inner, 2), swap(unit_size, inner, 2)
+        block = swap(block.astype(jnp.float16), inner, 2)
+        return block, swap(unit_size, inner, 2)
 
     def place(out, sent, end_slot):
         block, unit_size = sent
@@ -489,7 +490,7 @@
         served=1,
     )
     sent_a = deliver(*first)
-    low, high, low_beside, high_beside, out = tied(low, high, low_beside, high_beside, out)
+    low, high, out = tied(low, high, out)
     second = products(None, [client], [low, high], plan_served, blocks, scale_coef, served=1)
     sent_b = deliver(*second)
     out, _ = tied(out, second[1])

time: 441 us -> 437 us (level)
  waiting for transfers between devices: 225 us -> 220 us
  transfers between devices with their start and end apart: 33 -> 33, of which waited for: 10 -> 6; matrix products, arithmetic and copies ran while one was open for 2% -> 3% of each run, Pallas kernels for 32% -> 32%
where the time goes in v8:
time: 437 us; the launch traced here: 433 us
  waiting for transfers between devices  220 us (50%)
  Pallas kernels  147 us (34%)
  starting transfers between devices  48.5 us (11%)
  other arithmetic  11.5 us (3%)
  local copies, waits for them, and re-layouts  5.41 us (1%)
    ppermute x18, waiting for transfers between devices, moved(): pieces.append(lax.ppermute(piece, axis, route))  214 us
    pallas_call x5, Pallas kernels, products(): pl.pallas_call(functools.partial(products_body, sizes, scale_coef), grid_...  139 us
    ppermute x18, starting transfers between devices, moved(): pieces.append(lax.ppermute(piece, axis, route))  28 us
    ppermute x15, starting transfers between devices, moved(): return lax.ppermute(value, axis, route)  20.6 us
  transfers between devices with their start and end apart: 33, of which 6 were waited for; matrix products, arithmetic and copies ran while one was open for 3% of the time, Pallas kernels for 32%

profile of v8, /device:TPU:31, one launch (start us, length us, event | category | flops | bytes accessed | tf_op | source)
XLA Modules:
  0.0 433.0 jit_solution(749359098531616432)
XLA Ops:
  0.0 1.5 copy.6.flags_ref
  1.5 6.9 %shard_map.29 = (bf16[256,8320]{1,0:T(8,128)(2,1)}, bf16[128,8320]{1,0:T(8,128)(2,1)}, bf16[128,8320]{1,0:T(8,128)(2,1)}) custom-call(bf16[256,2,16,256]{3,2,1,0:T(8,128)(2,1)} %bitcast.32, s32[256,1]{1,0:T(8,128)} %copy.6.flags_ref), custom_call_target="tpu_custom_call" | custom-call | tf_op jit(solution)/shard_map/pallas_call | solution.py:87
  9.8 2.1 collective-permute-start.6
  12.9 42.9 %collective-permute-done.2.refs_6_.refs_4_.refs_0_ = bf16[128,8320]{1,0:T(8,128)(2,1)} collective-permute-done((bf16[128,8320]{1,0:T(8,128)(2,1)}, bf16[128,8320]{1,0:T(8,128)(2,1)}, u32[]{:S(2)}, u32[]{:S(2)}) %collective-permute-start.2) | collective-permute-done | bytes 2129952 | tf_op jit(solution)/shard_map/ppermute | solution.py:381
  56.1 45.4 %collective-permute-done.3.refs_7_.refs_5_.refs_1_ = bf16[128,8320]{1,0:T(8,128)(2,1)} collective-permute-done((bf16[128,8320]{1,0:T(8,128)(2,1)}, bf16[128,8320]{1,0:T(8,128)(2,1)}, u32[]{:S(2)}, u32[]{:S(2)}) %collective-permute-start.3) | collective-permute-done | bytes 2129952 | tf_op jit(solution)/shard_map/ppermute | solution.py:381
  101.5 1.5 collective-permute-start
  103.3 2.0 collective-permute-start.9
  105.5 45.7 %collective-permute-done.5.refs_9_ = bf16[128,8320]{1,0:T(8,128)(2,1)S(1)} collective-permute-done((bf16[128,8320]{1,0:T(8,128)(2,1)}, bf16[128,8320]{1,0:T(8,128)(2,1)S(1)}, u32[]{:S(2)}, u32[]{:S(2)}) %collective-permute-start.5) | collective-permute-done | bytes 2129952 | tf_op jit(solution)/shard_map/ppermute | solution.py:381
  153.9 2.1 collective-permute-start.17
  156.0 5.3 %collective-permute-start.16 = (bf16[128,8320]{1,0:T(8,128)(2,1)}, bf16[128,8320]{1,0:T(8,128)(2,1)}, u32[]{:S(2)}, u32[]{:S(2)}) collective-permute-start(bf16[128,8320]{1,0:T(8,128)(2,1)} %collective-permute-done.4.refs_8_), channel_id=1, source_target_pairs={{0,8},{4,12},{24,16},{28,20},{1,9},{5,13},{25,17},{29,21},{2,10},{... | collective-permute-start | bytes 6389768 | tf_op jit(solution)/shard_map/ppermute | solution.py:381
  166.0 35.9 %collective-permute-done.10.refs_8_.refs_9_.refs_18_ = bf16[128,8320]{1,0:T(8,128)(2,1)S(1)} collective-permute-done((bf16[128,8320]{1,0:T(8,128)(2,1)}, bf16[128,8320]{1,0:T(8,128)(2,1)S(1)}, u32[]{:S(2)}, u32[]{:S(2)}) %collective-permute-start.10) | collective-permute-done | bytes 2129952 | tf_op jit(solution)/shard_map/ppermute | solution.py:381
  201.9 2.0 collective-permute-start.14
  204.0 2.6 collective-permute-start.13
  206.6 2.2 collective-permute-start.19
  208.7 1.6 collective-permute-start.20
  210.4 2.0 collective-permute-start.24
  212.4 47.3 %shard_map.30.refs_12_ = f32[2,4,256,2048]{3,2,1,0:T(8,128)} custom-call(s32[20]{0:T(128)} %get-tuple-element.36.plan_ref, bf16[256,8320]{1,0:T(8,128)(2,1)} %get-tuple-element.32.refs_0_, bf16[256,8320]{1,0:T(8,128)(2,1)} %collective-permute-done.refs_1_, bf16[256,8320]{1,0:T(8,128)(2,1)} %collective-permute-done.1.refs_2_, ...), custom_call_target="tpu_custom_call" | custom-call | flops 34359738368 | bytes 83886080 | tf_op jit(solution)/shard_map/pallas_call | solution.py:307
  259.7 16.4 %shard_map.31.refs_22_ = f32[2,4,256,2048]{3,2,1,0:T(8,128)} custom-call(s32[8]{0:T(128)} %get-tuple-element.38.plan_ref, bf16[256,8320]{1,0:T(8,128)(2,1)} %get-tuple-element.32.refs_0_, bf16[256,8320]{1,0:T(8,128)(2,1)} %collective-permute-done.refs_1_, bf16[256,8320]{1,0:T(8,128)(2,1)} %collective-permute-done.1.refs_2_, ...), custom_call_target="tpu_custom_call", output_to_operand_aliasing={{}: (13, {})} | custom-call | flops 8589934592 | bytes 20971520 | tf_op jit(solution)/shard_map/pallas_call | solution.py:307
  276.1 2.1 collective-permute-start.26
  278.3 2.0 collective-permute-start.23
  282.1 44.1 %collective-permute-done.26.refs_21_ = bf16[128,8320]{1,0:T(8,128)(2,1)} collective-permute-done((bf16[128,8320]{1,0:T(8,128)(2,1)}, bf16[128,8320]{1,0:T(8,128)(2,1)}, u32[]{:S(2)}, u32[]{:S(2)}) %collective-permute-start.26) | collective-permute-done | bytes 2129952 | tf_op jit(solution)/shard_map/ppermute | solution.py:381
  326.2 2.0 collective-permute-start.18
  328.2 2.1 collective-permute-start.12
  331.6 3.0 collective-permute-start.27
  334.7 40.1 %shard_map.32 = (f32[2,4,256,2048]{3,2,1,0:T(8,128)}, f32[2,4,256,256]{3,2,1,0:T(8,128)}, f32[4,8,128]{2,1,0:T(8,128)}) custom-call(s32[16]{0:T(128)} %get-tuple-element.41.plan_ref, bf16[256,8320]{1,0:T(8,128)(2,1)} %get-tuple-element.32.refs_0_, bf16[256,8320]{1,0:T(8,128)(2,1)} %collective-permute-done.refs_1_, ...), custom_call_target="tpu_custom_call", output_to_operand_aliasing={{0}: (23, {})} | custom-call | flops 25769803776 | bytes 62914560 | tf_op jit(solution)/shard_map/pallas_call | solution.py:307
  374.9 1.8 convert_element_type.12
  377.9 19.1 %shard_map.33 = (f32[2,4,256,256]{3,2,1,0:T(8,128)}, f32[4,8,128]{2,1,0:T(8,128)}) custom-call(s32[8]{0:T(128)} %get-tuple-element.51.plan_ref, bf16[128,8320]{1,0:T(8,128)(2,1)} %collective-permute-done.2.refs_6_.refs_4_.refs_0_, bf16[128,8320]{1,0:T(8,128)(2,1)} %collective-permute-done.3.refs_7_.refs_5_.refs_1_, ...), custom_call_target="tpu_custom_call" | custom-call | flops 8589934592 | bytes 20971520 | tf_op jit(solution)/shard_map/pallas_call | solution.py:307
  399.7 2.7 convert_element_type.14
  403.7 16.3 %shard_map.34 = f32[2,4,256,2048]{3,2,1,0:T(8,128)} custom-call(s32[8]{0:T(128)} %get-tuple-element.31.plan_ref, bf16[256,8320]{1,0:T(8,128)(2,1)} %get-tuple-element.32.refs_0_, bf16[256,8320]{1,0:T(8,128)(2,1)} %collective-permute-done.refs_1_, bf16[256,8320]{1,0:T(8,128)(2,1)} %collective-permute-done.1.refs_2_, ...), custom_call_target="tpu_custom_call", output_to_operand_aliasing={{}: (9, {})} | custom-call | flops 8589934592 | bytes 20971520 | tf_op jit(solution)/shard_map/pallas_call | solution.py:307
  420.2 3.5 select_dynamic-update-slice_fusion.1
  423.8 5.8 %collective-permute-done.31 = f16[2,4,256,256]{3,2,1,0:T(8,128)(2,1)} collective-permute-done((f16[2,4,256,256]{3,2,1,0:T(8,128)(2,1)}, f16[2,4,256,256]{3,2,1,0:T(8,128)(2,1)}, u32[]{:S(2)}, u32[]{:S(2)}) %collective-permute-start.31) | collective-permute-done | bytes 1048608 | tf_op jit(solution)/shard_map/ppermute | solution.py:378
  429.5 3.5 select_dynamic-update-slice_fusion
  (63 shorter events, 19.1 us)
Async XLA Ops:
  8.3 47.5 %collective-permute-start.2 = (bf16[128,8320]{1,0:T(8,128)(2,1)}, bf16[128,8320]{1,0:T(8,128)(2,1)}, u32[]{:S(2)}, u32[]{:S(2)}) collective-permute-start(bf16[128,8320]{1,0:T(8,128)(2,1)} %get-tuple-element.33.refs_4_), channel_id=1, source_target_pairs={{0,8},{4,12},{8,0},{12,4},{16,24},{20,28},{24,16},{28,20},{1,9},{5... | collective-permute-start | bytes 6389768 | tf_op jit(solution)/shard_map/ppermute | solution.py:381
  8.5 93.0 %collective-permute-start.3 = (bf16[128,8320]{1,0:T(8,128)(2,1)}, bf16[128,8320]{1,0:T(8,128)(2,1)}, u32[]{:S(2)}, u32[]{:S(2)}) collective-permute-start(bf16[128,8320]{1,0:T(8,128)(2,1)} %get-tuple-element.34.refs_5_), channel_id=1, source_target_pairs={{0,8},{4,12},{8,0},{12,4},{16,24},{20,28},{24,16},{28,20},{1,9},{5... | collective-permute-start | bytes 6389768 | tf_op jit(solution)/shard_map/ppermute | solution.py:381
  9.8 93.2 %collective-permute-start.6 = (bf16[128,8320]{1,0:T(8,128)(2,1)}, bf16[128,8320]{1,0:T(8,128)(2,1)}, u32[]{:S(2)}, u32[]{:S(2)}) collective-permute-start(bf16[128,8320]{1,0:T(8,128)(2,1)} %get-tuple-element.33.refs_4_), channel_id=1, source_target_pairs={{8,16},{12,20},{16,8},{20,12},{9,17},{13,21},{17,9},{21,13},{10,18... | collective-permute-start | bytes 6389768 | tf_op jit(solution)/shard_map/ppermute | solution.py:381
  11.9 139.4 %collective-permute-start.1 = (bf16[256,8320]{1,0:T(8,128)(2,1)}, bf16[256,8320]{1,0:T(8,128)(2,1)}, u32[]{:S(2)}, u32[]{:S(2)}) collective-permute-start(bf16[256,8320]{1,0:T(8,128)(2,1)} %get-tuple-element.32.refs_0_), channel_id=1, source_target_pairs={{0,2},{1,3},{2,0},{3,1},{4,6},{5,7},{6,4},{7,5},{8,10},{9,11},{10,... | collective-permute-start | bytes 12779528 | tf_op jit(solution)/shard_map/ppermute | solution.py:378
  12.2 91.1 %collective-permute-start.7 = (bf16[128,8320]{1,0:T(8,128)(2,1)}, bf16[128,8320]{1,0:T(8,128)(2,1)S(1)}, u32[]{:S(2)}, u32[]{:S(2)}) collective-permute-start(bf16[128,8320]{1,0:T(8,128)(2,1)} %get-tuple-element.34.refs_5_), channel_id=1, source_target_pairs={{8,16},{12,20},{16,8},{20,12},{9,17},{13,21},{17,9},{21,13},{10,18... | collective-permute-start | bytes 6389768 | tf_op jit(solution)/shard_map/ppermute | solution.py:381
  55.9 49.4 %collective-permute-start.4 = (bf16[128,8320]{1,0:T(8,128)(2,1)}, bf16[128,8320]{1,0:T(8,128)(2,1)}, u32[]{:S(2)}, u32[]{:S(2)}) collective-permute-start(bf16[128,8320]{1,0:T(8,128)(2,1)} %get-tuple-element.33.refs_4_), channel_id=1, source_target_pairs={{0,4},{4,0},{8,12},{12,8},{16,20},{20,16},{24,28},{28,24},{1,5},{5... | collective-permute-start | bytes 6389768 | tf_op jit(solution)/shard_map/ppermute | solution.py:381
  101.5 52.4 %collective-permute-start = (bf16[256,8320]{1,0:T(8,128)(2,1)}, bf16[256,8320]{1,0:T(8,128)(2,1)}, u32[]{:S(2)}, u32[]{:S(2)}) collective-permute-start(bf16[256,8320]{1,0:T(8,128)(2,1)} %get-tuple-element.32.refs_0_), channel_id=1, source_target_pairs={{0,1},{1,0},{2,3},{3,2},{4,5},{5,4},{6,7},{7,6},{8,9},{9,8},{10,11... | collective-permute-start | bytes 12779528 | tf_op jit(solution)/shard_map/ppermute | solution.py:378
  103.1 48.2 %collective-permute-start.5 = (bf16[128,8320]{1,0:T(8,128)(2,1)}, bf16[128,8320]{1,0:T(8,128)(2,1)S(1)}, u32[]{:S(2)}, u32[]{:S(2)}) collective-permute-start(bf16[128,8320]{1,0:T(8,128)(2,1)} %get-tuple-element.34.refs_5_), channel_id=1, source_target_pairs={{0,4},{4,0},{8,12},{12,8},{16,20},{20,16},{24,28},{28,24},{1,5},{5... | collective-permute-start | bytes 6389768 | tf_op jit(solution)/shard_map/ppermute | solution.py:381
  103.3 52.7 %collective-permute-start.9 = (bf16[128,8320]{1,0:T(8,128)(2,1)}, bf16[128,8320]{1,0:T(8,128)(2,1)}, u32[]{:S(2)}, u32[]{:S(2)}) collective-permute-start(bf16[128,8320]{1,0:T(8,128)(2,1)} %collective-permute-done.2.refs_6_.refs_4_.refs_0_), channel_id=1, source_target_pairs={{8,16},{12,20},{16,8},{20,12},{9,17},{13,21},{17,9},{21,13},{10,18... | collective-permute-start | bytes 6389768 | tf_op jit(solution)/shard_map/ppermute | solution.py:381
  105.3 56.0 %collective-permute-start.11 = (bf16[128,8320]{1,0:T(8,128)(2,1)}, bf16[128,8320]{1,0:T(8,128)(2,1)}, u32[]{:S(2)}, u32[]{:S(2)}) collective-permute-start(bf16[128,8320]{1,0:T(8,128)(2,1)} %collective-permute-done.2.refs_6_.refs_4_.refs_0_), channel_id=1, source_target_pairs={{0,2},{1,3},{2,0},{3,1},{4,6},{5,7},{6,4},{7,5},{8,10},{9,11},{10,... | collective-permute-start | bytes 6389768 | tf_op jit(solution)/shard_map/ppermute | solution.py:381
  151.3 59.1 %collective-permute-start.8 = (bf16[256,8320]{1,0:T(8,128)(2,1)}, bf16[256,8320]{1,0:T(8,128)(2,1)}, u32[]{:S(2)}, u32[]{:S(2)}) collective-permute-start(bf16[256,8320]{1,0:T(8,128)(2,1)} %collective-permute-done.1.refs_2_), channel_id=1, source_target_pairs={{0,1},{1,0},{2,3},{3,2},{4,5},{5,4},{6,7},{7,6},{8,9},{9,8},{10,11... | collective-permute-start | bytes 12779528 | tf_op jit(solution)/shard_map/ppermute | solution.py:378
  152.6 49.3 %collective-permute-start.10 = (bf16[128,8320]{1,0:T(8,128)(2,1)}, bf16[128,8320]{1,0:T(8,128)(2,1)S(1)}, u32[]{:S(2)}, u32[]{:S(2)}) collective-permute-start(bf16[128,8320]{1,0:T(8,128)(2,1)} %collective-permute-done.6.refs_10_), channel_id=1, source_target_pairs={{8,0},{12,4},{16,24},{20,28},{9,1},{13,5},{17,25},{21,29},{10,2},{... | collective-permute-start | bytes 6389768 | tf_op jit(solution)/shard_map/ppermute | solution.py:381
  153.9 50.1 %collective-permute-start.17 = (bf16[128,8320]{1,0:T(8,128)(2,1)}, bf16[128,8320]{1,0:T(8,128)(2,1)}, u32[]{:S(2)}, u32[]{:S(2)}) collective-permute-start(bf16[128,8320]{1,0:T(8,128)(2,1)} %collective-permute-done.2.refs_6_.refs_4_.refs_0_), channel_id=1, source_target_pairs={{0,4},{4,0},{24,28},{28,24},{1,5},{5,1},{25,29},{29,25},{2,6},{6,2... | collective-permute-start | bytes 6389768 | tf_op jit(solution)/shard_map/ppermute | solution.py:381
  156.0 50.5 %collective-permute-start.16 = (bf16[128,8320]{1,0:T(8,128)(2,1)}, bf16[128,8320]{1,0:T(8,128)(2,1)}, u32[]{:S(2)}, u32[]{:S(2)}) collective-permute-start(bf16[128,8320]{1,0:T(8,128)(2,1)} %collective-permute-done.4.refs_8_), channel_id=1, source_target_pairs={{0,8},{4,12},{24,16},{28,20},{1,9},{5,13},{25,17},{29,21},{2,10},{... | collective-permute-start | bytes 6389768 | tf_op jit(solution)/shard_map/ppermute | solution.py:381
  161.3 47.4 %collective-permute-start.15 = (bf16[128,8320]{1,0:T(8,128)(2,1)}, bf16[128,8320]{1,0:T(8,128)(2,1)}, u32[]{:S(2)}, u32[]{:S(2)}) collective-permute-start(bf16[128,8320]{1,0:T(8,128)(2,1)} %collective-permute-done.3.refs_7_.refs_5_.refs_1_), channel_id=1, source_target_pairs={{0,2},{1,3},{2,0},{3,1},{4,6},{5,7},{6,4},{7,5},{8,10},{9,11},{10,... | collective-permute-start | bytes 6389768 | tf_op jit(solution)/shard_map/ppermute | solution.py:381
  201.9 74.2 %collective-permute-start.14 = (bf16[128,8320]{1,0:T(8,128)(2,1)}, bf16[128,8320]{1,0:T(8,128)(2,1)}, u32[]{:S(2)}, u32[]{:S(2)}) collective-permute-start(bf16[128,8320]{1,0:T(8,128)(2,1)} %copy-done.2), channel_id=1, source_target_pairs={{8,12},{12,8},{16,20},{20,16},{9,13},{13,9},{17,21},{21,17},{10,14... | collective-permute-start | bytes 6389768 | tf_op jit(solution)/shard_map/ppermute | solution.py:381
  204.0 74.3 %collective-permute-start.13 = (bf16[128,8320]{1,0:T(8,128)(2,1)}, bf16[128,8320]{1,0:T(8,128)(2,1)}, u32[]{:S(2)}, u32[]{:S(2)}) collective-permute-start(bf16[128,8320]{1,0:T(8,128)(2,1)} %copy-done.3), channel_id=1, source_target_pairs={{0,8},{4,12},{24,16},{28,20},{1,9},{5,13},{25,17},{29,21},{2,10},{... | collective-permute-start | bytes 6389768 | tf_op jit(solution)/shard_map/ppermute | solution.py:381
  206.6 73.7 %collective-permute-start.19 = (bf16[128,8320]{1,0:T(8,128)(2,1)}, bf16[128,8320]{1,0:T(8,128)(2,1)}, u32[]{:S(2)}, u32[]{:S(2)}) collective-permute-start(bf16[128,8320]{1,0:T(8,128)(2,1)} %collective-permute-done.2.refs_6_.refs_4_.refs_0_), channel_id=1, source_target_pairs={{0,1},{1,0},{2,3},{3,2},{4,5},{5,4},{6,7},{7,6},{8,9},{9,8},{10,11... | collective-permute-start | bytes 6389768 | tf_op jit(solution)/shard_map/ppermute | solution.py:378
  208.7 72.8 %collective-permute-start.20 = (bf16[128,8320]{1,0:T(8,128)(2,1)}, bf16[128,8320]{1,0:T(8,128)(2,1)}, u32[]{:S(2)}, u32[]{:S(2)}) collective-permute-start(bf16[128,8320]{1,0:T(8,128)(2,1)} %collective-permute-done.3.refs_7_.refs_5_.refs_1_), channel_id=1, source_target_pairs={{0,1},{1,0},{2,3},{3,2},{4,5},{5,4},{6,7},{7,6},{8,9},{9,8},{10,11... | collective-permute-start | bytes 6389768 | tf_op jit(solution)/shard_map/ppermute | solution.py:378
  210.4 71.5 %collective-permute-start.24 = (bf16[128,8320]{1,0:T(8,128)(2,1)}, bf16[128,8320]{1,0:T(8,128)(2,1)}, u32[]{:S(2)}, u32[]{:S(2)}) collective-permute-start(bf16[128,8320]{1,0:T(8,128)(2,1)} %collective-permute-done.3.refs_7_.refs_5_.refs_1_), channel_id=1, source_target_pairs={{8,16},{12,20},{16,8},{20,12},{9,17},{13,21},{17,9},{21,13},{10,18... | collective-permute-start | bytes 6389768 | tf_op jit(solution)/shard_map/ppermute | solution.py:381
  276.1 50.1 %collective-permute-start.26 = (bf16[128,8320]{1,0:T(8,128)(2,1)}, bf16[128,8320]{1,0:T(8,128)(2,1)}, u32[]{:S(2)}, u32[]{:S(2)}) collective-permute-start(bf16[128,8320]{1,0:T(8,128)(2,1)} %collective-permute-done.3.refs_7_.refs_5_.refs_1_), channel_id=1, source_target_pairs={{0,4},{4,0},{24,28},{28,24},{1,5},{5,1},{25,29},{29,25},{2,6},{6,2... | collective-permute-start | bytes 6389768 | tf_op jit(solution)/shard_map/ppermute | solution.py:381
  278.3 50.0 %collective-permute-start.23 = (bf16[128,8320]{1,0:T(8,128)(2,1)}, bf16[128,8320]{1,0:T(8,128)(2,1)}, u32[]{:S(2)}, u32[]{:S(2)}) collective-permute-start(bf16[128,8320]{1,0:T(8,128)(2,1)} %collective-permute-done.6.refs_10_), channel_id=1, source_target_pairs={{8,12},{12,8},{16,20},{20,16},{9,13},{13,9},{17,21},{21,17},{10,14... | collective-permute-start | bytes 6389768 | tf_op jit(solution)/shard_map/ppermute | solution.py:381
  280.2 50.1 %collective-permute-start.25 = (bf16[128,8320]{1,0:T(8,128)(2,1)}, bf16[128,8320]{1,0:T(8,128)(2,1)}, u32[]{:S(2)}, u32[]{:S(2)}) collective-permute-start(bf16[128,8320]{1,0:T(8,128)(2,1)} %copy-done.2), channel_id=1, source_target_pairs={{8,0},{12,4},{16,24},{20,28},{9,1},{13,5},{17,25},{21,29},{10,2},{... | collective-permute-start | bytes 6389768 | tf_op jit(solution)/shard_map/ppermute | solution.py:381
  281.5 50.1 %collective-permute-start.22 = (bf16[128,8320]{1,0:T(8,128)(2,1)}, bf16[128,8320]{1,0:T(8,128)(2,1)}, u32[]{:S(2)}, u32[]{:S(2)}) collective-permute-start(bf16[128,8320]{1,0:T(8,128)(2,1)} %collective-permute-done.15.refs_9_.refs_5_), channel_id=1, source_target_pairs={{0,1},{1,0},{2,3},{3,2},{4,5},{5,4},{6,7},{7,6},{8,9},{9,8},{10,11... | collective-permute-start | bytes 6389768 | tf_op jit(solution)/shard_map/ppermute | solution.py:378
  281.9 52.8 %collective-permute-start.21 = (bf16[128,8320]{1,0:T(8,128)(2,1)}, bf16[128,8320]{1,0:T(8,128)(2,1)}, u32[]{:S(2)}, u32[]{:S(2)}) collective-permute-start(bf16[128,8320]{1,0:T(8,128)(2,1)} %collective-permute-done.11.refs_8_.refs_4_), channel_id=1, source_target_pairs={{0,1},{1,0},{2,3},{3,2},{4,5},{5,4},{6,7},{7,6},{8,9},{9,8},{10,11... | collective-permute-start | bytes 6389768 | tf_op jit(solution)/shard_map/ppermute | solution.py:378
  326.2 48.6 %collective-permute-start.18 = (bf16[128,8320]{1,0:T(8,128)(2,1)}, bf16[128,8320]{1,0:T(8,128)(2,1)}, u32[]{:S(2)}, u32[]{:S(2)}) collective-permute-start(bf16[128,8320]{1,0:T(8,128)(2,1)} %collective-permute-done.13.refs_17_), channel_id=1, source_target_pairs={{8,16},{12,20},{16,8},{20,12},{9,17},{13,21},{17,9},{21,13},{10,18... | collective-permute-start | bytes 6389768 | tf_op jit(solution)/shard_map/ppermute | solution.py:378
  328.2 46.6 %collective-permute-start.12 = (bf16[128,8320]{1,0:T(8,128)(2,1)}, bf16[128,8320]{1,0:T(8,128)(2,1)}, u32[]{:S(2)}, u32[]{:S(2)}) collective-permute-start(bf16[128,8320]{1,0:T(8,128)(2,1)} %collective-permute-done.9.refs_4_.refs_5_.refs_14_), channel_id=1, source_target_pairs={{8,12},{12,8},{16,20},{20,16},{9,13},{13,9},{17,21},{21,17},{10,14... | collective-permute-start | bytes 6389768 | tf_op jit(solution)/shard_map/ppermute | solution.py:378
  330.3 72.1 %collective-permute-start.28 = (bf16[128,8320]{1,0:T(8,128)(2,1)}, bf16[128,8320]{1,0:T(8,128)(2,1)}, u32[]{:S(2)}, u32[]{:S(2)}) collective-permute-start(bf16[128,8320]{1,0:T(8,128)(2,1)} %collective-permute-done.14.refs_13_), channel_id=1, source_target_pairs={{8,0},{12,4},{16,24},{20,28},{9,1},{13,5},{17,25},{21,29},{10,2},{... | collective-permute-start | bytes 6389768 | tf_op jit(solution)/shard_map/ppermute | solution.py:378
  331.6 72.1 %collective-permute-start.27 = (bf16[128,8320]{1,0:T(8,128)(2,1)S(1)}, bf16[128,8320]{1,0:T(8,128)(2,1)}, u32[]{:S(2)}, u32[]{:S(2)}) collective-permute-start(bf16[128,8320]{1,0:T(8,128)(2,1)S(1)} %copy-done.1), channel_id=1, source_target_pairs={{0,4},{4,0},{24,28},{28,24},{1,5},{5,1},{25,29},{29,25},{2,6},{6,2... | collective-permute-start | bytes 6389768 | tf_op jit(solution)/shard_map/ppermute | solution.py:378
  376.6 43.6 %collective-permute-start.29 = (f16[2,4,256,256]{3,2,1,0:T(8,128)(2,1)S(1)}, f16[2,4,256,256]{3,2,1,0:T(8,128)(2,1)}, u32[]{:S(2)}, u32[]{:S(2)}) collective-permute-start(f16[2,4,256,256]{3,2,1,0:T(8,128)(2,1)S(1)} %convert_element_type.12), channel_id=1, source_target_pairs={{8,0},{12,4},{16,24},{20,28},{9,1},{13,5},{17,25},{21,29},{10,2},{... | collective-permute-start | bytes 3145736 | tf_op jit(solution)/shard_map/ppermute | solution.py:378
  397.1 23.1 %collective-permute-start.32 = (f32[4,8,128]{2,1,0:T(8,128)}, f32[4,8,128]{2,1,0:T(8,128)S(1)}, u32[]{:S(2)}, u32[]{:S(2)}) collective-permute-start(f32[4,8,128]{2,1,0:T(8,128)} %get-tuple-element.52), channel_id=1, source_target_pairs={{8,0},{12,4},{16,24},{20,28},{9,1},{13,5},{17,25},{21,29},{10,2},{... | collective-permute-start | bytes 49160 | tf_op jit(solution)/shard_map/ppermute | solution.py:378
  402.4 27.1 %collective-permute-start.31 = (f16[2,4,256,256]{3,2,1,0:T(8,128)(2,1)}, f16[2,4,256,256]{3,2,1,0:T(8,128)(2,1)}, u32[]{:S(2)}, u32[]{:S(2)}) collective-permute-start(f16[2,4,256,256]{3,2,1,0:T(8,128)(2,1)} %convert_element_type.14), channel_id=1, source_target_pairs={{8,0},{12,4},{16,24},{20,28},{9,1},{13,5},{17,25},{21,29},{10,2},{... | collective-permute-start | bytes 3145736 | tf_op jit(solution)/shard_map/ppermute | solution.py:378
  (6 other events, 221.1 us)

commit v9 on v8

--- a/solution.py
+++ b/solution.py
@@ -46,9 +46,15 @@
     return parts + [value]
 
 
-def laid_out_body(per_piece, spectra_ref, flags_ref, whole_ref, *piece_refs):
+def laid_out_body(per_piece, spectra_ref, flags_ref, whole_ref, *refs):
+    *piece_refs, flag_rows = refs
     high, parts, bins, taps = spectra_ref.shape
     half_width = bins * taps
+
+    @pl.when(pl.program_id(0) == 0)
+    def _():
+        flags = flags_ref[...].astype(jnp.float32)
+        flag_rows[...] = jnp.broadcast_to(flags, (LANES, flags.shape[1])).T
 
     def fill(out_ref):
         power = jnp.zeros((high, 1), jnp.float32)
@@ -58,7 +64,8 @@
             widened = flat.astype(jnp.float32)
             power = power + jnp.sum(widened * widened, axis=1, keepdims=True)
         power_mean = power / (parts * half_width)
-        factor = flags_ref[...].astype(jnp.float32) * lax.rsqrt(power_mean + 1e-06)
+        here = pl.ds(pl.multiple_of(pl.program_id(0) * high, high), high)
+        factor = flag_rows[here, 0:1] * lax.rsqrt(power_mean + 1e-06)
         norm = lax.rsqrt(jnp.maximum(power_mean, FLOOR))
         lane = lax.broadcasted_iota(jnp.int32, (high, LANES), 1)
         marks = jnp.zeros((high, LANES), jnp.float32)
@@ -89,13 +96,14 @@
         grid=(rows // high,),
         in_specs=[
             pl.BlockSpec((high, parts, bins, taps), lambda i: (i, 0, 0, 0)),
-            pl.BlockSpec((high, 1), lambda i: (i, 0)),
+            pl.BlockSpec((1, rows), lambda i: (0, 0)),
         ],
+        scratch_shapes=[pltpu.VMEM((rows, LANES), jnp.float32)],
         out_specs=[pl.BlockSpec((high, width), lambda i: (i, 0))]
         + [pl.BlockSpec((high, width), place(piece)) for piece in range(pieces)],
         out_shape=[jax.ShapeDtypeStruct((rows, width), spectra.dtype)]
         + [jax.ShapeDtypeStruct((rows // pieces, width), spectra.dtype)] * pieces,
-    )(spectra, flags.reshape(rows, 1))
+    )(spectra, flags.reshape(1, rows))
 
 
 def products_body(sizes, scale_coef, plan_ref, *refs):

time: 437 us -> 436 us (level)
  transfers between devices with their start and end apart: 33 -> 33, of which waited for: 6 -> 6; matrix products, arithmetic and copies ran while one was open for 3% -> 3% of each run, Pallas kernels for 32% -> 33%
where the time goes in v9:
time: 436 us; the launch traced here: 432 us
  waiting for transfers between devices  220 us (50%)
  Pallas kernels  147 us (34%)
  starting transfers between devices  48.5 us (11%)
  other arithmetic  11.5 us (3%)
    ppermute x18, waiting for transfers between devices, moved(): pieces.append(lax.ppermute(piece, axis, route))  214 us
    pallas_call x5, Pallas kernels, products(): pl.pallas_call(functools.partial(products_body, sizes, scale_coef), grid_...  139 us
    ppermute x18, starting transfers between devices, moved(): pieces.append(lax.ppermute(piece, axis, route))  28 us
    ppermute x15, starting transfers between devices, moved(): return lax.ppermute(value, axis, route)  20.6 us
  transfers between devices with their start and end apart: 33, of which 6 were waited for; matrix products, arithmetic and copies ran while one was open for 3% of the time, Pallas kernels for 33%

profile of v9, /device:TPU:31, one launch (start us, length us, event | category | flops | bytes accessed | tf_op | source)
XLA Modules:
  0.0 431.6 jit_solution(832045410143837100)
XLA Ops:
  0.0 7.0 %shard_map.29 = (bf16[256,8320]{1,0:T(8,128)(2,1)}, bf16[128,8320]{1,0:T(8,128)(2,1)}, bf16[128,8320]{1,0:T(8,128)(2,1)}) custom-call(bf16[256,2,16,256]{3,2,1,0:T(8,128)(2,1)} %bitcast.31, s32[1,256]{1,0:T(1,128)} %flags_ref.1), custom_call_target="tpu_custom_call" | custom-call | tf_op jit(solution)/shard_map/pallas_call | solution.py:94
  7.1 1.3 collective-permute-start.3
  8.4 2.1 collective-permute-start.6
  11.6 42.9 %collective-permute-done.2.refs_6_.refs_4_.refs_0_ = bf16[128,8320]{1,0:T(8,128)(2,1)} collective-permute-done((bf16[128,8320]{1,0:T(8,128)(2,1)}, bf16[128,8320]{1,0:T(8,128)(2,1)}, u32[]{:S(2)}, u32[]{:S(2)}) %collective-permute-start.2) | collective-permute-done | bytes 2129952 | tf_op jit(solution)/shard_map/ppermute | solution.py:389
  54.7 45.4 %collective-permute-done.3.refs_7_.refs_5_.refs_1_ = bf16[128,8320]{1,0:T(8,128)(2,1)} collective-permute-done((bf16[128,8320]{1,0:T(8,128)(2,1)}, bf16[128,8320]{1,0:T(8,128)(2,1)}, u32[]{:S(2)}, u32[]{:S(2)}) %collective-permute-start.3) | collective-permute-done | bytes 2129952 | tf_op jit(solution)/shard_map/ppermute | solution.py:389
  100.1 1.5 collective-permute-start
  101.9 2.0 collective-permute-start.9
  104.2 45.7 %collective-permute-done.5.refs_9_ = bf16[128,8320]{1,0:T(8,128)(2,1)S(1)} collective-permute-done((bf16[128,8320]{1,0:T(8,128)(2,1)}, bf16[128,8320]{1,0:T(8,128)(2,1)S(1)}, u32[]{:S(2)}, u32[]{:S(2)}) %collective-permute-start.5) | collective-permute-done | bytes 2129952 | tf_op jit(solution)/shard_map/ppermute | solution.py:389
  152.5 2.1 collective-permute-start.17
  154.7 5.3 %collective-permute-start.16 = (bf16[128,8320]{1,0:T(8,128)(2,1)}, bf16[128,8320]{1,0:T(8,128)(2,1)}, u32[]{:S(2)}, u32[]{:S(2)}) collective-permute-start(bf16[128,8320]{1,0:T(8,128)(2,1)} %collective-permute-done.4.refs_8_), channel_id=1, source_target_pairs={{0,8},{4,12},{24,16},{28,20},{1,9},{5,13},{25,17},{29,21},{2,10},{... | collective-permute-start | bytes 6389768 | tf_op jit(solution)/shard_map/ppermute | solution.py:389
  164.7 35.9 %collective-permute-done.10.refs_8_.refs_9_.refs_18_ = bf16[128,8320]{1,0:T(8,128)(2,1)S(1)} collective-permute-done((bf16[128,8320]{1,0:T(8,128)(2,1)}, bf16[128,8320]{1,0:T(8,128)(2,1)S(1)}, u32[]{:S(2)}, u32[]{:S(2)}) %collective-permute-start.10) | collective-permute-done | bytes 2129952 | tf_op jit(solution)/shard_map/ppermute | solution.py:389
  200.5 2.0 collective-permute-start.14
  202.6 2.6 collective-permute-start.13
  205.2 2.2 collective-permute-start.19
  207.4 1.6 collective-permute-start.20
  209.0 2.0 collective-permute-start.24
  211.0 47.3 %shard_map.30.refs_12_ = f32[2,4,256,2048]{3,2,1,0:T(8,128)} custom-call(s32[20]{0:T(128)} %get-tuple-element.36.plan_ref, bf16[256,8320]{1,0:T(8,128)(2,1)} %get-tuple-element.32.refs_0_, bf16[256,8320]{1,0:T(8,128)(2,1)} %collective-permute-done.refs_1_, bf16[256,8320]{1,0:T(8,128)(2,1)} %collective-permute-done.1.refs_2_, ...), custom_call_target="tpu_custom_call" | custom-call | flops 34359738368 | bytes 83886080 | tf_op jit(solution)/shard_map/pallas_call | solution.py:315
  258.3 16.4 %shard_map.31.refs_22_ = f32[2,4,256,2048]{3,2,1,0:T(8,128)} custom-call(s32[8]{0:T(128)} %get-tuple-element.38.plan_ref, bf16[256,8320]{1,0:T(8,128)(2,1)} %get-tuple-element.32.refs_0_, bf16[256,8320]{1,0:T(8,128)(2,1)} %collective-permute-done.refs_1_, bf16[256,8320]{1,0:T(8,128)(2,1)} %collective-permute-done.1.refs_2_, ...), custom_call_target="tpu_custom_call", output_to_operand_aliasing={{}: (13, {})} | custom-call | flops 8589934592 | bytes 20971520 | tf_op jit(solution)/shard_map/pallas_call | solution.py:315
  274.7 2.1 collective-permute-start.26
  276.9 2.0 collective-permute-start.23
  280.7 44.1 %collective-permute-done.26.refs_21_ = bf16[128,8320]{1,0:T(8,128)(2,1)} collective-permute-done((bf16[128,8320]{1,0:T(8,128)(2,1)}, bf16[128,8320]{1,0:T(8,128)(2,1)}, u32[]{:S(2)}, u32[]{:S(2)}) %collective-permute-start.26) | collective-permute-done | bytes 2129952 | tf_op jit(solution)/shard_map/ppermute | solution.py:389
  324.8 2.0 collective-permute-start.18
  326.9 2.1 collective-permute-start.12
  330.3 3.0 collective-permute-start.27
  333.3 40.1 %shard_map.32 = (f32[2,4,256,2048]{3,2,1,0:T(8,128)}, f32[2,4,256,256]{3,2,1,0:T(8,128)}, f32[4,8,128]{2,1,0:T(8,128)}) custom-call(s32[16]{0:T(128)} %get-tuple-element.41.plan_ref, bf16[256,8320]{1,0:T(8,128)(2,1)} %get-tuple-element.32.refs_0_, bf16[256,8320]{1,0:T(8,128)(2,1)} %collective-permute-done.refs_1_, ...), custom_call_target="tpu_custom_call", output_to_operand_aliasing={{0}: (23, {})} | custom-call | flops 25769803776 | bytes 62914560 | tf_op jit(solution)/shard_map/pallas_call | solution.py:315
  373.5 1.8 convert_element_type.12
  376.6 19.1 %shard_map.33 = (f32[2,4,256,256]{3,2,1,0:T(8,128)}, f32[4,8,128]{2,1,0:T(8,128)}) custom-call(s32[8]{0:T(128)} %get-tuple-element.51.plan_ref, bf16[128,8320]{1,0:T(8,128)(2,1)} %collective-permute-done.2.refs_6_.refs_4_.refs_0_, bf16[128,8320]{1,0:T(8,128)(2,1)} %collective-permute-done.3.refs_7_.refs_5_.refs_1_, ...), custom_call_target="tpu_custom_call" | custom-call | flops 8589934592 | bytes 20971520 | tf_op jit(solution)/shard_map/pallas_call | solution.py:315
  398.3 2.7 convert_element_type.14
  402.4 16.3 %shard_map.34 = f32[2,4,256,2048]{3,2,1,0:T(8,128)} custom-call(s32[8]{0:T(128)} %get-tuple-element.31.plan_ref, bf16[256,8320]{1,0:T(8,128)(2,1)} %get-tuple-element.32.refs_0_, bf16[256,8320]{1,0:T(8,128)(2,1)} %collective-permute-done.refs_1_, bf16[256,8320]{1,0:T(8,128)(2,1)} %collective-permute-done.1.refs_2_, ...), custom_call_target="tpu_custom_call", output_to_operand_aliasing={{}: (9, {})} | custom-call | flops 8589934592 | bytes 20971520 | tf_op jit(solution)/shard_map/pallas_call | solution.py:315
  418.9 3.5 select_dynamic-update-slice_fusion.1
  422.4 5.8 %collective-permute-done.31 = f16[2,4,256,256]{3,2,1,0:T(8,128)(2,1)} collective-permute-done((f16[2,4,256,256]{3,2,1,0:T(8,128)(2,1)}, f16[2,4,256,256]{3,2,1,0:T(8,128)(2,1)}, u32[]{:S(2)}, u32[]{:S(2)}) %collective-permute-start.31) | collective-permute-done | bytes 1048608 | tf_op jit(solution)/shard_map/ppermute | solution.py:386
  428.1 3.5 select_dynamic-update-slice_fusion
  (62 shorter events, 17.8 us)
Async XLA Ops:
  7.0 47.5 %collective-permute-start.2 = (bf16[128,8320]{1,0:T(8,128)(2,1)}, bf16[128,8320]{1,0:T(8,128)(2,1)}, u32[]{:S(2)}, u32[]{:S(2)}) collective-permute-start(bf16[128,8320]{1,0:T(8,128)(2,1)} %get-tuple-element.33.refs_4_), channel_id=1, source_target_pairs={{0,8},{4,12},{8,0},{12,4},{16,24},{20,28},{24,16},{28,20},{1,9},{5... | collective-permute-start | bytes 6389768 | tf_op jit(solution)/shard_map/ppermute | solution.py:389
  7.1 93.0 %collective-permute-start.3 = (bf16[128,8320]{1,0:T(8,128)(2,1)}, bf16[128,8320]{1,0:T(8,128)(2,1)}, u32[]{:S(2)}, u32[]{:S(2)}) collective-permute-start(bf16[128,8320]{1,0:T(8,128)(2,1)} %get-tuple-element.34.refs_5_), channel_id=1, source_target_pairs={{0,8},{4,12},{8,0},{12,4},{16,24},{20,28},{24,16},{28,20},{1,9},{5... | collective-permute-start | bytes 6389768 | tf_op jit(solution)/shard_map/ppermute | solution.py:389
  8.4 93.2 %collective-permute-start.6 = (bf16[128,8320]{1,0:T(8,128)(2,1)}, bf16[128,8320]{1,0:T(8,128)(2,1)}, u32[]{:S(2)}, u32[]{:S(2)}) collective-permute-start(bf16[128,8320]{1,0:T(8,128)(2,1)} %get-tuple-element.33.refs_4_), channel_id=1, source_target_pairs={{8,16},{12,20},{16,8},{20,12},{9,17},{13,21},{17,9},{21,13},{10,18... | collective-permute-start | bytes 6389768 | tf_op jit(solution)/shard_map/ppermute | solution.py:389
  10.5 139.4 %collective-permute-start.1 = (bf16[256,8320]{1,0:T(8,128)(2,1)}, bf16[256,8320]{1,0:T(8,128)(2,1)}, u32[]{:S(2)}, u32[]{:S(2)}) collective-permute-start(bf16[256,8320]{1,0:T(8,128)(2,1)} %get-tuple-element.32.refs_0_), channel_id=1, source_target_pairs={{0,2},{1,3},{2,0},{3,1},{4,6},{5,7},{6,4},{7,5},{8,10},{9,11},{10,... | collective-permute-start | bytes 12779528 | tf_op jit(solution)/shard_map/ppermute | solution.py:386
  10.8 91.1 %collective-permute-start.7 = (bf16[128,8320]{1,0:T(8,128)(2,1)}, bf16[128,8320]{1,0:T(8,128)(2,1)S(1)}, u32[]{:S(2)}, u32[]{:S(2)}) collective-permute-start(bf16[128,8320]{1,0:T(8,128)(2,1)} %get-tuple-element.34.refs_5_), channel_id=1, source_target_pairs={{8,16},{12,20},{16,8},{20,12},{9,17},{13,21},{17,9},{21,13},{10,18... | collective-permute-start | bytes 6389768 | tf_op jit(solution)/shard_map/ppermute | solution.py:389
  54.5 49.4 %collective-permute-start.4 = (bf16[128,8320]{1,0:T(8,128)(2,1)}, bf16[128,8320]{1,0:T(8,128)(2,1)}, u32[]{:S(2)}, u32[]{:S(2)}) collective-permute-start(bf16[128,8320]{1,0:T(8,128)(2,1)} %get-tuple-element.33.refs_4_), channel_id=1, source_target_pairs={{0,4},{4,0},{8,12},{12,8},{16,20},{20,16},{24,28},{28,24},{1,5},{5... | collective-permute-start | bytes 6389768 | tf_op jit(solution)/shard_map/ppermute | solution.py:389
  100.1 52.4 %collective-permute-start = (bf16[256,8320]{1,0:T(8,128)(2,1)}, bf16[256,8320]{1,0:T(8,128)(2,1)}, u32[]{:S(2)}, u32[]{:S(2)}) collective-permute-start(bf16[256,8320]{1,0:T(8,128)(2,1)} %get-tuple-element.32.refs_0_), channel_id=1, source_target_pairs={{0,1},{1,0},{2,3},{3,2},{4,5},{5,4},{6,7},{7,6},{8,9},{9,8},{10,11... | collective-permute-start | bytes 12779528 | tf_op jit(solution)/shard_map/ppermute | solution.py:386
  101.7 48.2 %collective-permute-start.5 = (bf16[128,8320]{1,0:T(8,128)(2,1)}, bf16[128,8320]{1,0:T(8,128)(2,1)S(1)}, u32[]{:S(2)}, u32[]{:S(2)}) collective-permute-start(bf16[128,8320]{1,0:T(8,128)(2,1)} %get-tuple-element.34.refs_5_), channel_id=1, source_target_pairs={{0,4},{4,0},{8,12},{12,8},{16,20},{20,16},{24,28},{28,24},{1,5},{5... | collective-permute-start | bytes 6389768 | tf_op jit(solution)/shard_map/ppermute | solution.py:389
  101.9 52.7 %collective-permute-start.9 = (bf16[128,8320]{1,0:T(8,128)(2,1)}, bf16[128,8320]{1,0:T(8,128)(2,1)}, u32[]{:S(2)}, u32[]{:S(2)}) collective-permute-start(bf16[128,8320]{1,0:T(8,128)(2,1)} %collective-permute-done.2.refs_6_.refs_4_.refs_0_), channel_id=1, source_target_pairs={{8,16},{12,20},{16,8},{20,12},{9,17},{13,21},{17,9},{21,13},{10,18... | collective-permute-start | bytes 6389768 | tf_op jit(solution)/shard_map/ppermute | solution.py:389
  103.9 56.0 %collective-permute-start.11 = (bf16[128,8320]{1,0:T(8,128)(2,1)}, bf16[128,8320]{1,0:T(8,128)(2,1)}, u32[]{:S(2)}, u32[]{:S(2)}) collective-permute-start(bf16[128,8320]{1,0:T(8,128)(2,1)} %collective-permute-done.2.refs_6_.refs_4_.refs_0_), channel_id=1, source_target_pairs={{0,2},{1,3},{2,0},{3,1},{4,6},{5,7},{6,4},{7,5},{8,10},{9,11},{10,... | collective-permute-start | bytes 6389768 | tf_op jit(solution)/shard_map/ppermute | solution.py:389
  149.9 59.1 %collective-permute-start.8 = (bf16[256,8320]{1,0:T(8,128)(2,1)}, bf16[256,8320]{1,0:T(8,128)(2,1)}, u32[]{:S(2)}, u32[]{:S(2)}) collective-permute-start(bf16[256,8320]{1,0:T(8,128)(2,1)} %collective-permute-done.1.refs_2_), channel_id=1, source_target_pairs={{0,1},{1,0},{2,3},{3,2},{4,5},{5,4},{6,7},{7,6},{8,9},{9,8},{10,11... | collective-permute-start | bytes 12779528 | tf_op jit(solution)/shard_map/ppermute | solution.py:386
  151.2 49.3 %collective-permute-start.10 = (bf16[128,8320]{1,0:T(8,128)(2,1)}, bf16[128,8320]{1,0:T(8,128)(2,1)S(1)}, u32[]{:S(2)}, u32[]{:S(2)}) collective-permute-start(bf16[128,8320]{1,0:T(8,128)(2,1)} %collective-permute-done.6.refs_10_), channel_id=1, source_target_pairs={{8,0},{12,4},{16,24},{20,28},{9,1},{13,5},{17,25},{21,29},{10,2},{... | collective-permute-start | bytes 6389768 | tf_op jit(solution)/shard_map/ppermute | solution.py:389
  152.5 50.1 %collective-permute-start.17 = (bf16[128,8320]{1,0:T(8,128)(2,1)}, bf16[128,8320]{1,0:T(8,128)(2,1)}, u32[]{:S(2)}, u32[]{:S(2)}) collective-permute-start(bf16[128,8320]{1,0:T(8,128)(2,1)} %collective-permute-done.2.refs_6_.refs_4_.refs_0_), channel_id=1, source_target_pairs={{0,4},{4,0},{24,28},{28,24},{1,5},{5,1},{25,29},{29,25},{2,6},{6,2... | collective-permute-start | bytes 6389768 | tf_op jit(solution)/shard_map/ppermute | solution.py:389
  154.7 50.5 %collective-permute-start.16 = (bf16[128,8320]{1,0:T(8,128)(2,1)}, bf16[128,8320]{1,0:T(8,128)(2,1)}, u32[]{:S(2)}, u32[]{:S(2)}) collective-permute-start(bf16[128,8320]{1,0:T(8,128)(2,1)} %collective-permute-done.4.refs_8_), channel_id=1, source_target_pairs={{0,8},{4,12},{24,16},{28,20},{1,9},{5,13},{25,17},{29,21},{2,10},{... | collective-permute-start | bytes 6389768 | tf_op jit(solution)/shard_map/ppermute | solution.py:389
  159.9 47.4 %collective-permute-start.15 = (bf16[128,8320]{1,0:T(8,128)(2,1)}, bf16[128,8320]{1,0:T(8,128)(2,1)}, u32[]{:S(2)}, u32[]{:S(2)}) collective-permute-start(bf16[128,8320]{1,0:T(8,128)(2,1)} %collective-permute-done.3.refs_7_.refs_5_.refs_1_), channel_id=1, source_target_pairs={{0,2},{1,3},{2,0},{3,1},{4,6},{5,7},{6,4},{7,5},{8,10},{9,11},{10,... | collective-permute-start | bytes 6389768 | tf_op jit(solution)/shard_map/ppermute | solution.py:389
  200.5 74.2 %collective-permute-start.14 = (bf16[128,8320]{1,0:T(8,128)(2,1)}, bf16[128,8320]{1,0:T(8,128)(2,1)}, u32[]{:S(2)}, u32[]{:S(2)}) collective-permute-start(bf16[128,8320]{1,0:T(8,128)(2,1)} %copy-done.2), channel_id=1, source_target_pairs={{8,12},{12,8},{16,20},{20,16},{9,13},{13,9},{17,21},{21,17},{10,14... | collective-permute-start | bytes 6389768 | tf_op jit(solution)/shard_map/ppermute | solution.py:389
  202.6 74.3 %collective-permute-start.13 = (bf16[128,8320]{1,0:T(8,128)(2,1)}, bf16[128,8320]{1,0:T(8,128)(2,1)}, u32[]{:S(2)}, u32[]{:S(2)}) collective-permute-start(bf16[128,8320]{1,0:T(8,128)(2,1)} %copy-done.3), channel_id=1, source_target_pairs={{0,8},{4,12},{24,16},{28,20},{1,9},{5,13},{25,17},{29,21},{2,10},{... | collective-permute-start | bytes 6389768 | tf_op jit(solution)/shard_map/ppermute | solution.py:389
  205.2 73.7 %collective-permute-start.19 = (bf16[128,8320]{1,0:T(8,128)(2,1)}, bf16[128,8320]{1,0:T(8,128)(2,1)}, u32[]{:S(2)}, u32[]{:S(2)}) collective-permute-start(bf16[128,8320]{1,0:T(8,128)(2,1)} %collective-permute-done.2.refs_6_.refs_4_.refs_0_), channel_id=1, source_target_pairs={{0,1},{1,0},{2,3},{3,2},{4,5},{5,4},{6,7},{7,6},{8,9},{9,8},{10,11... | collective-permute-start | bytes 6389768 | tf_op jit(solution)/shard_map/ppermute | solution.py:386
  207.4 72.8 %collective-permute-start.20 = (bf16[128,8320]{1,0:T(8,128)(2,1)}, bf16[128,8320]{1,0:T(8,128)(2,1)}, u32[]{:S(2)}, u32[]{:S(2)}) collective-permute-start(bf16[128,8320]{1,0:T(8,128)(2,1)} %collective-permute-done.3.refs_7_.refs_5_.refs_1_), channel_id=1, source_target_pairs={{0,1},{1,0},{2,3},{3,2},{4,5},{5,4},{6,7},{7,6},{8,9},{9,8},{10,11... | collective-permute-start | bytes 6389768 | tf_op jit(solution)/shard_map/ppermute | solution.py:386
  209.0 71.5 %collective-permute-start.24 = (bf16[128,8320]{1,0:T(8,128)(2,1)}, bf16[128,8320]{1,0:T(8,128)(2,1)}, u32[]{:S(2)}, u32[]{:S(2)}) collective-permute-start(bf16[128,8320]{1,0:T(8,128)(2,1)} %collective-permute-done.3.refs_7_.refs_5_.refs_1_), channel_id=1, source_target_pairs={{8,16},{12,20},{16,8},{20,12},{9,17},{13,21},{17,9},{21,13},{10,18... | collective-permute-start | bytes 6389768 | tf_op jit(solution)/shard_map/ppermute | solution.py:389
  274.7 50.1 %collective-permute-start.26 = (bf16[128,8320]{1,0:T(8,128)(2,1)}, bf16[128,8320]{1,0:T(8,128)(2,1)}, u32[]{:S(2)}, u32[]{:S(2)}) collective-permute-start(bf16[128,8320]{1,0:T(8,128)(2,1)} %collective-permute-done.3.refs_7_.refs_5_.refs_1_), channel_id=1, source_target_pairs={{0,4},{4,0},{24,28},{28,24},{1,5},{5,1},{25,29},{29,25},{2,6},{6,2... | collective-permute-start | bytes 6389768 | tf_op jit(solution)/shard_map/ppermute | solution.py:389
  276.9 50.0 %collective-permute-start.23 = (bf16[128,8320]{1,0:T(8,128)(2,1)}, bf16[128,8320]{1,0:T(8,128)(2,1)}, u32[]{:S(2)}, u32[]{:S(2)}) collective-permute-start(bf16[128,8320]{1,0:T(8,128)(2,1)} %collective-permute-done.6.refs_10_), channel_id=1, source_target_pairs={{8,12},{12,8},{16,20},{20,16},{9,13},{13,9},{17,21},{21,17},{10,14... | collective-permute-start | bytes 6389768 | tf_op jit(solution)/shard_map/ppermute | solution.py:389
  278.9 50.1 %collective-permute-start.25 = (bf16[128,8320]{1,0:T(8,128)(2,1)}, bf16[128,8320]{1,0:T(8,128)(2,1)}, u32[]{:S(2)}, u32[]{:S(2)}) collective-permute-start(bf16[128,8320]{1,0:T(8,128)(2,1)} %copy-done.2), channel_id=1, source_target_pairs={{8,0},{12,4},{16,24},{20,28},{9,1},{13,5},{17,25},{21,29},{10,2},{... | collective-permute-start | bytes 6389768 | tf_op jit(solution)/shard_map/ppermute | solution.py:389
  280.2 50.1 %collective-permute-start.22 = (bf16[128,8320]{1,0:T(8,128)(2,1)}, bf16[128,8320]{1,0:T(8,128)(2,1)}, u32[]{:S(2)}, u32[]{:S(2)}) collective-permute-start(bf16[128,8320]{1,0:T(8,128)(2,1)} %collective-permute-done.15.refs_9_.refs_5_), channel_id=1, source_target_pairs={{0,1},{1,0},{2,3},{3,2},{4,5},{5,4},{6,7},{7,6},{8,9},{9,8},{10,11... | collective-permute-start | bytes 6389768 | tf_op jit(solution)/shard_map/ppermute | solution.py:386
  280.5 52.8 %collective-permute-start.21 = (bf16[128,8320]{1,0:T(8,128)(2,1)}, bf16[128,8320]{1,0:T(8,128)(2,1)}, u32[]{:S(2)}, u32[]{:S(2)}) collective-permute-start(bf16[128,8320]{1,0:T(8,128)(2,1)} %collective-permute-done.11.refs_8_.refs_4_), channel_id=1, source_target_pairs={{0,1},{1,0},{2,3},{3,2},{4,5},{5,4},{6,7},{7,6},{8,9},{9,8},{10,11... | collective-permute-start | bytes 6389768 | tf_op jit(solution)/shard_map/ppermute | solution.py:386
  324.8 48.6 %collective-permute-start.18 = (bf16[128,8320]{1,0:T(8,128)(2,1)}, bf16[128,8320]{1,0:T(8,128)(2,1)}, u32[]{:S(2)}, u32[]{:S(2)}) collective-permute-start(bf16[128,8320]{1,0:T(8,128)(2,1)} %collective-permute-done.13.refs_17_), channel_id=1, source_target_pairs={{8,16},{12,20},{16,8},{20,12},{9,17},{13,21},{17,9},{21,13},{10,18... | collective-permute-start | bytes 6389768 | tf_op jit(solution)/shard_map/ppermute | solution.py:386
  326.9 46.6 %collective-permute-start.12 = (bf16[128,8320]{1,0:T(8,128)(2,1)}, bf16[128,8320]{1,0:T(8,128)(2,1)}, u32[]{:S(2)}, u32[]{:S(2)}) collective-permute-start(bf16[128,8320]{1,0:T(8,128)(2,1)} %collective-permute-done.9.refs_4_.refs_5_.refs_14_), channel_id=1, source_target_pairs={{8,12},{12,8},{16,20},{20,16},{9,13},{13,9},{17,21},{21,17},{10,14... | collective-permute-start | bytes 6389768 | tf_op jit(solution)/shard_map/ppermute | solution.py:386
  329.0 72.1 %collective-permute-start.28 = (bf16[128,8320]{1,0:T(8,128)(2,1)}, bf16[128,8320]{1,0:T(8,128)(2,1)}, u32[]{:S(2)}, u32[]{:S(2)}) collective-permute-start(bf16[128,8320]{1,0:T(8,128)(2,1)} %collective-permute-done.14.refs_13_), channel_id=1, source_target_pairs={{8,0},{12,4},{16,24},{20,28},{9,1},{13,5},{17,25},{21,29},{10,2},{... | collective-permute-start | bytes 6389768 | tf_op jit(solution)/shard_map/ppermute | solution.py:386
  330.3 72.1 %collective-permute-start.27 = (bf16[128,8320]{1,0:T(8,128)(2,1)S(1)}, bf16[128,8320]{1,0:T(8,128)(2,1)}, u32[]{:S(2)}, u32[]{:S(2)}) collective-permute-start(bf16[128,8320]{1,0:T(8,128)(2,1)S(1)} %copy-done.1), channel_id=1, source_target_pairs={{0,4},{4,0},{24,28},{28,24},{1,5},{5,1},{25,29},{29,25},{2,6},{6,2... | collective-permute-start | bytes 6389768 | tf_op jit(solution)/shard_map/ppermute | solution.py:386
  375.3 43.6 %collective-permute-start.29 = (f16[2,4,256,256]{3,2,1,0:T(8,128)(2,1)S(1)}, f16[2,4,256,256]{3,2,1,0:T(8,128)(2,1)}, u32[]{:S(2)}, u32[]{:S(2)}) collective-permute-start(f16[2,4,256,256]{3,2,1,0:T(8,128)(2,1)S(1)} %convert_element_type.12), channel_id=1, source_target_pairs={{8,0},{12,4},{16,24},{20,28},{9,1},{13,5},{17,25},{21,29},{10,2},{... | collective-permute-start | bytes 3145736 | tf_op jit(solution)/shard_map/ppermute | solution.py:386
  395.7 23.1 %collective-permute-start.32 = (f32[4,8,128]{2,1,0:T(8,128)}, f32[4,8,128]{2,1,0:T(8,128)S(1)}, u32[]{:S(2)}, u32[]{:S(2)}) collective-permute-start(f32[4,8,128]{2,1,0:T(8,128)} %get-tuple-element.52), channel_id=1, source_target_pairs={{8,0},{12,4},{16,24},{20,28},{9,1},{13,5},{17,25},{21,29},{10,2},{... | collective-permute-start | bytes 49160 | tf_op jit(solution)/shard_map/ppermute | solution.py:386
  401.1 27.1 %collective-permute-start.31 = (f16[2,4,256,256]{3,2,1,0:T(8,128)(2,1)}, f16[2,4,256,256]{3,2,1,0:T(8,128)(2,1)}, u32[]{:S(2)}, u32[]{:S(2)}) collective-permute-start(f16[2,4,256,256]{3,2,1,0:T(8,128)(2,1)} %convert_element_type.14), channel_id=1, source_target_pairs={{8,0},{12,4},{16,24},{20,28},{9,1},{13,5},{17,25},{21,29},{10,2},{... | collective-permute-start | bytes 3145736 | tf_op jit(solution)/shard_map/ppermute | solution.py:386
  (6 other events, 221.1 us)
